TPU v7x, 128 devices: a whole 4x4x4 slice. The times are simulated.
128 devices in a mesh: block: 8 (over y, core), row: 16 (over x, z).
Axes of the slice: x: 4, y: 4, z: 4, core: 2. Of those that a mesh axis runs over, the one named last changes fastest.
Arguments:
- snapshots: bfloat16 [32768, 2048], P('block', 'row'), may hold values from -6 to 6
- usable_frame_tallies: int32 [128], replicated, may hold values from 64 to 256, as said below
- retained_frequency_slots: int32 [64], replicated, may hold values from 0 to 127, as said below
- modes: bfloat16 [64, 2, 2048, 512], P('block', None, 'row'), may hold values from -0.09375 to 0.09375
Outputs:
- coefficients: float32 [128, 2, 64, 512], P('row', None, 'block')
- energy: float32 [64, 512], P('block')
Inputs may be any that keep to these rules, and one draw needn't show every extreme that they name: Only the first usable_frame_tallies[b] snapshots of block b are valid; some block is full. `retained_frequency_slots`: 64 distinct bins in increasing order; bin 0 and bin 256 // 2 - 1 are always kept.
All inputs are finite; a program needn't handle non-finite values.
Results may differ from a plain program's by a relative error of at most 0.004.
Values may be sent and summed in bfloat16 or wider, within the bound.
No kernel may reach another device: no remote copies, remote signals or barrier semaphores. Data moves between devices by JAX's collectives and lax.ppermute only.
A program may use at most 64 MiB of HBM per device.

v0:
```python
import jax
import jax.numpy as jnp
from jax import lax
from jax.sharding import PartitionSpec as P

FRAMES_PER_SEG = 256


def window_table(usable_frame_tallies, retained_frequency_slots):
    recording_epochs = jnp.arange(FRAMES_PER_SEG, dtype=jnp.int32)
    lengths = usable_frame_tallies.astype(jnp.float32)[:, None]
    frequency_power_statistics = recording_epochs.astype(jnp.float32)[None, :]
    domain_grid_locations = recording_epochs[None, :] < usable_frame_tallies[:, None]
    window = jnp.where(
        domain_grid_locations,
        jnp.sin(jnp.pi * (frequency_power_statistics + 0.5) / lengths) ** 2,
        0.0,
    )
    scaling = 1.0 / jnp.sqrt(jnp.sum(window * window, axis=1, keepdims=True))
    remaining_matrix_lines = (
        retained_frequency_slots[:, None] * recording_epochs[None, :] % FRAMES_PER_SEG
    )
    phase = remaining_matrix_lines.astype(jnp.float32) * (2.0 * jnp.pi / FRAMES_PER_SEG)
    trig = jnp.stack([jnp.cos(phase), -jnp.sin(phase)])
    return ((scaling * window)[:, None, None, :] * trig[None]).astype(jnp.bfloat16)


def shards(snapshots, usable_frame_tallies, retained_frequency_slots, modes):
    own_blocks = snapshots.shape[0] // FRAMES_PER_SEG
    row_width = snapshots.shape[1]
    first_block = lax.axis_index("block") * own_blocks
    own_counts = lax.dynamic_slice_in_dim(usable_frame_tallies, first_block, own_blocks, 0)
    table = window_table(own_counts, retained_frequency_slots)
    blocks_data = snapshots.reshape(own_blocks, FRAMES_PER_SEG, row_width)
    spectra = jnp.einsum(
        "bckt,btx->bckx", table, blocks_data, preferred_element_type=jnp.float32
    ).astype(jnp.bfloat16)
    moved = lax.all_to_all(spectra, "block", split_axis=2, concat_axis=0, tiled=True)
    real_part = moved[:, 0]
    imag_part = moved[:, 1]
    stacked_left = jnp.stack(
        [
            jnp.concatenate([real_part, imag_part], axis=-1),
            jnp.concatenate([imag_part, -real_part], axis=-1),
        ],
        axis=1,
    )
    mode_rows = modes.reshape(modes.shape[0], 2 * row_width, modes.shape[3])
    blocks_all = stacked_left.shape[0]
    share_rows = blocks_all // lax.axis_size("row")
    first_row = lax.axis_index("row") * share_rows
    weights = usable_frame_tallies.astype(jnp.float32)
    total_weight = jnp.sum(weights)
    whole = lax.psum(
        jnp.einsum("bckx,kxm->bckm", stacked_left, mode_rows, preferred_element_type=jnp.float32),
        "row",
    )
    coefficients = lax.dynamic_slice_in_dim(whole, first_row, share_rows, 0)
    power = whole[:, 0] ** 2 + whole[:, 1] ** 2
    energy = jnp.sum(weights[:, None, None] * power, axis=0) / total_weight
    return (coefficients, energy)


def solution(mesh):
    placed = (P("block", "row"), P(), P(), P("block", None, "row", None))
    return jax.shard_map(
        shards,
        mesh=mesh,
        in_specs=placed,
        out_specs=(P("row", None, "block", None), P("block", None)),
        check_vma=False,
    )
```

profile of v0, /device:TPU:0, one launch (start us, length us, event | category | flops | bytes accessed | tf_op | source)
XLA Modules:
  0.0 146.3 jit_solution(16269908741228497771)
XLA Ops:
  7.2 0.0 copy-start
  7.2 0.0 all-reduce.2.cloned.1.call-start
  7.2 0.9 fusion.21
  8.1 0.3 multiply_reduce_fusion
  8.4 0.2 fusion.18
  8.5 1.0 fusion.15
  9.6 1.6 %convolution_convert_fusion = bf16[16,2,64,128]{3,2,1,0:T(8,128)(2,1)S(1)} fusion(bf16[16,256,128,1]{2,1,3,0:T(8,128)(2,1)} %bitcast.40, f32[2,64,256]{2,1,0:T(8,128)S(1)} %pad_maximum_fusion, f32[16,256]{1,0:T(8,128)S(1)} %fusion.18), kind=kOutput, calls=%fused_computation.8 | convolution fusion | flops 135528448 | bytes 1720320 | tf_op jit(solution)/shard_map/bckt,btx->bckx/dot_general | solution.py:35
  11.2 0.5 copy.9
  11.8 14.7 %all_to_all.18 = bf16[16,2,64,128]{3,1,0,2:T(2,128)(2,1)S(1)} all-to-all(bf16[16,2,64,128]{3,1,0,2:T(2,128)(2,1)S(1)} %copy.9), channel_id=1, replica_groups=mesh['block'=8,'row'=16] {'block'}, dimensions={2} | all-to-all | bytes 1048576 | tf_op jit(solution)/shard_map/all_to_all | solution.py:38
  26.5 0.1 copy.10
  26.7 0.1 maximum_bitcast_fusion
  26.8 0.0 copy-done
  26.8 2.7 %convolution_bitcast_fusion = f32[128,2,8,512]{3,0,1,2:T(8,128)} fusion(bf16[8,256,512,1]{2,1,3,0:T(8,128)(2,1)S(1)} %bitcast.36, bf16[128,1,8,256]{3,0,1,2:T(8,128)(2,1)S(1)} %get-tuple-element.11, bf16[128,1,8,256]{3,0,1,2:T(8,128)(2,1)S(1)} %get-tuple-element.10), kind=kOutput, calls=%fused_computation | convolution fusion | flops 537395200 | bytes 7340032 | tf_op jit(solution)/shard_map/bckx,kxm->bckm/dot_general | solution.py:55
  29.5 0.0 copy-start.1
  29.5 0.0 all-reduce.2.cloned.1.call-update
  29.5 0.6 copy-done.1
  30.2 0.6 convert_reduce_fusion
  30.7 102.9 %all-reduce.2.cloned.1.call-done = f32[128,2,8,512]{3,0,1,2:T(8,128)} async-done(((f32[128,2,8,512]{3,0,1,2:T(8,128)}), f32[128,2,8,512]{3,0,1,2:T(8,128)}) %all-reduce.2.cloned.1.call-update) | async-done | bytes 4194320 | tf_op jit(solution)/shard_map/psum | solution.py:54
  133.6 1.0 constant_dynamic-slice_fusion
  134.6 0.9 copy.12
  135.5 2.8 %fusion.3 = f32[8,512]{1,0:T(8,128)S(1)} fusion(f32[128,2,8,512]{3,0,1,2:T(8,128)} %all-reduce.2.cloned.1.call-done, f32[128]{0:T(128)S(1)} %convert_element_type.38), kind=kLoop, calls=%fused_computation.5 | loop fusion | flops 2617344 | bytes 4211200 | tf_op jit(solution)/shard_map/reduce_sum | solution.py:60
  138.3 1.2 broadcast_divide_fusion
  (6 shorter events, 0.1 us)
Async XLA Ops:
  7.2 19.7 %copy-start = (bf16[8,2,128,512]{3,2,1,0:T(8,128)(2,1)S(1)}, bf16[8,2,128,512]{3,2,1,0:T(8,128)(2,1)}, u32[]{:S(2)}) copy-start(bf16[8,2,128,512]{3,2,1,0:T(8,128)(2,1)} %param.7) | copy-start | bytes 6291460
  7.2 126.4 %all-reduce.2.cloned.1.call-start = ((), (), s32[]{:S(2)}) async-start(), calls=%async_computation.1 | async-start | bytes 8388608 | tf_op jit(solution)/shard_map/psum | solution.py:54
  29.5 0.7 copy-start.1
Sparse Core Ops, SparseCore 0:
  29.7 103.9 all-reduce.1
where the time goes:
time: 147 us; the launch traced here: 146 us
  waiting for transfers between devices  103 us (70%)
  blocking collectives  14.7 us (10%)
  between operations  14.1 us (10%)
  other arithmetic  7.01 us (5%)
  matrix products  4.33 us (3%)
  local copies, waits for them, and re-layouts  3.14 us (2%)
    psum x1, waiting for transfers between devices, shards(): lax.psum(jnp.einsum('bckx,kxm->bckm', stacked_left, mode_rows, preferred_...  103 us
    all_to_all x1, blocking collectives, shards(): lax.all_to_all(spectra, 'block', split_axis=2, concat_axis=0, tiled=True)  14.7 us
  transfers between devices with their start and end apart: 1, of which 1 were waited for; matrix products, arithmetic and copies ran while one was open for 0% of the time, Pallas kernels for 0%

commit v1 on v0

--- a/solution.py
+++ b/solution.py
@@ -47,17 +47,24 @@
     )
     mode_rows = modes.reshape(modes.shape[0], 2 * row_width, modes.shape[3])
     blocks_all = stacked_left.shape[0]
-    share_rows = blocks_all // lax.axis_size("row")
+    rows = lax.axis_size("row")
+    share_rows = blocks_all // rows
     first_row = lax.axis_index("row") * share_rows
     weights = usable_frame_tallies.astype(jnp.float32)
     total_weight = jnp.sum(weights)
-    whole = lax.psum(
-        jnp.einsum("bckx,kxm->bckm", stacked_left, mode_rows, preferred_element_type=jnp.float32),
-        "row",
-    )
-    coefficients = lax.dynamic_slice_in_dim(whole, first_row, share_rows, 0)
-    power = whole[:, 0] ** 2 + whole[:, 1] ** 2
-    energy = jnp.sum(weights[:, None, None] * power, axis=0) / total_weight
+    partial = jnp.einsum(
+        "bckx,kxm->kcbm", stacked_left, mode_rows, preferred_element_type=jnp.float32
+    ).astype(jnp.bfloat16)
+    k, c, _, m = partial.shape
+    partial = partial.reshape(k, c, rows, share_rows, m).transpose(2, 0, 1, 3, 4)
+    pieces = lax.all_to_all(partial, "row", split_axis=0, concat_axis=0, tiled=True)
+    total = jnp.sum(pieces.astype(jnp.float32), axis=0)
+    coefficients = total.transpose(2, 1, 0, 3)
+    own_weights = lax.dynamic_slice_in_dim(weights, first_row, share_rows, 0)
+    power = total[:, 0] ** 2 + total[:, 1] ** 2
+    energy = jnp.sum(own_weights[None, :, None] * power, axis=1)
+    copies = jnp.broadcast_to(energy[None], (rows,) + energy.shape)
+    energy = jnp.sum(lax.all_to_all(copies, "row", 0, 0, tiled=True), axis=0) / total_weight
     return (coefficients, energy)
 
 

time: 147 us -> 77.3 us (0.53)
  waiting for transfers between devices: 103 us -> 36.5 us
  between operations: 14.1 us -> 0.79 us
  starting transfers between devices: 0.04 us -> 12 us
  matrix products: 4.33 us -> 2.36 us
    psum x1 -> x0, waiting for transfers between devices: 103 us -> none  [shards(): lax.psum(jnp.einsum('bckx,kxm->bckm', stacked_left, mode_rows, preferred_...]
    all_to_all x0 -> x2, waiting for transfers between devices: none -> 36.5 us  [the longest x1 29.6 us: shards(): lax.all_to_all(partial, 'row', split_axis=0, concat_axis=0, tiled=True)]
    all_to_all x0 -> x2, starting transfers between devices: none -> 12 us  [the longest x1 8.06 us: shards(): lax.all_to_all(partial, 'row', split_axis=0, concat_axis=0, tiled=True)]
    dot_general x1, matrix products: 2.68 us -> 0.71 us  [shards(): jnp.einsum('bckx,kxm->kcbm', stacked_left, mode_rows, preferred_element_t...]
    reshape x0 -> x1, local copies, waits for them, and re-layouts: none -> 1.62 us  [shards(): partial.reshape(k, c, rows, share_rows, m).transpose(2, 0, 1, 3, 4)]
  transfers between devices with their start and end apart: 1 -> 2, of which waited for: 1 -> 2; matrix products, arithmetic and copies ran while one was open for 0% -> 2% of each run, Pallas kernels for 0% -> 0%
where the time goes in v1:
time: 77.3 us; the launch traced here: 76.9 us
  waiting for transfers between devices  36.5 us (47%)
  blocking collectives  14.7 us (19%)
  starting transfers between devices  12 us (16%)
  other arithmetic  6.47 us (8%)
  local copies, waits for them, and re-layouts  3.97 us (5%)
  matrix products  2.36 us (3%)
  between operations  0.79 us (1%)
    all_to_all x1, waiting for transfers between devices, shards(): lax.all_to_all(partial, 'row', split_axis=0, concat_axis=0, tiled=True)  29.6 us
    all_to_all x1, blocking collectives, shards(): lax.all_to_all(spectra, 'block', split_axis=2, concat_axis=0, tiled=True)  14.7 us
    all_to_all x1, starting transfers between devices, shards(): lax.all_to_all(partial, 'row', split_axis=0, concat_axis=0, tiled=True)  8.06 us
    all_to_all x1, waiting for transfers between devices, shards(): lax.all_to_all(copies, 'row', 0, 0, tiled=True)  6.95 us
    all_to_all x1, starting transfers between devices, shards(): lax.all_to_all(copies, 'row', 0, 0, tiled=True)  3.95 us
    reduce_sum x1, other arithmetic, shards(): total = jnp.sum(pieces.astype(jnp.float32), axis=0)  2.01 us
    dot_general x1, matrix products, shards(): jnp.einsum('bckt,btx->bckx', table, blocks_data, preferred_element_type=j...  1.65 us
    reshape x1, local copies, waits for them, and re-layouts, shards(): partial.reshape(k, c, rows, share_rows, m).transpose(2, 0, 1, 3, 4)  1.62 us
  transfers between devices with their start and end apart: 2, of which 2 were waited for; matrix products, arithmetic and copies ran while one was open for 2% of the time, Pallas kernels for 0%

profile of v1, /device:TPU:0, one launch (start us, length us, event | category | flops | bytes accessed | tf_op | source)
XLA Modules:
  0.0 76.9 jit_solution(2151180923538195296)
XLA Ops:
  0.6 0.0 copy-start
  0.7 0.9 %fusion.21 = (f32[16]{0:T(128)S(1)}, s32[16]{0:T(128)S(1)}) fusion(s32[128]{0:T(128)} %param.5, s32[]{:T(128)S(6)} %select_n.32), kind=kLoop, calls=%fused_computation.43 | loop fusion | flops 16 | bytes 196 | tf_op jit(solution)/shard_map/convert_element_type | solution.py:11
  1.5 0.3 multiply_reduce_fusion
  1.8 0.2 fusion.18
  2.0 1.0 %fusion.15 = (f32[1,64,256]{2,1,0:T(8,128)S(1)}, f32[1,64,256]{2,1,0:T(8,128)S(1)}) fusion(s32[64]{0:T(128)} %param.6), kind=kLoop, calls=%fused_computation.31 | loop fusion | flops 245760 | bytes 131328 | tf_op jit(solution)/shard_map/cos | solution.py:24
  3.0 1.6 %convolution_convert_fusion = bf16[16,2,64,128]{3,2,1,0:T(8,128)(2,1)S(1)} fusion(bf16[16,256,128,1]{2,1,3,0:T(8,128)(2,1)} %bitcast.48, f32[2,64,256]{2,1,0:T(8,128)S(1)} %pad_maximum_fusion, f32[16,256]{1,0:T(8,128)S(1)} %fusion.18), kind=kOutput, calls=%fused_computation.4 | convolution fusion | flops 135528448 | bytes 1720320 | tf_op jit(solution)/shard_map/bckt,btx->bckx/dot_general | solution.py:35
  4.6 0.5 copy.14
  5.2 14.7 %all_to_all.28 = bf16[16,2,64,128]{3,1,0,2:T(2,128)(2,1)S(1)} all-to-all(bf16[16,2,64,128]{3,1,0,2:T(2,128)(2,1)S(1)} %copy.14), channel_id=1, replica_groups=mesh['block'=8,'row'=16] {'block'}, dimensions={2} | all-to-all | bytes 1048576 | tf_op jit(solution)/shard_map/all_to_all | solution.py:38
  19.9 0.1 copy.15
  20.1 0.1 maximum_bitcast_fusion
  20.2 0.0 copy-done
  20.3 0.7 convert_bitcast_fusion
  21.0 1.6 %copy.24 = bf16[8,2,16,8,512]{4,3,1,0,2:T(8,128)(2,1)} copy(bf16[8,2,16,8,512]{4,3,2,1,0:T(8,128)(2,1)S(1)} %convert_bitcast_fusion) | data formatting | bytes 4194304 | tf_op jit(solution)/shard_map/reshape | solution.py:59
  22.6 0.0 copy-start.1
  22.6 8.1 %all-to-all-start.1 = ((bf16[16,8,2,8,512]{4,3,2,1,0:T(8,128)(2,1)}), bf16[16,8,2,8,512]{4,3,2,1,0:T(8,128)(2,1)}, u32[]{:S(2)}, u32[]{:S(2)}) async-start(bf16[16,8,2,8,512]{4,3,2,1,0:T(8,128)(2,1)} %bitcast.43), calls=%async_computation.1 | async-start | bytes 4194304 | tf_op jit(solution)/shard_map/all_to_all | solution.py:60
  30.7 0.0 copy-done.1
  30.7 0.1 dynamic_slice.7
  30.8 29.6 %all-to-all-done.1 = bf16[16,8,2,8,512]{4,3,2,1,0:T(8,128)(2,1)} async-done(((bf16[16,8,2,8,512]{4,3,2,1,0:T(8,128)(2,1)}), bf16[16,8,2,8,512]{4,3,2,1,0:T(8,128)(2,1)}, u32[]{:S(2)}, u32[]{:S(2)}) %all-to-all-start.1) | async-done | bytes 2097184 | tf_op jit(solution)/shard_map/all_to_all | solution.py:60
  60.4 2.0 %convert_reduce_fusion = f32[8,2,8,512]{3,2,1,0:T(8,128)S(1)} fusion(bf16[16,8,2,8,512]{4,3,2,1,0:T(8,128)(2,1)} %all-to-all-done.1), kind=kLoop, calls=%fused_computation | loop fusion | flops 2031616 | bytes 2359296 | tf_op jit(solution)/shard_map/reduce_sum | solution.py:61
  62.4 0.1 fusion.8
  62.5 0.7 broadcast_in_dim.7
  63.2 3.9 %all-to-all-start.2 = ((f32[16,8,512]{2,1,0:T(8,128)}), f32[16,8,512]{2,1,0:T(8,128)S(1)}, u32[]{:S(2)}, u32[]{:S(2)}) async-start(f32[16,8,512]{2,1,0:T(8,128)} %broadcast_in_dim.7), calls=%async_computation.2 | async-start | bytes 524288 | tf_op jit(solution)/shard_map/all_to_all | solution.py:67
  67.1 0.7 convert_reduce_fusion.1
  67.8 0.9 %copy.19 = f32[8,2,8,512]{3,2,1,0:T(8,128)} copy(f32[8,2,8,512]{3,0,1,2:T(8,128)S(1)} %bitcast.46) | data formatting | bytes 524288
  68.7 7.0 %all-to-all-done.2 = f32[16,8,512]{2,1,0:T(8,128)S(1)} async-done(((f32[16,8,512]{2,1,0:T(8,128)}), f32[16,8,512]{2,1,0:T(8,128)S(1)}, u32[]{:S(2)}, u32[]{:S(2)}) %all-to-all-start.2) | async-done | bytes 262176 | tf_op jit(solution)/shard_map/all_to_all | solution.py:67
  75.6 1.2 %broadcast_divide_fusion = f32[8,512]{1,0:T(8,128)} fusion(f32[8,512]{1,0:T(8,128)S(1)} %reduce_sum.48, f32[]{:T(128)} %convert_reduce_fusion.1), kind=kLoop, calls=%fused_computation.38 | loop fusion | flops 4096 | bytes 32772 | tf_op jit(solution)/shard_map/div | solution.py:67
  (7 shorter events, 0.1 us)
Async XLA Ops:
  0.6 19.6 %copy-start = (bf16[8,2,128,512]{3,2,1,0:T(8,128)(2,1)S(1)}, bf16[8,2,128,512]{3,2,1,0:T(8,128)(2,1)}, u32[]{:S(2)}) copy-start(bf16[8,2,128,512]{3,2,1,0:T(8,128)(2,1)} %param.7) | copy-start | bytes 6291460
  22.6 8.1 %copy-start.1 = (s32[128]{0:T(128)S(1)}, s32[128]{0:T(128)}, u32[]{:S(2)}) copy-start(s32[128]{0:T(128)} %param.5) | copy-start | bytes 1540
  22.6 37.8 %all-to-all-start.1 = ((bf16[16,8,2,8,512]{4,3,2,1,0:T(8,128)(2,1)}), bf16[16,8,2,8,512]{4,3,2,1,0:T(8,128)(2,1)}, u32[]{:S(2)}, u32[]{:S(2)}) async-start(bf16[16,8,2,8,512]{4,3,2,1,0:T(8,128)(2,1)} %bitcast.43), calls=%async_computation.1 | async-start | bytes 4194304 | tf_op jit(solution)/shard_map/all_to_all | solution.py:60
  63.2 12.4 %all-to-all-start.2 = ((f32[16,8,512]{2,1,0:T(8,128)}), f32[16,8,512]{2,1,0:T(8,128)S(1)}, u32[]{:S(2)}, u32[]{:S(2)}) async-start(f32[16,8,512]{2,1,0:T(8,128)} %broadcast_in_dim.7), calls=%async_computation.2 | async-start | bytes 524288 | tf_op jit(solution)/shard_map/all_to_all | solution.py:67

commit v2 on v0

v2 whole, which is shorter than its diff:
```python
import functools

import jax
import jax.numpy as jnp
from jax import lax
from jax.experimental import pallas as pl
from jax.experimental.pallas import tpu as pltpu
from jax.sharding import PartitionSpec as P

FRAMES_PER_SEG = 256
SIDE = 4
VMEM = pl.BlockSpec(memory_space=pltpu.VMEM)
SMEM = pl.BlockSpec(memory_space=pltpu.SMEM)
bf16, f32 = jnp.bfloat16, jnp.float32


def window_table(usable_frame_tallies, retained_frequency_slots):
    recording_epochs = jnp.arange(FRAMES_PER_SEG, dtype=jnp.int32)
    lengths = usable_frame_tallies.astype(jnp.float32)[:, None]
    frequency_power_statistics = recording_epochs.astype(jnp.float32)[None, :]
    domain_grid_locations = recording_epochs[None, :] < usable_frame_tallies[:, None]
    window = jnp.where(
        domain_grid_locations,
        jnp.sin(jnp.pi * (frequency_power_statistics + 0.5) / lengths) ** 2,
        0.0,
    )
    scaling = 1.0 / jnp.sqrt(jnp.sum(window * window, axis=1, keepdims=True))
    remaining_matrix_lines = (
        retained_frequency_slots[:, None] * recording_epochs[None, :] % FRAMES_PER_SEG
    )
    phase = remaining_matrix_lines.astype(jnp.float32) * (2.0 * jnp.pi / FRAMES_PER_SEG)
    trig = jnp.stack([jnp.cos(phase), -jnp.sin(phase)])
    return ((scaling * window)[:, None, None, :] * trig[None]).astype(jnp.bfloat16)


def grid_place():
    row = lax.axis_index("row")
    return row // SIDE, row % SIDE


def project_kernel(spectra, modes, *refs):
    outs, acc = refs[:-1], refs[-1]
    x, z = grid_place()
    freqs, points, width = spectra.shape[1], spectra.shape[4], modes.shape[2]
    blocks = spectra.shape[0] * spectra.shape[3]
    half = freqs // 2
    for k in range(freqs):
        real = spectra[:, k, 0].reshape(blocks, points)
        imag = spectra[:, k, 1].reshape(blocks, points)
        left = jnp.concatenate(
            [
                jnp.concatenate([real, imag], axis=1),
                jnp.concatenate([imag, -real], axis=1),
            ],
            axis=0,
        )
        slot = k % 2
        acc[slot] = jnp.dot(left, modes[k], preferred_element_type=f32).reshape(acc.shape[1:])
        for i in range(SIDE):
            if k < half:
                piece = acc[slot, :, (x + i) % SIDE]
                out = outs[i]
            else:
                piece = acc[slot, :, :, (z + i) % SIDE]
                out = outs[SIDE + i]
            out[k % half] = piece.reshape(2, -1, width).astype(out.dtype)


def project(spectra, modes):
    freqs, width = modes.shape[0], modes.shape[2]
    blocks = spectra.shape[0] * spectra.shape[3]
    piece = (freqs // 2, 2, blocks // SIDE, width)
    shapes = [jax.ShapeDtypeStruct(piece, f32 if i == 0 else bf16) for i in range(SIDE)] * 2
    return pl.pallas_call(
        project_kernel,
        out_shape=shapes,
        in_specs=[VMEM, VMEM],
        out_specs=[VMEM] * len(shapes),
        scratch_shapes=[
            pltpu.VMEM((2, 2, SIDE, SIDE, blocks // (SIDE * SIDE), width), f32)
        ],
        compiler_params=pltpu.CompilerParams(vmem_limit_bytes=32 << 20),
        name="project",
    )(spectra, modes)


def fold_kernel(along_x, own, first, second, third, *refs):
    outs, acc = refs[:-1], refs[-1]
    x, z = grid_place()
    place = x if along_x else z
    width = own.shape[3]
    for k in range(own.shape[0]):
        total = own[k] + first[k].astype(f32) + second[k].astype(f32) + third[k].astype(f32)
        acc[k % 2] = total.reshape(acc.shape[1:])
        for i in range(SIDE):
            piece = acc[k % 2, :, (place + i) % SIDE].reshape(-1, width)
            outs[i][k] = piece.astype(outs[i].dtype)


def fold(along_x, parts):
    freqs, _, blocks, width = parts[0].shape
    shapes = [
        jax.ShapeDtypeStruct((freqs, 2 * blocks // SIDE, width), f32 if i == 0 else bf16)
        for i in range(SIDE)
    ]
    return pl.pallas_call(
        functools.partial(fold_kernel, along_x),
        out_shape=shapes,
        in_specs=[VMEM] * SIDE,
        out_specs=[VMEM] * SIDE,
        scratch_shapes=[pltpu.VMEM((2, 2, SIDE, blocks // SIDE, width), f32)],
        compiler_params=pltpu.CompilerParams(vmem_limit_bytes=32 << 20),
        name="fold_x" if along_x else "fold_z",
    )(*parts)


def finish_kernel(tallies, *refs):
    parts, (coefficients, energy) = refs[: 2 * SIDE], refs[2 * SIDE :]
    blocks, _, freqs, width = coefficients.shape
    first = lax.axis_index("row") * blocks
    places = lax.broadcasted_iota(jnp.int32, (blocks, width), 0)
    weights = jnp.zeros((blocks, width), f32)
    for j in range(blocks):
        weights = jnp.where(places == j, tallies[first + j].astype(f32), weights)
    half = freqs // 2
    for k in range(freqs):
        group = parts[SIDE * (k // half) : SIDE * (k // half) + SIDE]
        total = sum(part[k % half].astype(f32) for part in group)
        real, imag = total[:blocks], total[blocks:]
        coefficients[:, 0, k, :] = real
        coefficients[:, 1, k, :] = imag
        power = jnp.sum(weights * (real * real + imag * imag), axis=0, keepdims=True)
        energy[:, k : k + 1, :] = jnp.broadcast_to(power[None], (energy.shape[0], 1, width))


def finish(tallies, rows, parts):
    half, blocks2, width = parts[0].shape
    return pl.pallas_call(
        finish_kernel,
        out_shape=[
            jax.ShapeDtypeStruct((blocks2 // 2, 2, 2 * half, width), f32),
            jax.ShapeDtypeStruct((rows, 2 * half, width), f32),
        ],
        in_specs=[SMEM] + [VMEM] * len(parts),
        out_specs=[VMEM, VMEM],
        compiler_params=pltpu.CompilerParams(vmem_limit_bytes=32 << 20),
        name="finish",
    )(tallies, *parts)


def mean_kernel(parts, tallies, energy):
    weight = jnp.sum(tallies[...].astype(f32), axis=1, keepdims=True)
    energy[...] = jnp.sum(parts[...], axis=0) / weight


def shards(snapshots, usable_frame_tallies, retained_frequency_slots, modes):
    own_blocks = snapshots.shape[0] // FRAMES_PER_SEG
    row_width = snapshots.shape[1]
    rows = lax.axis_size("row")
    groups = lax.axis_size("block")
    first_block = lax.axis_index("block") * own_blocks
    own_counts = lax.dynamic_slice_in_dim(usable_frame_tallies, first_block, own_blocks, 0)
    table = window_table(own_counts, retained_frequency_slots)
    blocks_data = snapshots.reshape(own_blocks, FRAMES_PER_SEG, row_width)
    spectra = jnp.einsum(
        "bckt,btx->kcbx", table, blocks_data, preferred_element_type=jnp.float32
    ).astype(jnp.bfloat16)
    spectra = spectra.reshape((groups, -1) + spectra.shape[1:])
    moved = lax.all_to_all(spectra, "block", split_axis=0, concat_axis=0, tiled=True)

    def along(value, dx, dz):
        pairs = [
            (x * SIDE + z, (x + dx) % SIDE * SIDE + (z + dz) % SIDE)
            for x in range(SIDE)
            for z in range(SIDE)
        ]
        return lax.ppermute(value, "row", pairs)

    mode_rows = modes.reshape(modes.shape[0], 2 * row_width, modes.shape[3])
    pieces = project(moved, mode_rows)
    by_x = [pieces[0]] + [along(pieces[i], i, 0) for i in range(1, SIDE)]
    by_z = [pieces[SIDE]] + [along(pieces[SIDE + i], 0, i) for i in range(1, SIDE)]
    from_x = fold(False, by_x)
    from_z = fold(True, by_z)
    last = [from_x[0]] + [along(from_x[i], 0, i) for i in range(1, SIDE)]
    last += [from_z[0]] + [along(from_z[i], i, 0) for i in range(1, SIDE)]
    coefficients, energy_parts = finish(usable_frame_tallies, rows, last)
    swapped = lax.all_to_all(energy_parts, "row", 0, 0, tiled=True)
    energy = pl.pallas_call(
        mean_kernel,
        out_shape=jax.ShapeDtypeStruct(energy_parts.shape[1:], f32),
        in_specs=[VMEM, VMEM],
        out_specs=VMEM,
        name="mean",
    )(swapped, usable_frame_tallies.reshape(1, -1))
    return (coefficients, energy)


def solution(mesh):
    placed = (P("block", "row"), P(), P(), P("block", None, "row", None))
    return jax.shard_map(
        shards,
        mesh=mesh,
        in_specs=placed,
        out_specs=(P("row", None, "block", None), P("block", None)),
        check_vma=False,
    )
```

time: 147 us -> 66.5 us (0.45)
  waiting for transfers between devices: 103 us -> 5.26 us
  starting transfers between devices: 0.04 us -> 24.9 us
  blocking collectives: 14.7 us -> 28.1 us
  between operations: 14.1 us -> 0.74 us
  other arithmetic: 7.01 us -> 2.23 us
  Pallas kernels: 0 us -> 4.17 us
  matrix products: 4.33 us -> 0.42 us
  local copies, waits for them, and re-layouts: 3.14 us -> 0.37 us
    psum x1 -> x0, waiting for transfers between devices: 103 us -> none  [shards(): lax.psum(jnp.einsum('bckx,kxm->bckm', stacked_left, mode_rows, preferred_...]
    ppermute x0 -> x12, starting transfers between devices: none -> 24.9 us  [along(): return lax.ppermute(value, 'row', pairs)]
    all_to_all x1 -> x2, blocking collectives: 14.7 us -> 28.1 us  [the longest x1 14.7 us: shards(): lax.all_to_all(spectra, 'block', split_axis=0, concat_axis=0, tiled=True)]
    ppermute x0 -> x12, waiting for transfers between devices: none -> 5.26 us  [along(): return lax.ppermute(value, 'row', pairs)]
    pallas_call x0 -> x5, Pallas kernels: none -> 4.17 us  [the longest x1 1.64 us: shards(): pl.pallas_call(mean_kernel, out_shape=jax.ShapeDtypeStruct(energy_parts.s...]
    dot_general x2 -> x1, matrix products: 4.33 us -> 0.42 us  [shards(): jnp.einsum('bckt,btx->kcbx', table, blocks_data, preferred_element_type=j...]
    reduce_sum x2 -> x0, other arithmetic: 3.39 us -> none  [the longest x1 2.82 us: shards(): energy = jnp.sum(weights[:, None, None] * power, axis=0) / total_weight]
    unnamed x5 -> x6, local copies, waits for them, and re-layouts: 1.49 us -> 0.02 us
  transfers between devices with their start and end apart: 1 -> 12, of which waited for: 1 -> 5; matrix products, arithmetic and copies ran while one was open for 0% -> 0% of each run, Pallas kernels for 0% -> 0%
where the time goes in v2:
time: 66.5 us; the launch traced here: 66.3 us
  blocking collectives  28.1 us (42%)
  starting transfers between devices  24.9 us (37%)
  waiting for transfers between devices  5.26 us (8%)
  Pallas kernels  4.17 us (6%)
  other arithmetic  2.23 us (3%)
  between operations  0.74 us (1%)
    ppermute x12, starting transfers between devices, along(): return lax.ppermute(value, 'row', pairs)  24.9 us
    all_to_all x1, blocking collectives, shards(): lax.all_to_all(spectra, 'block', split_axis=0, concat_axis=0, tiled=True)  14.7 us
    all_to_all x1, blocking collectives, shards(): swapped = lax.all_to_all(energy_parts, 'row', 0, 0, tiled=True)  13.4 us
    ppermute x12, waiting for transfers between devices, along(): return lax.ppermute(value, 'row', pairs)  5.26 us
    pallas_call x1, Pallas kernels, shards(): pl.pallas_call(mean_kernel, out_shape=jax.ShapeDtypeStruct(energy_parts.s...  1.64 us
    pallas_call x1, Pallas kernels, finish(): pl.pallas_call(finish_kernel, out_shape=[jax.ShapeDtypeStruct((blocks2 //...  1.42 us
  transfers between devices with their start and end apart: 12, of which 5 were waited for; matrix products, arithmetic and copies ran while one was open for 0% of the time, Pallas kernels for 0%

profile of v2, /device:TPU:0, one launch (start us, length us, event | category | flops | bytes accessed | tf_op | source)
XLA Modules:
  0.0 66.3 jit_solution(13154086088523495084)
XLA Ops:
  0.6 0.0 copy-start
  0.7 0.8 %fusion.13 = (f32[16]{0:T(128)S(1)}, s32[16]{0:T(128)S(1)}) fusion(s32[128]{0:T(128)} %tallies.1, s32[]{:T(128)S(6)} %select_n.29), kind=kLoop, calls=%fused_computation.24 | loop fusion | flops 16 | bytes 196 | tf_op jit(solution)/shard_map/convert_element_type | solution.py:19
  1.5 0.3 multiply_reduce_fusion
  1.7 0.2 fusion.12
  1.9 1.0 %fusion.9 = (f32[1,64,256]{2,1,0:T(8,128)S(1)}, f32[1,64,256]{2,1,0:T(8,128)S(1)}) fusion(s32[64]{0:T(128)} %param.6), kind=kLoop, calls=%fused_computation.16 | loop fusion | flops 245760 | bytes 131328 | tf_op jit(solution)/shard_map/cos | solution.py:32
  2.9 0.0 copy-start.1
  2.9 0.4 fusion
  3.4 0.3 copy.6
  3.7 14.7 %all_to_all.10.spectra = bf16[8,8,2,16,128]{4,3,2,1,0:T(8,128)(2,1)S(1)} all-to-all(bf16[8,8,2,16,128]{4,3,2,1,0:T(8,128)(2,1)S(1)} %bitcast.14), channel_id=1, replica_groups=mesh['block'=8,'row'=16] {'block'}, dimensions={0} | all-to-all | bytes 1048576 | tf_op jit(solution)/shard_map/all_to_all | solution.py:169
  18.5 0.8 %project.1 = (f32[4,2,32,512]{3,2,1,0:T(8,128)S(1)}, bf16[4,2,32,512]{3,2,1,0:T(8,128)(2,1)S(1)}, bf16[4,2,32,512]{3,2,1,0:T(8,128)(2,1)S(1)}, bf16[4,2,32,512]{...) custom-call(bf16[8,8,2,16,128]{4,3,2,1,0:T(8,128)(2,1)S(1)} %all_to_, ...), custom_call_target="tpu_custom_call" | custom-call | tf_op jit(solution)/shard_map/project/pallas_call | solution.py:74
  19.3 1.6 %collective-permute-start = (bf16[4,2,32,512]{3,2,1,0:T(8,128)(2,1)S(1)}, bf16[4,2,32,512]{3,2,1,0:T(8,128)(2,1)S(1)}, u32[]{:S(2)}, u32[]{:S(2)}) collective-permute-start(bf16[4,2,32,512]{3,2,1,0:T(8,128)(2,1)S(1)} %get-tuple-element.21), channel_id=1, source_target_pairs={{0,4},{1,5},{2,6},{3,7},{4,8},{5,9},{6,10},{7,11},{8,12},{9,13},{1... | collective-permute-start | bytes 786440 | tf_op jit(solution)/shard_map/ppermute | solution.py:177
  20.9 2.7 %collective-permute-start.1 = (bf16[4,2,32,512]{3,2,1,0:T(8,128)(2,1)S(1)}, bf16[4,2,32,512]{3,2,1,0:T(8,128)(2,1)S(1)}, u32[]{:S(2)}, u32[]{:S(2)}) collective-permute-start(bf16[4,2,32,512]{3,2,1,0:T(8,128)(2,1)S(1)} %get-tuple-element.22), channel_id=1, source_target_pairs={{0,8},{1,9},{2,10},{3,11},{4,12},{5,13},{6,14},{7,15},{8,0},{9,1},... | collective-permute-start | bytes 786440 | tf_op jit(solution)/shard_map/ppermute | solution.py:177
  23.6 1.5 %collective-permute-start.2 = (bf16[4,2,32,512]{3,2,1,0:T(8,128)(2,1)S(1)}, bf16[4,2,32,512]{3,2,1,0:T(8,128)(2,1)S(1)}, u32[]{:S(2)}, u32[]{:S(2)}) collective-permute-start(bf16[4,2,32,512]{3,2,1,0:T(8,128)(2,1)S(1)} %get-tuple-element.23), channel_id=1, source_target_pairs={{0,12},{1,13},{2,14},{3,15},{4,0},{5,1},{6,2},{7,3},{8,4},{9,5},{1... | collective-permute-start | bytes 786440 | tf_op jit(solution)/shard_map/ppermute | solution.py:177
  25.0 1.9 %collective-permute-start.6 = (bf16[4,2,32,512]{3,2,1,0:T(8,128)(2,1)S(1)}, bf16[4,2,32,512]{3,2,1,0:T(8,128)(2,1)S(1)}, u32[]{:S(2)}, u32[]{:S(2)}) collective-permute-start(bf16[4,2,32,512]{3,2,1,0:T(8,128)(2,1)S(1)} %get-tuple-element.29), channel_id=1, source_target_pairs={{0,1},{1,2},{2,3},{3,0},{4,5},{5,6},{6,7},{7,4},{8,9},{9,10},{10,1... | collective-permute-start | bytes 786440 | tf_op jit(solution)/shard_map/ppermute | solution.py:177
  26.9 3.6 %collective-permute-start.7 = (bf16[4,2,32,512]{3,2,1,0:T(8,128)(2,1)S(1)}, bf16[4,2,32,512]{3,2,1,0:T(8,128)(2,1)S(1)}, u32[]{:S(2)}, u32[]{:S(2)}) collective-permute-start(bf16[4,2,32,512]{3,2,1,0:T(8,128)(2,1)S(1)} %get-tuple-element.30), channel_id=1, source_target_pairs={{0,2},{1,3},{2,0},{3,1},{4,6},{5,7},{6,4},{7,5},{8,10},{9,11},{10,... | collective-permute-start | bytes 786440 | tf_op jit(solution)/shard_map/ppermute | solution.py:177
  30.5 2.3 %collective-permute-start.8 = (bf16[4,2,32,512]{3,2,1,0:T(8,128)(2,1)S(1)}, bf16[4,2,32,512]{3,2,1,0:T(8,128)(2,1)S(1)}, u32[]{:S(2)}, u32[]{:S(2)}) collective-permute-start(bf16[4,2,32,512]{3,2,1,0:T(8,128)(2,1)S(1)} %get-tuple-element.31), channel_id=1, source_target_pairs={{0,3},{1,0},{2,1},{3,2},{4,7},{5,4},{6,5},{7,6},{8,11},{9,8},{10,9... | collective-permute-start | bytes 786440 | tf_op jit(solution)/shard_map/ppermute | solution.py:177
  32.8 2.0 %collective-permute-done.1.second = bf16[4,2,32,512]{3,2,1,0:T(8,128)(2,1)S(1)} collective-permute-done((bf16[4,2,32,512]{3,2,1,0:T(8,128)(2,1)S(1)}, bf16[4,2,32,512]{3,2,1,0:T(8,128)(2,1)S(1)}, u32[]{:S(2)}, u32[]{:S(2)}) %collective-permute-start.1) | collective-permute-done | bytes 262176 | tf_op jit(solution)/shard_map/ppermute | solution.py:177
  34.9 0.1 fold_z.1
  35.0 2.0 %collective-permute-start.3 = (bf16[4,16,512]{2,1,0:T(8,128)(2,1)S(1)}, bf16[4,16,512]{2,1,0:T(8,128)(2,1)S(1)}, u32[]{:S(2)}, u32[]{:S(2)}) collective-permute-start(bf16[4,16,512]{2,1,0:T(8,128)(2,1)S(1)} %get-tuple-element.25), channel_id=1, source_target_pairs={{0,1},{1,2},{2,3},{3,0},{4,5},{5,6},{6,7},{7,4},{8,9},{9,10},{10,1... | collective-permute-start | bytes 196616 | tf_op jit(solution)/shard_map/ppermute | solution.py:177
  37.0 3.6 %collective-permute-start.4 = (bf16[4,16,512]{2,1,0:T(8,128)(2,1)S(1)}, bf16[4,16,512]{2,1,0:T(8,128)(2,1)S(1)}, u32[]{:S(2)}, u32[]{:S(2)}) collective-permute-start(bf16[4,16,512]{2,1,0:T(8,128)(2,1)S(1)} %get-tuple-element.26), channel_id=1, source_target_pairs={{0,2},{1,3},{2,0},{3,1},{4,6},{5,7},{6,4},{7,5},{8,10},{9,11},{10,... | collective-permute-start | bytes 196616 | tf_op jit(solution)/shard_map/ppermute | solution.py:177
  40.6 1.0 %collective-permute-start.5 = (bf16[4,16,512]{2,1,0:T(8,128)(2,1)S(1)}, bf16[4,16,512]{2,1,0:T(8,128)(2,1)S(1)}, u32[]{:S(2)}, u32[]{:S(2)}) collective-permute-start(bf16[4,16,512]{2,1,0:T(8,128)(2,1)S(1)} %get-tuple-element.27), channel_id=1, source_target_pairs={{0,3},{1,0},{2,1},{3,2},{4,7},{5,4},{6,5},{7,6},{8,11},{9,8},{10,9... | collective-permute-start | bytes 196616 | tf_op jit(solution)/shard_map/ppermute | solution.py:177
  41.6 0.5 collective-permute-done.7.second
  42.2 0.1 fold_x.1
  42.3 0.9 %collective-permute-start.9 = (bf16[4,16,512]{2,1,0:T(8,128)(2,1)S(1)}, bf16[4,16,512]{2,1,0:T(8,128)(2,1)S(1)}, u32[]{:S(2)}, u32[]{:S(2)}) collective-permute-start(bf16[4,16,512]{2,1,0:T(8,128)(2,1)S(1)} %get-tuple-element.33), channel_id=1, source_target_pairs={{0,4},{1,5},{2,6},{3,7},{4,8},{5,9},{6,10},{7,11},{8,12},{9,13},{1... | collective-permute-start | bytes 196616 | tf_op jit(solution)/shard_map/ppermute | solution.py:177
  43.2 2.4 %collective-permute-start.10 = (bf16[4,16,512]{2,1,0:T(8,128)(2,1)S(1)}, bf16[4,16,512]{2,1,0:T(8,128)(2,1)S(1)}, u32[]{:S(2)}, u32[]{:S(2)}) collective-permute-start(bf16[4,16,512]{2,1,0:T(8,128)(2,1)S(1)} %get-tuple-element.34), channel_id=1, source_target_pairs={{0,8},{1,9},{2,10},{3,11},{4,12},{5,13},{6,14},{7,15},{8,0},{9,1},... | collective-permute-start | bytes 196616 | tf_op jit(solution)/shard_map/ppermute | solution.py:177
  45.6 1.6 %collective-permute-start.11 = (bf16[4,16,512]{2,1,0:T(8,128)(2,1)S(1)}, bf16[4,16,512]{2,1,0:T(8,128)(2,1)S(1)}, u32[]{:S(2)}, u32[]{:S(2)}) collective-permute-start(bf16[4,16,512]{2,1,0:T(8,128)(2,1)S(1)} %get-tuple-element.35), channel_id=1, source_target_pairs={{0,12},{1,13},{2,14},{3,15},{4,0},{5,1},{6,2},{7,3},{8,4},{9,5},{1... | collective-permute-start | bytes 196616 | tf_op jit(solution)/shard_map/ppermute | solution.py:177
  47.1 0.7 %collective-permute-done.9.refs_5_ = bf16[4,16,512]{2,1,0:T(8,128)(2,1)S(1)} collective-permute-done((bf16[4,16,512]{2,1,0:T(8,128)(2,1)S(1)}, bf16[4,16,512]{2,1,0:T(8,128)(2,1)S(1)}, u32[]{:S(2)}, u32[]{:S(2)}) %collective-permute-start.9) | collective-permute-done | bytes 65568 | tf_op jit(solution)/shard_map/ppermute | solution.py:177
  47.9 1.1 %collective-permute-done.10.refs_6_ = bf16[4,16,512]{2,1,0:T(8,128)(2,1)S(1)} collective-permute-done((bf16[4,16,512]{2,1,0:T(8,128)(2,1)S(1)}, bf16[4,16,512]{2,1,0:T(8,128)(2,1)S(1)}, u32[]{:S(2)}, u32[]{:S(2)}) %collective-permute-start.10) | collective-permute-done | bytes 65568 | tf_op jit(solution)/shard_map/ppermute | solution.py:177
  48.9 0.9 %collective-permute-done.11.refs_7_ = bf16[4,16,512]{2,1,0:T(8,128)(2,1)S(1)} collective-permute-done((bf16[4,16,512]{2,1,0:T(8,128)(2,1)S(1)}, bf16[4,16,512]{2,1,0:T(8,128)(2,1)S(1)}, u32[]{:S(2)}, u32[]{:S(2)}) %collective-permute-start.11) | collective-permute-done | bytes 65568 | tf_op jit(solution)/shard_map/ppermute | solution.py:177
  49.8 1.4 %finish.1 = (f32[8,2,8,512]{3,2,1,0:T(8,128)}, f32[16,8,512]{2,1,0:T(8,128)S(1)}) custom-call(s32[128]{0:T(128)S(1)} %copy-done.2, f32[4,16,512]{2,1,0:T(8,128)S(1)} %get-tuple-element.24.refs_0_, bf16[4,16,512]{2,1,0:T(8,128)(2,1)S(1)} %collective-permute-done.3.refs_1_, bf16[4,16,512]{2,1,0:T(8,128)(2,1)S(1)} %collective-permute-done.4.refs_2_, ...), custom_call_target="tpu_custom_call" | custom-call | tf_op jit(solution)/shard_map/finish/pallas_call | solution.py:138
  51.2 13.4 %all_to_all.11.parts = f32[16,8,512]{2,1,0:T(8,128)} all-to-all(f32[16,8,512]{2,1,0:T(8,128)S(1)} %get-tuple-element.37), channel_id=1, replica_groups=mesh['block'=8,'row'=16] {'row'}, dimensions={0} | all-to-all | bytes 524288 | tf_op jit(solution)/shard_map/all_to_all | solution.py:188
  64.6 1.6 %mean.1 = f32[8,512]{1,0:T(8,128)} custom-call(f32[16,8,512]{2,1,0:T(8,128)} %all_to_all.11.parts, s32[1,128]{1,0:T(1,128)} %bitcast.13), custom_call_target="tpu_custom_call" | custom-call | tf_op jit(solution)/shard_map/mean/pallas_call | solution.py:189
  (14 shorter events, 0.0 us)
Async XLA Ops:
  0.6 2.3 %copy-start = (bf16[4096,128]{1,0:T(8,128)(2,1)S(1)}, bf16[4096,128]{1,0:T(8,128)(2,1)}, u32[]{:S(2)}) copy-start(bf16[4096,128]{1,0:T(8,128)(2,1)} %param.4) | copy-start | bytes 3145732
  2.9 15.5 %copy-start.1 = (bf16[8,2,128,512]{3,2,1,0:T(8,128)(2,1)S(1)}, bf16[8,2,128,512]{3,2,1,0:T(8,128)(2,1)}, u32[]{:S(2)}) copy-start(bf16[8,2,128,512]{3,2,1,0:T(8,128)(2,1)} %param.7) | copy-start | bytes 6291460
  18.5 31.3 %copy-start.2 = (s32[128]{0:T(128)S(1)}, s32[128]{0:T(128)}, u32[]{:S(2)}) copy-start(s32[128]{0:T(128)} %tallies.1) | copy-start | bytes 1540
  19.3 11.2 %collective-permute-start = (bf16[4,2,32,512]{3,2,1,0:T(8,128)(2,1)S(1)}, bf16[4,2,32,512]{3,2,1,0:T(8,128)(2,1)S(1)}, u32[]{:S(2)}, u32[]{:S(2)}) collective-permute-start(bf16[4,2,32,512]{3,2,1,0:T(8,128)(2,1)S(1)} %get-tuple-element.21), channel_id=1, source_target_pairs={{0,4},{1,5},{2,6},{3,7},{4,8},{5,9},{6,10},{7,11},{8,12},{9,13},{1... | collective-permute-start | bytes 786440 | tf_op jit(solution)/shard_map/ppermute | solution.py:177
  20.9 14.0 %collective-permute-start.1 = (bf16[4,2,32,512]{3,2,1,0:T(8,128)(2,1)S(1)}, bf16[4,2,32,512]{3,2,1,0:T(8,128)(2,1)S(1)}, u32[]{:S(2)}, u32[]{:S(2)}) collective-permute-start(bf16[4,2,32,512]{3,2,1,0:T(8,128)(2,1)S(1)} %get-tuple-element.22), channel_id=1, source_target_pairs={{0,8},{1,9},{2,10},{3,11},{4,12},{5,13},{6,14},{7,15},{8,0},{9,1},... | collective-permute-start | bytes 786440 | tf_op jit(solution)/shard_map/ppermute | solution.py:177
  23.6 11.3 %collective-permute-start.2 = (bf16[4,2,32,512]{3,2,1,0:T(8,128)(2,1)S(1)}, bf16[4,2,32,512]{3,2,1,0:T(8,128)(2,1)S(1)}, u32[]{:S(2)}, u32[]{:S(2)}) collective-permute-start(bf16[4,2,32,512]{3,2,1,0:T(8,128)(2,1)S(1)} %get-tuple-element.23), channel_id=1, source_target_pairs={{0,12},{1,13},{2,14},{3,15},{4,0},{5,1},{6,2},{7,3},{8,4},{9,5},{1... | collective-permute-start | bytes 786440 | tf_op jit(solution)/shard_map/ppermute | solution.py:177
  25.0 15.6 %collective-permute-start.6 = (bf16[4,2,32,512]{3,2,1,0:T(8,128)(2,1)S(1)}, bf16[4,2,32,512]{3,2,1,0:T(8,128)(2,1)S(1)}, u32[]{:S(2)}, u32[]{:S(2)}) collective-permute-start(bf16[4,2,32,512]{3,2,1,0:T(8,128)(2,1)S(1)} %get-tuple-element.29), channel_id=1, source_target_pairs={{0,1},{1,2},{2,3},{3,0},{4,5},{5,6},{6,7},{7,4},{8,9},{9,10},{10,1... | collective-permute-start | bytes 786440 | tf_op jit(solution)/shard_map/ppermute | solution.py:177
  26.9 15.2 %collective-permute-start.7 = (bf16[4,2,32,512]{3,2,1,0:T(8,128)(2,1)S(1)}, bf16[4,2,32,512]{3,2,1,0:T(8,128)(2,1)S(1)}, u32[]{:S(2)}, u32[]{:S(2)}) collective-permute-start(bf16[4,2,32,512]{3,2,1,0:T(8,128)(2,1)S(1)} %get-tuple-element.30), channel_id=1, source_target_pairs={{0,2},{1,3},{2,0},{3,1},{4,6},{5,7},{6,4},{7,5},{8,10},{9,11},{10,... | collective-permute-start | bytes 786440 | tf_op jit(solution)/shard_map/ppermute | solution.py:177
  30.5 11.6 %collective-permute-start.8 = (bf16[4,2,32,512]{3,2,1,0:T(8,128)(2,1)S(1)}, bf16[4,2,32,512]{3,2,1,0:T(8,128)(2,1)S(1)}, u32[]{:S(2)}, u32[]{:S(2)}) collective-permute-start(bf16[4,2,32,512]{3,2,1,0:T(8,128)(2,1)S(1)} %get-tuple-element.31), channel_id=1, source_target_pairs={{0,3},{1,0},{2,1},{3,2},{4,7},{5,4},{6,5},{7,6},{8,11},{9,8},{10,9... | collective-permute-start | bytes 786440 | tf_op jit(solution)/shard_map/ppermute | solution.py:177
  35.0 10.5 %collective-permute-start.3 = (bf16[4,16,512]{2,1,0:T(8,128)(2,1)S(1)}, bf16[4,16,512]{2,1,0:T(8,128)(2,1)S(1)}, u32[]{:S(2)}, u32[]{:S(2)}) collective-permute-start(bf16[4,16,512]{2,1,0:T(8,128)(2,1)S(1)} %get-tuple-element.25), channel_id=1, source_target_pairs={{0,1},{1,2},{2,3},{3,0},{4,5},{5,6},{6,7},{7,4},{8,9},{9,10},{10,1... | collective-permute-start | bytes 196616 | tf_op jit(solution)/shard_map/ppermute | solution.py:177
  37.0 10.1 %collective-permute-start.4 = (bf16[4,16,512]{2,1,0:T(8,128)(2,1)S(1)}, bf16[4,16,512]{2,1,0:T(8,128)(2,1)S(1)}, u32[]{:S(2)}, u32[]{:S(2)}) collective-permute-start(bf16[4,16,512]{2,1,0:T(8,128)(2,1)S(1)} %get-tuple-element.26), channel_id=1, source_target_pairs={{0,2},{1,3},{2,0},{3,1},{4,6},{5,7},{6,4},{7,5},{8,10},{9,11},{10,... | collective-permute-start | bytes 196616 | tf_op jit(solution)/shard_map/ppermute | solution.py:177
  40.6 6.5 %collective-permute-start.5 = (bf16[4,16,512]{2,1,0:T(8,128)(2,1)S(1)}, bf16[4,16,512]{2,1,0:T(8,128)(2,1)S(1)}, u32[]{:S(2)}, u32[]{:S(2)}) collective-permute-start(bf16[4,16,512]{2,1,0:T(8,128)(2,1)S(1)} %get-tuple-element.27), channel_id=1, source_target_pairs={{0,3},{1,0},{2,1},{3,2},{4,7},{5,4},{6,5},{7,6},{8,11},{9,8},{10,9... | collective-permute-start | bytes 196616 | tf_op jit(solution)/shard_map/ppermute | solution.py:177
  42.3 5.5 %collective-permute-start.9 = (bf16[4,16,512]{2,1,0:T(8,128)(2,1)S(1)}, bf16[4,16,512]{2,1,0:T(8,128)(2,1)S(1)}, u32[]{:S(2)}, u32[]{:S(2)}) collective-permute-start(bf16[4,16,512]{2,1,0:T(8,128)(2,1)S(1)} %get-tuple-element.33), channel_id=1, source_target_pairs={{0,4},{1,5},{2,6},{3,7},{4,8},{5,9},{6,10},{7,11},{8,12},{9,13},{1... | collective-permute-start | bytes 196616 | tf_op jit(solution)/shard_map/ppermute | solution.py:177
  43.2 5.8 %collective-permute-start.10 = (bf16[4,16,512]{2,1,0:T(8,128)(2,1)S(1)}, bf16[4,16,512]{2,1,0:T(8,128)(2,1)S(1)}, u32[]{:S(2)}, u32[]{:S(2)}) collective-permute-start(bf16[4,16,512]{2,1,0:T(8,128)(2,1)S(1)} %get-tuple-element.34), channel_id=1, source_target_pairs={{0,8},{1,9},{2,10},{3,11},{4,12},{5,13},{6,14},{7,15},{8,0},{9,1},... | collective-permute-start | bytes 196616 | tf_op jit(solution)/shard_map/ppermute | solution.py:177
  45.6 4.3 %collective-permute-start.11 = (bf16[4,16,512]{2,1,0:T(8,128)(2,1)S(1)}, bf16[4,16,512]{2,1,0:T(8,128)(2,1)S(1)}, u32[]{:S(2)}, u32[]{:S(2)}) collective-permute-start(bf16[4,16,512]{2,1,0:T(8,128)(2,1)S(1)} %get-tuple-element.35), channel_id=1, source_target_pairs={{0,12},{1,13},{2,14},{3,15},{4,0},{5,1},{6,2},{7,3},{8,4},{9,5},{1... | collective-permute-start | bytes 196616 | tf_op jit(solution)/shard_map/ppermute | solution.py:177

commit v3 on v0

v3 whole, which is shorter than its diff:
```python
import jax
import jax.numpy as jnp
from jax import lax
from jax.experimental import pallas as pl
from jax.experimental.pallas import tpu as pltpu
from jax.sharding import PartitionSpec as P

FRAMES_PER_SEG = 256
FARTHEST_FIRST = (2, 1, 3)
PARTS = 4
SIDE = 4
VMEM = pl.BlockSpec(memory_space=pltpu.VMEM)
SMEM = pl.BlockSpec(memory_space=pltpu.SMEM)
SMALL = 8 << 20
bf16, f32 = jnp.bfloat16, jnp.float32


def transform_kernel(
    tallies_hbm, slots_hbm, snapshots_hbm, spectra, acc, tallies, slots, snapshots, sems
):
    copies = [
        pltpu.make_async_copy(tallies_hbm, tallies, sems.at[0]),
        pltpu.make_async_copy(slots_hbm, slots, sems.at[1]),
    ]
    share = snapshots.shape[0] // PARTS
    for part in range(PARTS):
        rows = pl.ds(part * share, share)
        copies.append(
            pltpu.make_async_copy(
                snapshots_hbm.at[rows, :], snapshots.at[rows, :], sems.at[2 + part]
            )
        )
    for copy in copies:
        copy.start()
    copies[0].wait()
    copies[1].wait()
    freqs, _, blocks, points = spectra.shape
    start = lax.axis_index("block") * blocks
    spots = lax.broadcasted_iota(jnp.int32, (blocks, FRAMES_PER_SEG), 0)
    lengths = jnp.zeros((blocks, FRAMES_PER_SEG), jnp.int32)
    for j in range(blocks):
        lengths = jnp.where(spots == j, tallies[start + j], lengths)
    times = lax.broadcasted_iota(jnp.int32, (blocks, FRAMES_PER_SEG), 1)
    angle = jnp.pi * (times.astype(f32) + 0.5) / lengths.astype(f32)
    window = jnp.where(times < lengths, jnp.sin(angle) ** 2, 0.0)
    window = window * (1.0 / jnp.sqrt(jnp.sum(window * window, axis=1, keepdims=True)))
    turns = lax.dot_general(
        slots[...].astype(f32).astype(bf16),
        times[:1].astype(f32).astype(bf16),
        (((0,), (0,)), ((), ())),
        preferred_element_type=f32,
    )
    turns = (turns.astype(jnp.int32) % FRAMES_PER_SEG).astype(f32)
    phase = turns * (2.0 * jnp.pi / FRAMES_PER_SEG)
    waves = jnp.concatenate([jnp.cos(phase), -jnp.sin(phase)], axis=0)
    for j in range(blocks):
        if j % (blocks // PARTS) == 0:
            copies[2 + j // (blocks // PARTS)].wait()
        table = (window[j : j + 1] * waves).astype(bf16)
        frames = snapshots[j * FRAMES_PER_SEG : (j + 1) * FRAMES_PER_SEG, :]
        acc[pl.ds(j, 2 * freqs, stride=blocks), :] = jnp.dot(
            table, frames, preferred_element_type=f32
        )
    for c in range(2):
        rows = acc[c * freqs * blocks : (c + 1) * freqs * blocks, :]
        spectra[:, c] = rows.reshape(freqs, blocks, points).astype(bf16)


def transform(tallies, slots, snapshots):
    blocks, points = snapshots.shape[0] // FRAMES_PER_SEG, snapshots.shape[1]
    freqs = slots.shape[0]
    return pl.pallas_call(
        transform_kernel,
        out_shape=jax.ShapeDtypeStruct((freqs, 2, blocks, points), bf16),
        in_specs=[pl.BlockSpec(memory_space=pltpu.HBM)] * 3,
        out_specs=VMEM,
        scratch_shapes=[
            pltpu.VMEM((2 * freqs * blocks, points), f32),
            pltpu.SMEM(tallies.shape, jnp.int32),
            pltpu.VMEM((1, freqs), jnp.int32),
            pltpu.VMEM(snapshots.shape, bf16),
            pltpu.SemaphoreType.DMA((2 + PARTS,)),
        ],
        compiler_params=pltpu.CompilerParams(vmem_limit_bytes=SMALL),
        name="transform",
    )(
        *[
            pltpu.with_memory_space_constraint(v, pltpu.HBM)
            for v in (tallies, slots.reshape(1, -1), snapshots)
        ]
    )


def places():
    row = lax.axis_index("row")
    x, z = row // SIDE, row % SIDE
    x_first = lax.axis_index("block") % 2 == 0
    return x_first, jnp.where(x_first, x, z), jnp.where(x_first, z, x)


def project_kernel(spectra, modes, *refs):
    outs, acc = refs[:-1], refs[-1]
    x_first, place, _ = places()
    step = jnp.where(x_first, 1, SIDE)
    freqs, points, width = spectra.shape[1], spectra.shape[4], modes.shape[2]
    blocks = spectra.shape[0] * spectra.shape[3]
    for k in range(freqs):
        real = spectra[:, k, 0].reshape(blocks, points)
        imag = spectra[:, k, 1].reshape(blocks, points)
        left = jnp.concatenate(
            [
                jnp.concatenate([real, imag], axis=1),
                jnp.concatenate([imag, -real], axis=1),
            ],
            axis=0,
        )
        slot = k % 2
        acc[slot] = jnp.dot(left, modes[k], preferred_element_type=f32).reshape(acc.shape[1:])
        for i in range(SIDE):
            first = (place + i) % SIDE * jnp.where(x_first, SIDE, 1)
            piece = jnp.stack([acc[slot, :, first + j * step] for j in range(SIDE)], axis=1)
            outs[i][k] = piece.reshape(2, -1, width).astype(outs[i].dtype)


def project(spectra, modes):
    freqs, width = modes.shape[0], modes.shape[2]
    blocks = spectra.shape[0] * spectra.shape[3]
    piece = (freqs, 2, blocks // SIDE, width)
    return pl.pallas_call(
        project_kernel,
        out_shape=[jax.ShapeDtypeStruct(piece, f32 if i == 0 else bf16) for i in range(SIDE)],
        in_specs=[VMEM, VMEM],
        out_specs=[VMEM] * SIDE,
        scratch_shapes=[pltpu.VMEM((2, 2, SIDE * SIDE, blocks // (SIDE * SIDE), width), f32)],
        compiler_params=pltpu.CompilerParams(vmem_limit_bytes=SMALL),
        name="project",
    )(spectra, modes)


def fold_kernel(own, first, second, third, *refs):
    outs, acc = refs[:-1], refs[-1]
    _, _, place = places()
    width = own.shape[3]
    for k in range(own.shape[0]):
        total = own[k] + first[k].astype(f32) + second[k].astype(f32) + third[k].astype(f32)
        acc[k % 2] = total.reshape(acc.shape[1:])
        for i in range(SIDE):
            piece = acc[k % 2, :, (place + i) % SIDE].reshape(-1, width)
            outs[i][k] = piece.astype(outs[i].dtype)


def fold(parts):
    freqs, _, blocks, width = parts[0].shape
    piece = (freqs, 2 * blocks // SIDE, width)
    return pl.pallas_call(
        fold_kernel,
        out_shape=[jax.ShapeDtypeStruct(piece, f32 if i == 0 else bf16) for i in range(SIDE)],
        in_specs=[VMEM] * SIDE,
        out_specs=[VMEM] * SIDE,
        scratch_shapes=[pltpu.VMEM((2, 2, SIDE, blocks // SIDE, width), f32)],
        compiler_params=pltpu.CompilerParams(vmem_limit_bytes=SMALL),
        name="fold",
    )(*parts)


def energy_kernel(tallies, all_tallies, own, first, second, third, energy, own_energy):
    freqs, rows, width = own.shape
    blocks = rows // 2
    start = lax.axis_index("row") * blocks
    total_weight = jnp.sum(all_tallies[...].astype(f32), axis=1, keepdims=True)
    spots = lax.broadcasted_iota(jnp.int32, (rows, width), 0) % blocks
    weights = jnp.zeros((rows, width), f32)
    for j in range(blocks):
        weights = jnp.where(spots == j, tallies[start + j].astype(f32), weights)
    weights = weights / total_weight
    for k in range(freqs):
        total = own[k] + first[k].astype(f32) + second[k].astype(f32) + third[k].astype(f32)
        power = jnp.sum(weights * (total * total), axis=0, keepdims=True)
        own_energy[k : k + 1, :] = power
    energy[...] = jnp.broadcast_to(own_energy[...].astype(bf16)[None], energy.shape)


def coefficients_kernel(own, first, second, third, coefficients):
    blocks = coefficients.shape[0]
    for k in range(own.shape[0]):
        total = own[k] + first[k].astype(f32) + second[k].astype(f32) + third[k].astype(f32)
        coefficients[:, 0, k, :] = total[:blocks]
        coefficients[:, 1, k, :] = total[blocks:]


def sum_kernel(parts, energy):
    energy[...] = jnp.sum(parts[...].astype(f32), axis=0)


def shards(snapshots, usable_frame_tallies, retained_frequency_slots, modes):
    row_width = snapshots.shape[1]
    rows = lax.axis_size("row")
    groups = lax.axis_size("block")
    spectra = transform(usable_frame_tallies, retained_frequency_slots, snapshots)
    spectra = spectra.reshape((groups, -1) + spectra.shape[1:])
    moved = lax.all_to_all(spectra, "block", split_axis=0, concat_axis=0, tiled=True)

    def along(value, stage, distance):
        pairs = []
        for block in range(groups):
            for x in range(SIDE):
                for z in range(SIDE):
                    if (block % 2 == 0) == (stage == 0):
                        target = (x + distance) % SIDE * SIDE + z
                    else:
                        target = x * SIDE + (z + distance) % SIDE
                    pairs.append((block * rows + x * SIDE + z, block * rows + target))
        return lax.ppermute(value, ("block", "row"), pairs)

    mode_rows = modes.reshape(modes.shape[0], 2 * row_width, modes.shape[3])
    pieces = project(moved, mode_rows)
    pieces = fold([pieces[0]] + [along(pieces[i], 0, i) for i in FARTHEST_FIRST])
    last = [pieces[0]] + [along(pieces[i], 1, i) for i in FARTHEST_FIRST]
    freqs, double, width = last[0].shape
    energy_parts = pl.pallas_call(
        energy_kernel,
        out_shape=jax.ShapeDtypeStruct((rows, freqs, width), bf16),
        in_specs=[SMEM] + [VMEM] * (1 + SIDE),
        out_specs=VMEM,
        scratch_shapes=[pltpu.VMEM((freqs, width), f32)],
        compiler_params=pltpu.CompilerParams(vmem_limit_bytes=SMALL),
        name="energy",
    )(usable_frame_tallies, usable_frame_tallies.reshape(1, -1), *last)
    swapped = lax.all_to_all(energy_parts, "row", 0, 0, tiled=True)
    coefficients = pl.pallas_call(
        coefficients_kernel,
        out_shape=jax.ShapeDtypeStruct((double // 2, 2, freqs, width), f32),
        in_specs=[VMEM] * SIDE,
        out_specs=VMEM,
        compiler_params=pltpu.CompilerParams(vmem_limit_bytes=SMALL),
        name="coefficients",
    )(*last)
    energy = pl.pallas_call(
        sum_kernel,
        out_shape=jax.ShapeDtypeStruct((freqs, width), f32),
        in_specs=[VMEM],
        out_specs=VMEM,
        compiler_params=pltpu.CompilerParams(vmem_limit_bytes=SMALL),
        name="total",
    )(swapped)
    return (coefficients, energy)


def solution(mesh):
    placed = (P("block", "row"), P(), P(), P("block", None, "row", None))
    return jax.shard_map(
        shards,
        mesh=mesh,
        in_specs=placed,
        out_specs=(P("row", None, "block", None), P("block", None)),
        check_vma=False,
    )
```

time: 147 us -> 62.2 us (0.42)
  waiting for transfers between devices: 103 us -> 20.1 us
  starting transfers between devices: 0.04 us -> 20.2 us
  between operations: 14.1 us -> 0.68 us
  other arithmetic: 7.01 us -> 0 us
  Pallas kernels: 0 us -> 6.15 us
  matrix products: 4.33 us -> 0 us
  local copies, waits for them, and re-layouts: 3.14 us -> 0.01 us
    psum x1 -> x0, waiting for transfers between devices: 103 us -> none  [shards(): lax.psum(jnp.einsum('bckx,kxm->bckm', stacked_left, mode_rows, preferred_...]
    ppermute x0 -> x6, starting transfers between devices: none -> 13.5 us  [along(): return lax.ppermute(value, ('block', 'row'), pairs)]
    ppermute x0 -> x6, waiting for transfers between devices: none -> 13.1 us  [along(): return lax.ppermute(value, ('block', 'row'), pairs)]
    all_to_all x0 -> x1, waiting for transfers between devices: none -> 7.03 us  [shards(): swapped = lax.all_to_all(energy_parts, 'row', 0, 0, tiled=True)]
    all_to_all x0 -> x1, starting transfers between devices: none -> 6.68 us  [shards(): swapped = lax.all_to_all(energy_parts, 'row', 0, 0, tiled=True)]
    pallas_call x0 -> x6, Pallas kernels: none -> 6.15 us  [the longest x1 2.3 us: transform(): pl.pallas_call(transform_kernel, out_shape=jax.ShapeDtypeStruct((freqs, 2...]
    dot_general x2 -> x0, matrix products: 4.33 us -> none  [the longest x1 2.68 us: shards(): jnp.einsum('bckx,kxm->bckm', stacked_left, mode_rows, preferred_element_t...]
    reduce_sum x3 -> x0, other arithmetic: 3.64 us -> none  [the longest x1 2.82 us: shards(): energy = jnp.sum(weights[:, None, None] * power, axis=0) / total_weight]
  transfers between devices with their start and end apart: 1 -> 7, of which waited for: 1 -> 5; matrix products, arithmetic and copies ran while one was open for 0% -> 0% of each run, Pallas kernels for 0% -> 1%
where the time goes in v3:
time: 62.2 us; the launch traced here: 62 us
  starting transfers between devices  20.2 us (32%)
  waiting for transfers between devices  20.1 us (32%)
  blocking collectives  14.7 us (24%)
  Pallas kernels  6.15 us (10%)
  between operations  0.68 us (1%)
    all_to_all x1, blocking collectives, shards(): lax.all_to_all(spectra, 'block', split_axis=0, concat_axis=0, tiled=True)  14.7 us
    ppermute x6, starting transfers between devices, along(): return lax.ppermute(value, ('block', 'row'), pairs)  13.5 us
    ppermute x6, waiting for transfers between devices, along(): return lax.ppermute(value, ('block', 'row'), pairs)  13.1 us
    all_to_all x1, waiting for transfers between devices, shards(): swapped = lax.all_to_all(energy_parts, 'row', 0, 0, tiled=True)  7.03 us
    all_to_all x1, starting transfers between devices, shards(): swapped = lax.all_to_all(energy_parts, 'row', 0, 0, tiled=True)  6.68 us
    pallas_call x1, Pallas kernels, transform(): pl.pallas_call(transform_kernel, out_shape=jax.ShapeDtypeStruct((freqs, 2...  2.3 us
    pallas_call x1, Pallas kernels, shards(): pl.pallas_call(energy_kernel, out_shape=jax.ShapeDtypeStruct((rows, freqs...  1.33 us
  transfers between devices with their start and end apart: 7, of which 5 were waited for; matrix products, arithmetic and copies ran while one was open for 0% of the time, Pallas kernels for 1%

profile of v3, /device:TPU:0, one launch (start us, length us, event | category | flops | bytes accessed | tf_op | source)
XLA Modules:
  0.0 62.0 jit_solution(9953100128186560039)
XLA Ops:
  0.6 0.0 copy-start
  0.6 2.3 %transform.1 = bf16[64,2,16,128]{3,2,1,0:T(8,128)(2,1)S(1)} custom-call(s32[128]{0:T(128)} %tallies.1, s32[1,64]{1,0:T(1,128)} %bitcast.7, bf16[4096,128]{1,0:T(8,128)(2,1)} %snapshots_hbm.1), custom_call_target="tpu_custom_call" | custom-call | tf_op jit(solution)/shard_map/transform/pallas_call | solution.py:72
  2.9 14.7 %all_to_all.10.spectra = bf16[8,8,2,16,128]{4,3,2,1,0:T(8,128)(2,1)S(1)} all-to-all(bf16[8,8,2,16,128]{4,3,2,1,0:T(8,128)(2,1)S(1)} %bitcast.5), channel_id=1, replica_groups=mesh['block'=8,'row'=16] {'block'}, dimensions={0} | all-to-all | bytes 1048576 | tf_op jit(solution)/shard_map/all_to_all | solution.py:201
  17.7 0.0 copy-done
  17.7 0.0 copy-start.1
  17.7 0.8 %project.1 = (f32[8,2,32,512]{3,2,1,0:T(8,128)S(1)}, bf16[8,2,32,512]{3,2,1,0:T(8,128)(2,1)S(1)}, bf16[8,2,32,512]{3,2,1,0:T(8,128)(2,1)S(1)}, bf16[8,2,32,512]{3,2,1,0:T(8,128)(2,1)S(1)}) custom-call(bf16[8,8,2,16,128]{4,3,2,1,0:T(8,128)(2,1)S(1)} %all_to_all.10.spectra, bf16[8,256,512]{2,1,0:T(8,128)(2,1)S(1)} %bitcast.4), custom_call_target="tpu_custom_call" | custom-call | tf_op jit(solution)/shard_map/project/pallas_call | solution.py:129
  18.5 3.1 %collective-permute-start = (bf16[8,2,32,512]{3,2,1,0:T(8,128)(2,1)S(1)}, bf16[8,2,32,512]{3,2,1,0:T(8,128)(2,1)S(1)}, u32[]{:S(2)}, u32[]{:S(2)}) collective-permute-start(bf16[8,2,32,512]{3,2,1,0:T(8,128)(2,1)S(1)} %get-tuple-element.11), channel_id=1, source_target_pairs={{0,8},{1,9},{2,10},{3,11},{4,12},{5,13},{6,14},{7,15},{8,0},{9,1},... | collective-permute-start | bytes 1572872 | tf_op jit(solution)/shard_map/ppermute | solution.py:213
  21.6 0.6 collective-permute-start.1
  22.2 2.6 %collective-permute-start.2 = (bf16[8,2,32,512]{3,2,1,0:T(8,128)(2,1)S(1)}, bf16[8,2,32,512]{3,2,1,0:T(8,128)(2,1)S(1)}, u32[]{:S(2)}, u32[]{:S(2)}) collective-permute-start(bf16[8,2,32,512]{3,2,1,0:T(8,128)(2,1)S(1)} %get-tuple-element.13), channel_id=1, source_target_pairs={{0,12},{1,13},{2,14},{3,15},{4,0},{5,1},{6,2},{7,3},{8,4},{9,5},{1... | collective-permute-start | bytes 1572872 | tf_op jit(solution)/shard_map/ppermute | solution.py:213
  24.9 4.5 %collective-permute-done.first = bf16[8,2,32,512]{3,2,1,0:T(8,128)(2,1)S(1)} collective-permute-done((bf16[8,2,32,512]{3,2,1,0:T(8,128)(2,1)S(1)}, bf16[8,2,32,512]{3,2,1,0:T(8,128)(2,1)S(1)}, u32[]{:S(2)}, u32[]{:S(2)}) %collective-permute-start) | collective-permute-done | bytes 524320 | tf_op jit(solution)/shard_map/ppermute | solution.py:213
  29.4 5.5 %collective-permute-done.1.second = bf16[8,2,32,512]{3,2,1,0:T(8,128)(2,1)S(1)} collective-permute-done((bf16[8,2,32,512]{3,2,1,0:T(8,128)(2,1)S(1)}, bf16[8,2,32,512]{3,2,1,0:T(8,128)(2,1)S(1)}, u32[]{:S(2)}, u32[]{:S(2)}) %collective-permute-start.1) | collective-permute-done | bytes 524320 | tf_op jit(solution)/shard_map/ppermute | solution.py:213
  34.9 0.1 collective-permute-done.2.third
  35.0 0.3 fold.1
  35.3 4.0 %collective-permute-start.3 = (bf16[8,16,512]{2,1,0:T(8,128)(2,1)S(1)}, bf16[8,16,512]{2,1,0:T(8,128)(2,1)S(1)}, u32[]{:S(2)}, u32[]{:S(2)}) collective-permute-start(bf16[8,16,512]{2,1,0:T(8,128)(2,1)S(1)} %get-tuple-element.15), channel_id=1, source_target_pairs={{0,2},{1,3},{2,0},{3,1},{4,6},{5,7},{6,4},{7,5},{8,10},{9,11},{10,... | collective-permute-start | bytes 393224 | tf_op jit(solution)/shard_map/ppermute | solution.py:213
  39.3 1.0 %collective-permute-start.4 = (bf16[8,16,512]{2,1,0:T(8,128)(2,1)S(1)}, bf16[8,16,512]{2,1,0:T(8,128)(2,1)S(1)}, u32[]{:S(2)}, u32[]{:S(2)}) collective-permute-start(bf16[8,16,512]{2,1,0:T(8,128)(2,1)S(1)} %get-tuple-element.16), channel_id=1, source_target_pairs={{0,1},{1,2},{2,3},{3,0},{4,5},{5,6},{6,7},{7,4},{8,9},{9,10},{10,1... | collective-permute-start | bytes 393224 | tf_op jit(solution)/shard_map/ppermute | solution.py:213
  40.3 2.2 %collective-permute-start.5 = (bf16[8,16,512]{2,1,0:T(8,128)(2,1)S(1)}, bf16[8,16,512]{2,1,0:T(8,128)(2,1)S(1)}, u32[]{:S(2)}, u32[]{:S(2)}) collective-permute-start(bf16[8,16,512]{2,1,0:T(8,128)(2,1)S(1)} %get-tuple-element.17), channel_id=1, source_target_pairs={{0,3},{1,0},{2,1},{3,2},{4,7},{5,4},{6,5},{7,6},{8,11},{9,8},{10,9... | collective-permute-start | bytes 393224 | tf_op jit(solution)/shard_map/ppermute | solution.py:213
  42.5 0.0 collective-permute-done.3.first
  42.5 2.9 %collective-permute-done.4.second = bf16[8,16,512]{2,1,0:T(8,128)(2,1)S(1)} collective-permute-done((bf16[8,16,512]{2,1,0:T(8,128)(2,1)S(1)}, bf16[8,16,512]{2,1,0:T(8,128)(2,1)S(1)}, u32[]{:S(2)}, u32[]{:S(2)}) %collective-permute-start.4) | collective-permute-done | bytes 131104 | tf_op jit(solution)/shard_map/ppermute | solution.py:213
  45.5 0.0 collective-permute-done.5.third
  45.5 0.0 copy-done.1
  45.5 1.3 %energy.1 = bf16[16,8,512]{2,1,0:T(8,128)(2,1)} custom-call(s32[128]{0:T(128)S(1)} %copy-done.1, s32[1,128]{1,0:T(1,128)S(1)} %bitcast.6, f32[8,16,512]{2,1,0:T(8,128)S(1)} %get-tuple-element.14.own, bf16[8,16,512]{2,1,0:T(8,128)(2,1)S(1)} %collective-permute-done.3.first, bf16[8,16,512]{2,1,0:T(8,128)(2,1)S(1)} %collective-permute-done.4.second, ...), custom_call_target="tpu_custom_call" | custom-call | tf_op jit(solution)/shard_map/energy/pallas_call | solution.py:220
  46.8 6.7 %all-to-all-start.1 = ((bf16[16,8,512]{2,1,0:T(8,128)(2,1)}), bf16[16,8,512]{2,1,0:T(8,128)(2,1)S(1)}, u32[]{:S(2)}, u32[]{:S(2)}) async-start(bf16[16,8,512]{2,1,0:T(8,128)(2,1)} %energy.1), calls=%async_computation.1 | async-start | bytes 262144 | tf_op jit(solution)/shard_map/all_to_all | solution.py:229
  53.5 0.8 %coefficients.1 = f32[8,2,8,512]{3,2,1,0:T(8,128)} custom-call(f32[8,16,512]{2,1,0:T(8,128)S(1)} %get-tuple-element.14.own, bf16[8,16,512]{2,1,0:T(8,128)(2,1)S(1)} %collective-permute-done.3.first, bf16[8,16,512]{2,1,0:T(8,128)(2,1)S(1)} %collective-permute-done.4.second, bf16[8,16,512]{2,1,0:T(8,128)(2,1)S(1)} %collective-permute-done.5.third), custom_call_target="tpu_custom_call" | custom-call | tf_op jit(solution)/shard_map/coefficients/pallas_call | solution.py:230
  54.3 7.0 %all-to-all-done.1.parts = bf16[16,8,512]{2,1,0:T(8,128)(2,1)S(1)} async-done(((bf16[16,8,512]{2,1,0:T(8,128)(2,1)}), bf16[16,8,512]{2,1,0:T(8,128)(2,1)S(1)}, u32[]{:S(2)}, u32[]{:S(2)}) %all-to-all-start.1) | async-done | bytes 131104 | tf_op jit(solution)/shard_map/all_to_all | solution.py:229
  61.3 0.6 %total.1 = f32[8,512]{1,0:T(8,128)} custom-call(bf16[16,8,512]{2,1,0:T(8,128)(2,1)S(1)} %all-to-all-done.1.parts), custom_call_target="tpu_custom_call" | custom-call | tf_op jit(solution)/shard_map/total/pallas_call | solution.py:238
Async XLA Ops:
  0.6 17.1 %copy-start = (bf16[8,2,128,512]{3,2,1,0:T(8,128)(2,1)S(1)}, bf16[8,2,128,512]{3,2,1,0:T(8,128)(2,1)}, u32[]{:S(2)}) copy-start(bf16[8,2,128,512]{3,2,1,0:T(8,128)(2,1)} %param.7) | copy-start | bytes 6291460
  17.7 27.8 %copy-start.1 = (s32[128]{0:T(128)S(1)}, s32[128]{0:T(128)}, u32[]{:S(2)}) copy-start(s32[128]{0:T(128)} %tallies.1) | copy-start | bytes 1540
  18.5 10.9 %collective-permute-start = (bf16[8,2,32,512]{3,2,1,0:T(8,128)(2,1)S(1)}, bf16[8,2,32,512]{3,2,1,0:T(8,128)(2,1)S(1)}, u32[]{:S(2)}, u32[]{:S(2)}) collective-permute-start(bf16[8,2,32,512]{3,2,1,0:T(8,128)(2,1)S(1)} %get-tuple-element.11), channel_id=1, source_target_pairs={{0,8},{1,9},{2,10},{3,11},{4,12},{5,13},{6,14},{7,15},{8,0},{9,1},... | collective-permute-start | bytes 1572872 | tf_op jit(solution)/shard_map/ppermute | solution.py:213
  21.6 13.3 %collective-permute-start.1 = (bf16[8,2,32,512]{3,2,1,0:T(8,128)(2,1)S(1)}, bf16[8,2,32,512]{3,2,1,0:T(8,128)(2,1)S(1)}, u32[]{:S(2)}, u32[]{:S(2)}) collective-permute-start(bf16[8,2,32,512]{3,2,1,0:T(8,128)(2,1)S(1)} %get-tuple-element.12), channel_id=1, source_target_pairs={{0,4},{1,5},{2,6},{3,7},{4,8},{5,9},{6,10},{7,11},{8,12},{9,13},{1... | collective-permute-start | bytes 1572872 | tf_op jit(solution)/shard_map/ppermute | solution.py:213
  22.2 12.8 %collective-permute-start.2 = (bf16[8,2,32,512]{3,2,1,0:T(8,128)(2,1)S(1)}, bf16[8,2,32,512]{3,2,1,0:T(8,128)(2,1)S(1)}, u32[]{:S(2)}, u32[]{:S(2)}) collective-permute-start(bf16[8,2,32,512]{3,2,1,0:T(8,128)(2,1)S(1)} %get-tuple-element.13), channel_id=1, source_target_pairs={{0,12},{1,13},{2,14},{3,15},{4,0},{5,1},{6,2},{7,3},{8,4},{9,5},{1... | collective-permute-start | bytes 1572872 | tf_op jit(solution)/shard_map/ppermute | solution.py:213
  35.3 7.2 %collective-permute-start.3 = (bf16[8,16,512]{2,1,0:T(8,128)(2,1)S(1)}, bf16[8,16,512]{2,1,0:T(8,128)(2,1)S(1)}, u32[]{:S(2)}, u32[]{:S(2)}) collective-permute-start(bf16[8,16,512]{2,1,0:T(8,128)(2,1)S(1)} %get-tuple-element.15), channel_id=1, source_target_pairs={{0,2},{1,3},{2,0},{3,1},{4,6},{5,7},{6,4},{7,5},{8,10},{9,11},{10,... | collective-permute-start | bytes 393224 | tf_op jit(solution)/shard_map/ppermute | solution.py:213
  39.3 6.2 %collective-permute-start.4 = (bf16[8,16,512]{2,1,0:T(8,128)(2,1)S(1)}, bf16[8,16,512]{2,1,0:T(8,128)(2,1)S(1)}, u32[]{:S(2)}, u32[]{:S(2)}) collective-permute-start(bf16[8,16,512]{2,1,0:T(8,128)(2,1)S(1)} %get-tuple-element.16), channel_id=1, source_target_pairs={{0,1},{1,2},{2,3},{3,0},{4,5},{5,6},{6,7},{7,4},{8,9},{9,10},{10,1... | collective-permute-start | bytes 393224 | tf_op jit(solution)/shard_map/ppermute | solution.py:213
  40.3 5.2 %collective-permute-start.5 = (bf16[8,16,512]{2,1,0:T(8,128)(2,1)S(1)}, bf16[8,16,512]{2,1,0:T(8,128)(2,1)S(1)}, u32[]{:S(2)}, u32[]{:S(2)}) collective-permute-start(bf16[8,16,512]{2,1,0:T(8,128)(2,1)S(1)} %get-tuple-element.17), channel_id=1, source_target_pairs={{0,3},{1,0},{2,1},{3,2},{4,7},{5,4},{6,5},{7,6},{8,11},{9,8},{10,9... | collective-permute-start | bytes 393224 | tf_op jit(solution)/shard_map/ppermute | solution.py:213
  46.8 14.5 %all-to-all-start.1 = ((bf16[16,8,512]{2,1,0:T(8,128)(2,1)}), bf16[16,8,512]{2,1,0:T(8,128)(2,1)S(1)}, u32[]{:S(2)}, u32[]{:S(2)}) async-start(bf16[16,8,512]{2,1,0:T(8,128)(2,1)} %energy.1), calls=%async_computation.1 | async-start | bytes 262144 | tf_op jit(solution)/shard_map/all_to_all | solution.py:229

commit v4 on v3

--- a/solution.py
+++ b/solution.py
@@ -15,8 +15,31 @@
 bf16, f32 = jnp.bfloat16, jnp.float32
 
 
-def transform_kernel(
-    tallies_hbm, slots_hbm, snapshots_hbm, spectra, acc, tallies, slots, snapshots, sems
+def windows(tallies, start, blocks):
+    spots = lax.broadcasted_iota(jnp.int32, (blocks, FRAMES_PER_SEG), 0)
+    lengths = jnp.zeros((blocks, FRAMES_PER_SEG), jnp.int32)
+    for j in range(blocks):
+        lengths = jnp.where(spots == j, tallies[start + j], lengths)
+    times = lax.broadcasted_iota(jnp.int32, (blocks, FRAMES_PER_SEG), 1)
+    angle = jnp.pi * (times.astype(f32) + 0.5) / lengths.astype(f32)
+    window = jnp.where(times < lengths, jnp.sin(angle) ** 2, 0.0)
+    return window * (1.0 / jnp.sqrt(jnp.sum(window * window, axis=1, keepdims=True)))
+
+
+def transform_blocks(window, waves, snapshots, acc, arrived):
+    blocks, rows = window.shape[0], waves.shape[0]
+    for j in range(blocks):
+        arrived(j)
+        table = (window[j : j + 1] * waves).astype(bf16)
+        frames = snapshots[j * FRAMES_PER_SEG : (j + 1) * FRAMES_PER_SEG, :]
+        acc[pl.ds(j, rows, stride=blocks), :] = jnp.dot(
+            table, frames, preferred_element_type=f32
+        )
+
+
+def own_kernel(
+    tallies_hbm, slots_hbm, snapshots_hbm, spectra, waves, other_window,
+    acc, tallies, slots, snapshots, sems,
 ):
     copies = [
         pltpu.make_async_copy(tallies_hbm, tallies, sems.at[0]),
@@ -34,61 +57,86 @@
         copy.start()
     copies[0].wait()
     copies[1].wait()
-    freqs, _, blocks, points = spectra.shape
-    start = lax.axis_index("block") * blocks
-    spots = lax.broadcasted_iota(jnp.int32, (blocks, FRAMES_PER_SEG), 0)
-    lengths = jnp.zeros((blocks, FRAMES_PER_SEG), jnp.int32)
-    for j in range(blocks):
-        lengths = jnp.where(spots == j, tallies[start + j], lengths)
-    times = lax.broadcasted_iota(jnp.int32, (blocks, FRAMES_PER_SEG), 1)
-    angle = jnp.pi * (times.astype(f32) + 0.5) / lengths.astype(f32)
-    window = jnp.where(times < lengths, jnp.sin(angle) ** 2, 0.0)
-    window = window * (1.0 / jnp.sqrt(jnp.sum(window * window, axis=1, keepdims=True)))
+    block = lax.axis_index("block")
+    core = block % 2
+    blocks = other_window.shape[0]
+    window = windows(tallies, block * blocks, blocks)
+    other_window[...] = windows(tallies, (block + 1 - 2 * core) * blocks, blocks)
+    times = lax.broadcasted_iota(jnp.int32, (1, FRAMES_PER_SEG), 1)
     turns = lax.dot_general(
         slots[...].astype(f32).astype(bf16),
-        times[:1].astype(f32).astype(bf16),
+        times.astype(f32).astype(bf16),
         (((0,), (0,)), ((), ())),
         preferred_element_type=f32,
     )
+    turns = turns.reshape(SIDE, 2, -1, FRAMES_PER_SEG)
+    turns = jnp.where(core == 0, turns[:, 0], turns[:, 1]).reshape(-1, FRAMES_PER_SEG)
     turns = (turns.astype(jnp.int32) % FRAMES_PER_SEG).astype(f32)
     phase = turns * (2.0 * jnp.pi / FRAMES_PER_SEG)
-    waves = jnp.concatenate([jnp.cos(phase), -jnp.sin(phase)], axis=0)
-    for j in range(blocks):
+    waves[...] = jnp.concatenate([jnp.cos(phase), -jnp.sin(phase)], axis=0)
+
+    def arrived(j):
         if j % (blocks // PARTS) == 0:
             copies[2 + j // (blocks // PARTS)].wait()
-        table = (window[j : j + 1] * waves).astype(bf16)
-        frames = snapshots[j * FRAMES_PER_SEG : (j + 1) * FRAMES_PER_SEG, :]
-        acc[pl.ds(j, 2 * freqs, stride=blocks), :] = jnp.dot(
-            table, frames, preferred_element_type=f32
-        )
-    for c in range(2):
-        rows = acc[c * freqs * blocks : (c + 1) * freqs * blocks, :]
-        spectra[:, c] = rows.reshape(freqs, blocks, points).astype(bf16)
+
+    transform_blocks(window, waves[...], snapshots, acc, arrived)
+    spectra[...] = acc[...].astype(bf16).reshape(spectra.shape)
+
+
+def other_kernel(own, waves, window, snapshots, *refs):
+    outs, acc = refs[:-1], refs[-1]
+    block = lax.axis_index("block")
+    y, core = block // 2, block % 2
+    transform_blocks(window[...], waves[...], snapshots, acc, lambda j: None)
+    _, _, freqs, blocks, points = own.shape
+    size = freqs * blocks
+    for i in range(SIDE):
+        target = (y + i) % SIDE
+        for c in range(2):
+            rows = pl.ds(pl.multiple_of((c * SIDE + target) * size, size), size)
+            outs[i][:, c, core] = own[c, target]
+            outs[i][:, c, 1 - core] = acc[rows, :].astype(bf16).reshape(freqs, blocks, points)
 
 
 def transform(tallies, slots, snapshots):
     blocks, points = snapshots.shape[0] // FRAMES_PER_SEG, snapshots.shape[1]
-    freqs = slots.shape[0]
-    return pl.pallas_call(
-        transform_kernel,
-        out_shape=jax.ShapeDtypeStruct((freqs, 2, blocks, points), bf16),
+    freqs = slots.shape[0] // (2 * SIDE)
+    rows = 2 * SIDE * freqs
+    swap = [(b, b ^ 1) for b in range(lax.axis_size("block"))]
+    others = lax.ppermute(snapshots, "block", swap)
+    own, waves, window = pl.pallas_call(
+        own_kernel,
+        out_shape=[
+            jax.ShapeDtypeStruct((2, SIDE, freqs, blocks, points), bf16),
+            jax.ShapeDtypeStruct((rows, FRAMES_PER_SEG), f32),
+            jax.ShapeDtypeStruct((blocks, FRAMES_PER_SEG), f32),
+        ],
         in_specs=[pl.BlockSpec(memory_space=pltpu.HBM)] * 3,
-        out_specs=VMEM,
+        out_specs=[VMEM] * 3,
         scratch_shapes=[
-            pltpu.VMEM((2 * freqs * blocks, points), f32),
+            pltpu.VMEM((rows * blocks, points), f32),
             pltpu.SMEM(tallies.shape, jnp.int32),
-            pltpu.VMEM((1, freqs), jnp.int32),
+            pltpu.VMEM((1, slots.shape[0]), jnp.int32),
             pltpu.VMEM(snapshots.shape, bf16),
             pltpu.SemaphoreType.DMA((2 + PARTS,)),
         ],
         compiler_params=pltpu.CompilerParams(vmem_limit_bytes=SMALL),
-        name="transform",
+        name="transform_own",
     )(
         *[
             pltpu.with_memory_space_constraint(v, pltpu.HBM)
             for v in (tallies, slots.reshape(1, -1), snapshots)
         ]
     )
+    return pl.pallas_call(
+        other_kernel,
+        out_shape=[jax.ShapeDtypeStruct((freqs, 2, 2, blocks, points), bf16)] * SIDE,
+        in_specs=[VMEM] * 4,
+        out_specs=[VMEM] * SIDE,
+        scratch_shapes=[pltpu.VMEM((rows * blocks, points), f32)],
+        compiler_params=pltpu.CompilerParams(vmem_limit_bytes=SMALL),
+        name="transform_other",
+    )(own, waves, window, others)
 
 
 def places():
@@ -98,15 +146,16 @@
     return x_first, jnp.where(x_first, x, z), jnp.where(x_first, z, x)
 
 
-def project_kernel(spectra, modes, *refs):
-    outs, acc = refs[:-1], refs[-1]
+def project_kernel(*refs):
+    spectra, modes, outs, acc = refs[:SIDE], refs[SIDE], refs[SIDE + 1 : -1], refs[-1]
     x_first, place, _ = places()
-    step = jnp.where(x_first, 1, SIDE)
-    freqs, points, width = spectra.shape[1], spectra.shape[4], modes.shape[2]
-    blocks = spectra.shape[0] * spectra.shape[3]
+    y = lax.axis_index("block") // 2
+    freqs, points, width = spectra[0].shape[0], spectra[0].shape[4], modes.shape[2]
     for k in range(freqs):
-        real = spectra[:, k, 0].reshape(blocks, points)
-        imag = spectra[:, k, 1].reshape(blocks, points)
+        real, imag = (
+            jnp.concatenate([part[k, c].reshape(-1, points) for part in spectra], axis=0)
+            for c in range(2)
+        )
         left = jnp.concatenate(
             [
                 jnp.concatenate([real, imag], axis=1),
@@ -117,24 +166,29 @@
         slot = k % 2
         acc[slot] = jnp.dot(left, modes[k], preferred_element_type=f32).reshape(acc.shape[1:])
         for i in range(SIDE):
-            first = (place + i) % SIDE * jnp.where(x_first, SIDE, 1)
-            piece = jnp.stack([acc[slot, :, first + j * step] for j in range(SIDE)], axis=1)
+            target = (place + i) % SIDE
+            piece = []
+            for j in range(SIDE):
+                x = jnp.where(x_first, target, j)
+                z = jnp.where(x_first, j, target)
+                piece.append(acc[slot, :, (y + SIDE - x) % SIDE * SIDE + z])
+            piece = jnp.stack(piece, axis=1)
             outs[i][k] = piece.reshape(2, -1, width).astype(outs[i].dtype)
 
 
 def project(spectra, modes):
     freqs, width = modes.shape[0], modes.shape[2]
-    blocks = spectra.shape[0] * spectra.shape[3]
+    blocks = SIDE * spectra[0].shape[2] * spectra[0].shape[3]
     piece = (freqs, 2, blocks // SIDE, width)
     return pl.pallas_call(
         project_kernel,
         out_shape=[jax.ShapeDtypeStruct(piece, f32 if i == 0 else bf16) for i in range(SIDE)],
-        in_specs=[VMEM, VMEM],
+        in_specs=[VMEM] * (SIDE + 1),
         out_specs=[VMEM] * SIDE,
         scratch_shapes=[pltpu.VMEM((2, 2, SIDE * SIDE, blocks // (SIDE * SIDE), width), f32)],
         compiler_params=pltpu.CompilerParams(vmem_limit_bytes=SMALL),
         name="project",
-    )(spectra, modes)
+    )(*spectra, modes)
 
 
 def fold_kernel(own, first, second, third, *refs):
@@ -197,8 +251,14 @@
     rows = lax.axis_size("row")
     groups = lax.axis_size("block")
     spectra = transform(usable_frame_tallies, retained_frequency_slots, snapshots)
-    spectra = spectra.reshape((groups, -1) + spectra.shape[1:])
-    moved = lax.all_to_all(spectra, "block", split_axis=0, concat_axis=0, tiled=True)
+
+    def along_y(value, distance):
+        pairs = [(b, (b + 2 * distance) % groups) for b in range(groups)]
+        return lax.ppermute(value, "block", pairs)
+
+    moved = {0: spectra[0]}
+    for i in FARTHEST_FIRST:
+        moved[i] = along_y(spectra[i], i)
 
     def along(value, stage, distance):
         pairs = []
@@ -213,7 +273,7 @@
         return lax.ppermute(value, ("block", "row"), pairs)
 
     mode_rows = modes.reshape(modes.shape[0], 2 * row_width, modes.shape[3])
-    pieces = project(moved, mode_rows)
+    pieces = project([moved[i] for i in range(SIDE)], mode_rows)
     pieces = fold([pieces[0]] + [along(pieces[i], 0, i) for i in FARTHEST_FIRST])
     last = [pieces[0]] + [along(pieces[i], 1, i) for i in FARTHEST_FIRST]
     freqs, double, width = last[0].shape

time: 62.2 us -> 59.4 us (0.955)
  blocking collectives: 14.7 us -> 0 us
  starting transfers between devices: 20.2 us -> 26.3 us
  waiting for transfers between devices: 20.1 us -> 26 us
    all_to_all x1 -> x0, blocking collectives: 14.7 us -> none  [shards(): lax.all_to_all(spectra, 'block', split_axis=0, concat_axis=0, tiled=True)]
    ppermute x0 -> x4, starting transfers between devices: none -> 6.06 us  [the longest x3 5.98 us: along_y(): return lax.ppermute(value, 'block', pairs)]
    ppermute x0 -> x4, waiting for transfers between devices: none -> 5.87 us  [the longest x3 4.98 us: along_y(): return lax.ppermute(value, 'block', pairs)]
    pallas_call x1 -> x2, Pallas kernels: 2.3 us -> 2.36 us  [the longest x1 1.96 us: transform(): pl.pallas_call(own_kernel, out_shape=[jax.ShapeDtypeStruct((2, SIDE, freq...]
  transfers between devices with their start and end apart: 7 -> 11, of which waited for: 5 -> 8; matrix products, arithmetic and copies ran while one was open for 0% -> 0% of each run, Pallas kernels for 1% -> 5%
where the time goes in v4:
time: 59.4 us; the launch traced here: 59.2 us
  starting transfers between devices  26.3 us (44%)
  waiting for transfers between devices  26 us (44%)
  Pallas kernels  6.21 us (10%)
  between operations  0.7 us (1%)
    ppermute x6, starting transfers between devices, along(): return lax.ppermute(value, ('block', 'row'), pairs)  13.5 us
    ppermute x6, waiting for transfers between devices, along(): return lax.ppermute(value, ('block', 'row'), pairs)  13.1 us
    all_to_all x1, waiting for transfers between devices, shards(): swapped = lax.all_to_all(energy_parts, 'row', 0, 0, tiled=True)  7.03 us
    all_to_all x1, starting transfers between devices, shards(): swapped = lax.all_to_all(energy_parts, 'row', 0, 0, tiled=True)  6.68 us
    ppermute x3, starting transfers between devices, along_y(): return lax.ppermute(value, 'block', pairs)  5.98 us
    ppermute x3, waiting for transfers between devices, along_y(): return lax.ppermute(value, 'block', pairs)  4.98 us
    pallas_call x1, Pallas kernels, transform(): pl.pallas_call(own_kernel, out_shape=[jax.ShapeDtypeStruct((2, SIDE, freq...  1.96 us
    pallas_call x1, Pallas kernels, shards(): pl.pallas_call(energy_kernel, out_shape=jax.ShapeDtypeStruct((rows, freqs...  1.34 us
  transfers between devices with their start and end apart: 11, of which 8 were waited for; matrix products, arithmetic and copies ran while one was open for 0% of the time, Pallas kernels for 5%

profile of v4, /device:TPU:0, one launch (start us, length us, event | category | flops | bytes accessed | tf_op | source)
XLA Modules:
  0.0 59.2 jit_solution(14289837993695334132)
XLA Ops:
  0.6 0.0 copy-start
  0.6 0.1 collective-permute-start
  0.7 2.0 %transform_own.1 = (bf16[2,4,8,16,128]{4,3,2,1,0:T(8,128)(2,1)S(1)}, f32[64,256]{1,0:T(8,128)S(1)}, f32[16,256]{1,0:T(8,128)S(1)}) custom-call(s32[128]{0:T(128)} %tallies.1, s32[1,64]{1,0:T(1,128)} %bitcast.5, bf16[4096,128]{1,0:T(8,128)(2,1)} %snapshots_hbm.1), custom_call_target="tpu_custom_call" | custom-call | tf_op jit(solution)/shard_map/transform_own/pallas_call | solution.py:107
  2.7 0.9 %collective-permute-done.snapshots = bf16[4096,128]{1,0:T(8,128)(2,1)S(1)} collective-permute-done((bf16[4096,128]{1,0:T(8,128)(2,1)}, bf16[4096,128]{1,0:T(8,128)(2,1)S(1)}, u32[]{:S(2)}, u32[]{:S(2)}) %collective-permute-start) | collective-permute-done | bytes 1048608 | tf_op jit(solution)/shard_map/ppermute | solution.py:106
  3.6 0.4 transform_other.1
  4.0 1.7 %collective-permute-start.1 = (bf16[8,2,2,16,128]{4,3,2,1,0:T(8,128)(2,1)S(1)}, bf16[8,2,2,16,128]{4,3,2,1,0:T(8,128)(2,1)S(1)}, u32[]{:S(2)}, u32[]{:S(2)}) collective-permute-start(bf16[8,2,2,16,128]{4,3,2,1,0:T(8,128)(2,1)S(1)} %get-tuple-element.21), channel_id=1, source_target_pairs={{0,32},{16,48},{32,64},{48,80},{64,96},{80,112},{96,0},{112,16},{1... | collective-permute-start | bytes 393224 | tf_op jit(solution)/shard_map/ppermute | solution.py:257
  5.7 2.9 %collective-permute-start.2 = (bf16[8,2,2,16,128]{4,3,2,1,0:T(8,128)(2,1)S(1)}, bf16[8,2,2,16,128]{4,3,2,1,0:T(8,128)(2,1)S(1)}, u32[]{:S(2)}, u32[]{:S(2)}) collective-permute-start(bf16[8,2,2,16,128]{4,3,2,1,0:T(8,128)(2,1)S(1)} %get-tuple-element.22), channel_id=1, source_target_pairs={{0,64},{16,80},{32,96},{48,112},{64,0},{80,16},{96,32},{112,48},{1... | collective-permute-start | bytes 393224 | tf_op jit(solution)/shard_map/ppermute | solution.py:257
  8.6 1.3 %collective-permute-start.3 = (bf16[8,2,2,16,128]{4,3,2,1,0:T(8,128)(2,1)S(1)}, bf16[8,2,2,16,128]{4,3,2,1,0:T(8,128)(2,1)S(1)}, u32[]{:S(2)}, u32[]{:S(2)}) collective-permute-start(bf16[8,2,2,16,128]{4,3,2,1,0:T(8,128)(2,1)S(1)} %get-tuple-element.23), channel_id=1, source_target_pairs={{0,96},{16,112},{32,0},{48,16},{64,32},{80,48},{96,64},{112,80},{1... | collective-permute-start | bytes 393224 | tf_op jit(solution)/shard_map/ppermute | solution.py:257
  10.0 1.0 %collective-permute-done.1.refs_1_ = bf16[8,2,2,16,128]{4,3,2,1,0:T(8,128)(2,1)S(1)} collective-permute-done((bf16[8,2,2,16,128]{4,3,2,1,0:T(8,128)(2,1)S(1)}, bf16[8,2,2,16,128]{4,3,2,1,0:T(8,128)(2,1)S(1)}, u32[]{:S(2)}, u32[]{:S(2)}) %collective-permute-start.1) | collective-permute-done | bytes 131104 | tf_op jit(solution)/shard_map/ppermute | solution.py:257
  11.0 4.0 %collective-permute-done.2.refs_2_ = bf16[8,2,2,16,128]{4,3,2,1,0:T(8,128)(2,1)S(1)} collective-permute-done((bf16[8,2,2,16,128]{4,3,2,1,0:T(8,128)(2,1)S(1)}, bf16[8,2,2,16,128]{4,3,2,1,0:T(8,128)(2,1)S(1)}, u32[]{:S(2)}, u32[]{:S(2)}) %collective-permute-start.2) | collective-permute-done | bytes 131104 | tf_op jit(solution)/shard_map/ppermute | solution.py:257
  15.0 0.0 collective-permute-done.3.refs_3_
  15.0 0.0 copy-done
  15.0 0.8 %project.1 = (f32[8,2,32,512]{3,2,1,0:T(8,128)S(1)}, bf16[8,2,32,512]{3,2,1,0:T(8,128)(2,1)S(1)}, bf16[8,2,32,512]{3,2,1,0:T(8,128)(2,1)S(1)}, bf16[8,2,32,512]{3,2,1,0:T(8,128)(2,1)S(1)}) custom-call(bf16[8,2,2,16,128]{4,3,2,1,0:T(8,128)(2,1)S(1)} %get-tuple-element.20.refs_0_, bf16[8,2,2,16,128]{4,3,2,1,0:T(8,128)(2,1)S(1)} %collective-permute-done.1.refs_1_, ...), custom_call_target="tpu_custom_call" | custom-call | tf_op jit(solution)/shard_map/project/pallas_call | solution.py:183
  15.8 3.1 %collective-permute-start.4 = (bf16[8,2,32,512]{3,2,1,0:T(8,128)(2,1)S(1)}, bf16[8,2,32,512]{3,2,1,0:T(8,128)(2,1)S(1)}, u32[]{:S(2)}, u32[]{:S(2)}) collective-permute-start(bf16[8,2,32,512]{3,2,1,0:T(8,128)(2,1)S(1)} %get-tuple-element.25), channel_id=1, source_target_pairs={{0,8},{1,9},{2,10},{3,11},{4,12},{5,13},{6,14},{7,15},{8,0},{9,1},... | collective-permute-start | bytes 1572872 | tf_op jit(solution)/shard_map/ppermute | solution.py:273
  18.9 0.6 %collective-permute-start.5 = (bf16[8,2,32,512]{3,2,1,0:T(8,128)(2,1)S(1)}, bf16[8,2,32,512]{3,2,1,0:T(8,128)(2,1)S(1)}, u32[]{:S(2)}, u32[]{:S(2)}) collective-permute-start(bf16[8,2,32,512]{3,2,1,0:T(8,128)(2,1)S(1)} %get-tuple-element.26), channel_id=1, source_target_pairs={{0,4},{1,5},{2,6},{3,7},{4,8},{5,9},{6,10},{7,11},{8,12},{9,13},{1... | collective-permute-start | bytes 1572872 | tf_op jit(solution)/shard_map/ppermute | solution.py:273
  19.4 2.6 %collective-permute-start.6 = (bf16[8,2,32,512]{3,2,1,0:T(8,128)(2,1)S(1)}, bf16[8,2,32,512]{3,2,1,0:T(8,128)(2,1)S(1)}, u32[]{:S(2)}, u32[]{:S(2)}) collective-permute-start(bf16[8,2,32,512]{3,2,1,0:T(8,128)(2,1)S(1)} %get-tuple-element.27), channel_id=1, source_target_pairs={{0,12},{1,13},{2,14},{3,15},{4,0},{5,1},{6,2},{7,3},{8,4},{9,5},{1... | collective-permute-start | bytes 1572872 | tf_op jit(solution)/shard_map/ppermute | solution.py:273
  22.1 4.5 %collective-permute-done.4.first = bf16[8,2,32,512]{3,2,1,0:T(8,128)(2,1)S(1)} collective-permute-done((bf16[8,2,32,512]{3,2,1,0:T(8,128)(2,1)S(1)}, bf16[8,2,32,512]{3,2,1,0:T(8,128)(2,1)S(1)}, u32[]{:S(2)}, u32[]{:S(2)}) %collective-permute-start.4) | collective-permute-done | bytes 524320 | tf_op jit(solution)/shard_map/ppermute | solution.py:273
  26.6 5.5 %collective-permute-done.5.second = bf16[8,2,32,512]{3,2,1,0:T(8,128)(2,1)S(1)} collective-permute-done((bf16[8,2,32,512]{3,2,1,0:T(8,128)(2,1)S(1)}, bf16[8,2,32,512]{3,2,1,0:T(8,128)(2,1)S(1)}, u32[]{:S(2)}, u32[]{:S(2)}) %collective-permute-start.5) | collective-permute-done | bytes 524320 | tf_op jit(solution)/shard_map/ppermute | solution.py:273
  32.1 0.1 collective-permute-done.6.third
  32.3 0.3 fold.1
  32.6 4.0 %collective-permute-start.7 = (bf16[8,16,512]{2,1,0:T(8,128)(2,1)S(1)}, bf16[8,16,512]{2,1,0:T(8,128)(2,1)S(1)}, u32[]{:S(2)}, u32[]{:S(2)}) collective-permute-start(bf16[8,16,512]{2,1,0:T(8,128)(2,1)S(1)} %get-tuple-element.29), channel_id=1, source_target_pairs={{0,2},{1,3},{2,0},{3,1},{4,6},{5,7},{6,4},{7,5},{8,10},{9,11},{10,... | collective-permute-start | bytes 393224 | tf_op jit(solution)/shard_map/ppermute | solution.py:273
  36.5 1.0 %collective-permute-start.8 = (bf16[8,16,512]{2,1,0:T(8,128)(2,1)S(1)}, bf16[8,16,512]{2,1,0:T(8,128)(2,1)S(1)}, u32[]{:S(2)}, u32[]{:S(2)}) collective-permute-start(bf16[8,16,512]{2,1,0:T(8,128)(2,1)S(1)} %get-tuple-element.30), channel_id=1, source_target_pairs={{0,1},{1,2},{2,3},{3,0},{4,5},{5,6},{6,7},{7,4},{8,9},{9,10},{10,1... | collective-permute-start | bytes 393224 | tf_op jit(solution)/shard_map/ppermute | solution.py:273
  37.5 2.2 %collective-permute-start.9 = (bf16[8,16,512]{2,1,0:T(8,128)(2,1)S(1)}, bf16[8,16,512]{2,1,0:T(8,128)(2,1)S(1)}, u32[]{:S(2)}, u32[]{:S(2)}) collective-permute-start(bf16[8,16,512]{2,1,0:T(8,128)(2,1)S(1)} %get-tuple-element.31), channel_id=1, source_target_pairs={{0,3},{1,0},{2,1},{3,2},{4,7},{5,4},{6,5},{7,6},{8,11},{9,8},{10,9... | collective-permute-start | bytes 393224 | tf_op jit(solution)/shard_map/ppermute | solution.py:273
  39.8 0.0 collective-permute-done.7.first
  39.8 2.9 %collective-permute-done.8.second = bf16[8,16,512]{2,1,0:T(8,128)(2,1)S(1)} collective-permute-done((bf16[8,16,512]{2,1,0:T(8,128)(2,1)S(1)}, bf16[8,16,512]{2,1,0:T(8,128)(2,1)S(1)}, u32[]{:S(2)}, u32[]{:S(2)}) %collective-permute-start.8) | collective-permute-done | bytes 131104 | tf_op jit(solution)/shard_map/ppermute | solution.py:273
  42.7 0.0 collective-permute-done.9.third
  42.7 0.0 copy-done.1
  42.7 1.3 %energy.1 = bf16[16,8,512]{2,1,0:T(8,128)(2,1)} custom-call(s32[128]{0:T(128)S(1)} %copy-done.1, s32[1,128]{1,0:T(1,128)S(1)} %bitcast.4, f32[8,16,512]{2,1,0:T(8,128)S(1)} %get-tuple-element.28.own, bf16[8,16,512]{2,1,0:T(8,128)(2,1)S(1)} %collective-permute-done.7.first, bf16[8,16,512]{2,1,0:T(8,128)(2,1)S(1)} %collective-permute-done.8.second, ...), custom_call_target="tpu_custom_call" | custom-call | tf_op jit(solution)/shard_map/energy/pallas_call | solution.py:280
  44.0 6.7 %all-to-all-start = ((bf16[16,8,512]{2,1,0:T(8,128)(2,1)}), bf16[16,8,512]{2,1,0:T(8,128)(2,1)S(1)}, u32[]{:S(2)}, u32[]{:S(2)}) async-start(bf16[16,8,512]{2,1,0:T(8,128)(2,1)} %energy.1), calls=%async_computation | async-start | bytes 262144 | tf_op jit(solution)/shard_map/all_to_all | solution.py:289
  50.7 0.8 %coefficients.1 = f32[8,2,8,512]{3,2,1,0:T(8,128)} custom-call(f32[8,16,512]{2,1,0:T(8,128)S(1)} %get-tuple-element.28.own, bf16[8,16,512]{2,1,0:T(8,128)(2,1)S(1)} %collective-permute-done.7.first, bf16[8,16,512]{2,1,0:T(8,128)(2,1)S(1)} %collective-permute-done.8.second, bf16[8,16,512]{2,1,0:T(8,128)(2,1)S(1)} %collective-permute-done.9.third), custom_call_target="tpu_custom_call" | custom-call | tf_op jit(solution)/shard_map/coefficients/pallas_call | solution.py:290
  51.5 7.0 %all-to-all-done.parts = bf16[16,8,512]{2,1,0:T(8,128)(2,1)S(1)} async-done(((bf16[16,8,512]{2,1,0:T(8,128)(2,1)}), bf16[16,8,512]{2,1,0:T(8,128)(2,1)S(1)}, u32[]{:S(2)}, u32[]{:S(2)}) %all-to-all-start) | async-done | bytes 131104 | tf_op jit(solution)/shard_map/all_to_all | solution.py:289
  58.6 0.6 %total.1 = f32[8,512]{1,0:T(8,128)} custom-call(bf16[16,8,512]{2,1,0:T(8,128)(2,1)S(1)} %all-to-all-done.parts), custom_call_target="tpu_custom_call" | custom-call | tf_op jit(solution)/shard_map/total/pallas_call | solution.py:298
  (1 shorter events, 0.0 us)
Async XLA Ops:
  0.6 14.3 %copy-start = (bf16[8,2,128,512]{3,2,1,0:T(8,128)(2,1)S(1)}, bf16[8,2,128,512]{3,2,1,0:T(8,128)(2,1)}, u32[]{:S(2)}) copy-start(bf16[8,2,128,512]{3,2,1,0:T(8,128)(2,1)} %param.7) | copy-start | bytes 6291460
  0.6 3.0 %collective-permute-start = (bf16[4096,128]{1,0:T(8,128)(2,1)}, bf16[4096,128]{1,0:T(8,128)(2,1)S(1)}, u32[]{:S(2)}, u32[]{:S(2)}) collective-permute-start(bf16[4096,128]{1,0:T(8,128)(2,1)} %snapshots_hbm.1), channel_id=1, source_target_pairs={{0,16},{16,0},{32,48},{48,32},{64,80},{80,64},{96,112},{112,96},{1... | collective-permute-start | bytes 3145736 | tf_op jit(solution)/shard_map/ppermute | solution.py:106
  4.0 7.0 %collective-permute-start.1 = (bf16[8,2,2,16,128]{4,3,2,1,0:T(8,128)(2,1)S(1)}, bf16[8,2,2,16,128]{4,3,2,1,0:T(8,128)(2,1)S(1)}, u32[]{:S(2)}, u32[]{:S(2)}) collective-permute-start(bf16[8,2,2,16,128]{4,3,2,1,0:T(8,128)(2,1)S(1)} %get-tuple-element.21), channel_id=1, source_target_pairs={{0,32},{16,48},{32,64},{48,80},{64,96},{80,112},{96,0},{112,16},{1... | collective-permute-start | bytes 393224 | tf_op jit(solution)/shard_map/ppermute | solution.py:257
  5.7 9.2 %collective-permute-start.2 = (bf16[8,2,2,16,128]{4,3,2,1,0:T(8,128)(2,1)S(1)}, bf16[8,2,2,16,128]{4,3,2,1,0:T(8,128)(2,1)S(1)}, u32[]{:S(2)}, u32[]{:S(2)}) collective-permute-start(bf16[8,2,2,16,128]{4,3,2,1,0:T(8,128)(2,1)S(1)} %get-tuple-element.22), channel_id=1, source_target_pairs={{0,64},{16,80},{32,96},{48,112},{64,0},{80,16},{96,32},{112,48},{1... | collective-permute-start | bytes 393224 | tf_op jit(solution)/shard_map/ppermute | solution.py:257
  8.6 6.3 %collective-permute-start.3 = (bf16[8,2,2,16,128]{4,3,2,1,0:T(8,128)(2,1)S(1)}, bf16[8,2,2,16,128]{4,3,2,1,0:T(8,128)(2,1)S(1)}, u32[]{:S(2)}, u32[]{:S(2)}) collective-permute-start(bf16[8,2,2,16,128]{4,3,2,1,0:T(8,128)(2,1)S(1)} %get-tuple-element.23), channel_id=1, source_target_pairs={{0,96},{16,112},{32,0},{48,16},{64,32},{80,48},{96,64},{112,80},{1... | collective-permute-start | bytes 393224 | tf_op jit(solution)/shard_map/ppermute | solution.py:257
  15.0 27.7 %copy-start.1 = (s32[128]{0:T(128)S(1)}, s32[128]{0:T(128)}, u32[]{:S(2)}) copy-start(s32[128]{0:T(128)} %tallies.1) | copy-start | bytes 1540
  15.8 10.9 %collective-permute-start.4 = (bf16[8,2,32,512]{3,2,1,0:T(8,128)(2,1)S(1)}, bf16[8,2,32,512]{3,2,1,0:T(8,128)(2,1)S(1)}, u32[]{:S(2)}, u32[]{:S(2)}) collective-permute-start(bf16[8,2,32,512]{3,2,1,0:T(8,128)(2,1)S(1)} %get-tuple-element.25), channel_id=1, source_target_pairs={{0,8},{1,9},{2,10},{3,11},{4,12},{5,13},{6,14},{7,15},{8,0},{9,1},... | collective-permute-start | bytes 1572872 | tf_op jit(solution)/shard_map/ppermute | solution.py:273
  18.9 13.3 %collective-permute-start.5 = (bf16[8,2,32,512]{3,2,1,0:T(8,128)(2,1)S(1)}, bf16[8,2,32,512]{3,2,1,0:T(8,128)(2,1)S(1)}, u32[]{:S(2)}, u32[]{:S(2)}) collective-permute-start(bf16[8,2,32,512]{3,2,1,0:T(8,128)(2,1)S(1)} %get-tuple-element.26), channel_id=1, source_target_pairs={{0,4},{1,5},{2,6},{3,7},{4,8},{5,9},{6,10},{7,11},{8,12},{9,13},{1... | collective-permute-start | bytes 1572872 | tf_op jit(solution)/shard_map/ppermute | solution.py:273
  19.4 12.8 %collective-permute-start.6 = (bf16[8,2,32,512]{3,2,1,0:T(8,128)(2,1)S(1)}, bf16[8,2,32,512]{3,2,1,0:T(8,128)(2,1)S(1)}, u32[]{:S(2)}, u32[]{:S(2)}) collective-permute-start(bf16[8,2,32,512]{3,2,1,0:T(8,128)(2,1)S(1)} %get-tuple-element.27), channel_id=1, source_target_pairs={{0,12},{1,13},{2,14},{3,15},{4,0},{5,1},{6,2},{7,3},{8,4},{9,5},{1... | collective-permute-start | bytes 1572872 | tf_op jit(solution)/shard_map/ppermute | solution.py:273
  32.6 7.2 %collective-permute-start.7 = (bf16[8,16,512]{2,1,0:T(8,128)(2,1)S(1)}, bf16[8,16,512]{2,1,0:T(8,128)(2,1)S(1)}, u32[]{:S(2)}, u32[]{:S(2)}) collective-permute-start(bf16[8,16,512]{2,1,0:T(8,128)(2,1)S(1)} %get-tuple-element.29), channel_id=1, source_target_pairs={{0,2},{1,3},{2,0},{3,1},{4,6},{5,7},{6,4},{7,5},{8,10},{9,11},{10,... | collective-permute-start | bytes 393224 | tf_op jit(solution)/shard_map/ppermute | solution.py:273
  36.5 6.2 %collective-permute-start.8 = (bf16[8,16,512]{2,1,0:T(8,128)(2,1)S(1)}, bf16[8,16,512]{2,1,0:T(8,128)(2,1)S(1)}, u32[]{:S(2)}, u32[]{:S(2)}) collective-permute-start(bf16[8,16,512]{2,1,0:T(8,128)(2,1)S(1)} %get-tuple-element.30), channel_id=1, source_target_pairs={{0,1},{1,2},{2,3},{3,0},{4,5},{5,6},{6,7},{7,4},{8,9},{9,10},{10,1... | collective-permute-start | bytes 393224 | tf_op jit(solution)/shard_map/ppermute | solution.py:273
  37.5 5.2 %collective-permute-start.9 = (bf16[8,16,512]{2,1,0:T(8,128)(2,1)S(1)}, bf16[8,16,512]{2,1,0:T(8,128)(2,1)S(1)}, u32[]{:S(2)}, u32[]{:S(2)}) collective-permute-start(bf16[8,16,512]{2,1,0:T(8,128)(2,1)S(1)} %get-tuple-element.31), channel_id=1, source_target_pairs={{0,3},{1,0},{2,1},{3,2},{4,7},{5,4},{6,5},{7,6},{8,11},{9,8},{10,9... | collective-permute-start | bytes 393224 | tf_op jit(solution)/shard_map/ppermute | solution.py:273
  44.0 14.5 %all-to-all-start = ((bf16[16,8,512]{2,1,0:T(8,128)(2,1)}), bf16[16,8,512]{2,1,0:T(8,128)(2,1)S(1)}, u32[]{:S(2)}, u32[]{:S(2)}) async-start(bf16[16,8,512]{2,1,0:T(8,128)(2,1)} %energy.1), calls=%async_computation | async-start | bytes 262144 | tf_op jit(solution)/shard_map/all_to_all | solution.py:289

commit v5 on v4

--- a/solution.py
+++ b/solution.py
@@ -165,38 +165,56 @@
         )
         slot = k % 2
         acc[slot] = jnp.dot(left, modes[k], preferred_element_type=f32).reshape(acc.shape[1:])
-        for i in range(SIDE):
-            target = (place + i) % SIDE
+        half = k // (freqs // 2)
+        for i, flip in enumerate((0, 3 - 2 * half, 1 + 2 * half, 2)):
+            target = place ^ flip
             piece = []
             for j in range(SIDE):
                 x = jnp.where(x_first, target, j)
                 z = jnp.where(x_first, j, target)
                 piece.append(acc[slot, :, (y + SIDE - x) % SIDE * SIDE + z])
             piece = jnp.stack(piece, axis=1)
-            outs[i][k] = piece.reshape(2, -1, width).astype(outs[i].dtype)
+            out = outs[half * SIDE + i]
+            out[k % (freqs // 2)] = piece.reshape(2, -1, width).astype(out.dtype)
 
 
 def project(spectra, modes):
     freqs, width = modes.shape[0], modes.shape[2]
     blocks = SIDE * spectra[0].shape[2] * spectra[0].shape[3]
-    piece = (freqs, 2, blocks // SIDE, width)
+    piece = (freqs // 2, 2, blocks // SIDE, width)
     return pl.pallas_call(
         project_kernel,
-        out_shape=[jax.ShapeDtypeStruct(piece, f32 if i == 0 else bf16) for i in range(SIDE)],
+        out_shape=[jax.ShapeDtypeStruct(piece, t) for t in (f32, f32, bf16, bf16) * 2],
         in_specs=[VMEM] * (SIDE + 1),
-        out_specs=[VMEM] * SIDE,
+        out_specs=[VMEM] * (2 * SIDE),
         scratch_shapes=[pltpu.VMEM((2, 2, SIDE * SIDE, blocks // (SIDE * SIDE), width), f32)],
         compiler_params=pltpu.CompilerParams(vmem_limit_bytes=SMALL),
         name="project",
     )(*spectra, modes)
 
 
-def fold_kernel(own, first, second, third, *refs):
-    outs, acc = refs[:-1], refs[-1]
+def relay_kernel(held, came, out):
+    out[...] = (held[...] + came[...].astype(f32)).astype(bf16)
+
+
+def relay(held, came):
+    return pl.pallas_call(
+        relay_kernel,
+        out_shape=jax.ShapeDtypeStruct(came.shape, bf16),
+        in_specs=[VMEM] * 2,
+        out_specs=VMEM,
+        compiler_params=pltpu.CompilerParams(vmem_limit_bytes=SMALL),
+        name="relay",
+    )(held, came)
+
+
+def fold_kernel(*refs):
+    parts, outs, acc = refs[:6], refs[6:-1], refs[-1]
     _, _, place = places()
-    width = own.shape[3]
-    for k in range(own.shape[0]):
-        total = own[k] + first[k].astype(f32) + second[k].astype(f32) + third[k].astype(f32)
+    half, width = parts[0].shape[0], parts[0].shape[3]
+    for k in range(2 * half):
+        own, direct, relayed = parts[3 * (k // half) : 3 * (k // half) + 3]
+        total = own[k % half] + direct[k % half].astype(f32) + relayed[k % half].astype(f32)
         acc[k % 2] = total.reshape(acc.shape[1:])
         for i in range(SIDE):
             piece = acc[k % 2, :, (place + i) % SIDE].reshape(-1, width)
@@ -204,12 +222,12 @@
 
 
 def fold(parts):
-    freqs, _, blocks, width = parts[0].shape
-    piece = (freqs, 2 * blocks // SIDE, width)
+    half, _, blocks, width = parts[0].shape
+    piece = (2 * half, 2 * blocks // SIDE, width)
     return pl.pallas_call(
         fold_kernel,
         out_shape=[jax.ShapeDtypeStruct(piece, f32 if i == 0 else bf16) for i in range(SIDE)],
-        in_specs=[VMEM] * SIDE,
+        in_specs=[VMEM] * 6,
         out_specs=[VMEM] * SIDE,
         scratch_shapes=[pltpu.VMEM((2, 2, SIDE, blocks // SIDE, width), f32)],
         compiler_params=pltpu.CompilerParams(vmem_limit_bytes=SMALL),
@@ -260,22 +278,34 @@
     for i in FARTHEST_FIRST:
         moved[i] = along_y(spectra[i], i)
 
-    def along(value, stage, distance):
+    def along(value, stage, move):
         pairs = []
         for block in range(groups):
             for x in range(SIDE):
                 for z in range(SIDE):
                     if (block % 2 == 0) == (stage == 0):
-                        target = (x + distance) % SIDE * SIDE + z
+                        target = move(x) * SIDE + z
                     else:
-                        target = x * SIDE + (z + distance) % SIDE
+                        target = x * SIDE + move(z)
                     pairs.append((block * rows + x * SIDE + z, block * rows + target))
         return lax.ppermute(value, ("block", "row"), pairs)
 
+    def flipped(value, bits):
+        return along(value, 0, lambda place: place ^ bits)
+
+    def onward(value, distance):
+        return along(value, 1, lambda place: (place + distance) % SIDE)
+
     mode_rows = modes.reshape(modes.shape[0], 2 * row_width, modes.shape[3])
     pieces = project([moved[i] for i in range(SIDE)], mode_rows)
-    pieces = fold([pieces[0]] + [along(pieces[i], 0, i) for i in FARTHEST_FIRST])
-    last = [pieces[0]] + [along(pieces[i], 1, i) for i in FARTHEST_FIRST]
+    own_a, held_a, direct_a, far_a, own_b, held_b, direct_b, far_b = pieces
+    far_a, far_b = flipped(far_a, 1), flipped(far_b, 3)
+    direct_a, direct_b = flipped(direct_a, 1), flipped(direct_b, 3)
+    relayed_a = flipped(relay(held_a, far_a), 3)
+    relayed_b = flipped(relay(held_b, far_b), 1)
+    pieces = fold([own_a, direct_a, relayed_a, own_b, direct_b, relayed_b])
+    came = {i: onward(pieces[i], i) for i in (1, 3, 2)}
+    last = [pieces[0]] + [came[i] for i in range(1, SIDE)]
     freqs, double, width = last[0].shape
     energy_parts = pl.pallas_call(
         energy_kernel,

time: 59.4 us -> 57.5 us (0.968)
  waiting for transfers between devices: 26 us -> 24.6 us
  starting transfers between devices: 26.3 us -> 25.7 us
    all_to_all x1, starting transfers between devices: 6.68 us -> 5.07 us  [shards(): swapped = lax.all_to_all(energy_parts, 'row', 0, 0, tiled=True)]
    ppermute x6 -> x9, waiting for transfers between devices: 13.1 us -> 11.7 us  [along(): return lax.ppermute(value, ('block', 'row'), pairs)]
    ppermute x6 -> x9, starting transfers between devices: 13.5 us -> 14.6 us  [along(): return lax.ppermute(value, ('block', 'row'), pairs)]
  transfers between devices with their start and end apart: 11 -> 14, of which waited for: 8 -> 12; matrix products, arithmetic and copies ran while one was open for 0% -> 0% of each run, Pallas kernels for 5% -> 5%
where the time goes in v5:
time: 57.5 us; the launch traced here: 57.3 us
  starting transfers between devices  25.7 us (45%)
  waiting for transfers between devices  24.6 us (43%)
  Pallas kernels  6.28 us (11%)
  between operations  0.71 us (1%)
    ppermute x9, starting transfers between devices, along(): return lax.ppermute(value, ('block', 'row'), pairs)  14.6 us
    ppermute x9, waiting for transfers between devices, along(): return lax.ppermute(value, ('block', 'row'), pairs)  11.7 us
    all_to_all x1, waiting for transfers between devices, shards(): swapped = lax.all_to_all(energy_parts, 'row', 0, 0, tiled=True)  7.03 us
    ppermute x3, starting transfers between devices, along_y(): return lax.ppermute(value, 'block', pairs)  5.98 us
    all_to_all x1, starting transfers between devices, shards(): swapped = lax.all_to_all(energy_parts, 'row', 0, 0, tiled=True)  5.07 us
    ppermute x3, waiting for transfers between devices, along_y(): return lax.ppermute(value, 'block', pairs)  4.98 us
    pallas_call x1, Pallas kernels, transform(): pl.pallas_call(own_kernel, out_shape=[jax.ShapeDtypeStruct((2, SIDE, freq...  1.96 us
    pallas_call x1, Pallas kernels, shards(): pl.pallas_call(energy_kernel, out_shape=jax.ShapeDtypeStruct((rows, freqs...  1.34 us
  transfers between devices with their start and end apart: 14, of which 12 were waited for; matrix products, arithmetic and copies ran while one was open for 0% of the time, Pallas kernels for 5%

profile of v5, /device:TPU:0, one launch (start us, length us, event | category | flops | bytes accessed | tf_op | source)
XLA Modules:
  0.0 57.3 jit_solution(473808715808029950)
XLA Ops:
  0.7 2.0 %transform_own.1 = (bf16[2,4,8,16,128]{4,3,2,1,0:T(8,128)(2,1)S(1)}, f32[64,256]{1,0:T(8,128)S(1)}, f32[16,256]{1,0:T(8,128)S(1)}) custom-call(s32[128]{0:T(128)} %tallies.1, s32[1,64]{1,0:T(1,128)} %bitcast.5, bf16[4096,128]{1,0:T(8,128)(2,1)} %snapshots_hbm.1), custom_call_target="tpu_custom_call" | custom-call | tf_op jit(solution)/shard_map/transform_own/pallas_call | solution.py:107
  2.7 0.9 %collective-permute-done.snapshots = bf16[4096,128]{1,0:T(8,128)(2,1)S(1)} collective-permute-done((bf16[4096,128]{1,0:T(8,128)(2,1)}, bf16[4096,128]{1,0:T(8,128)(2,1)S(1)}, u32[]{:S(2)}, u32[]{:S(2)}) %collective-permute-start) | collective-permute-done | bytes 1048608 | tf_op jit(solution)/shard_map/ppermute | solution.py:106
  3.6 0.4 transform_other.1
  4.0 1.7 %collective-permute-start.1 = (bf16[8,2,2,16,128]{4,3,2,1,0:T(8,128)(2,1)S(1)}, bf16[8,2,2,16,128]{4,3,2,1,0:T(8,128)(2,1)S(1)}, u32[]{:S(2)}, u32[]{:S(2)}) collective-permute-start(bf16[8,2,2,16,128]{4,3,2,1,0:T(8,128)(2,1)S(1)} %get-tuple-element.25), channel_id=1, source_target_pairs={{0,32},{16,48},{32,64},{48,80},{64,96},{80,112},{96,0},{112,16},{1... | collective-permute-start | bytes 393224 | tf_op jit(solution)/shard_map/ppermute | solution.py:275
  5.7 2.9 %collective-permute-start.2 = (bf16[8,2,2,16,128]{4,3,2,1,0:T(8,128)(2,1)S(1)}, bf16[8,2,2,16,128]{4,3,2,1,0:T(8,128)(2,1)S(1)}, u32[]{:S(2)}, u32[]{:S(2)}) collective-permute-start(bf16[8,2,2,16,128]{4,3,2,1,0:T(8,128)(2,1)S(1)} %get-tuple-element.26), channel_id=1, source_target_pairs={{0,64},{16,80},{32,96},{48,112},{64,0},{80,16},{96,32},{112,48},{1... | collective-permute-start | bytes 393224 | tf_op jit(solution)/shard_map/ppermute | solution.py:275
  8.6 1.3 %collective-permute-start.3 = (bf16[8,2,2,16,128]{4,3,2,1,0:T(8,128)(2,1)S(1)}, bf16[8,2,2,16,128]{4,3,2,1,0:T(8,128)(2,1)S(1)}, u32[]{:S(2)}, u32[]{:S(2)}) collective-permute-start(bf16[8,2,2,16,128]{4,3,2,1,0:T(8,128)(2,1)S(1)} %get-tuple-element.27), channel_id=1, source_target_pairs={{0,96},{16,112},{32,0},{48,16},{64,32},{80,48},{96,64},{112,80},{1... | collective-permute-start | bytes 393224 | tf_op jit(solution)/shard_map/ppermute | solution.py:275
  10.0 1.0 %collective-permute-done.1.refs_1_ = bf16[8,2,2,16,128]{4,3,2,1,0:T(8,128)(2,1)S(1)} collective-permute-done((bf16[8,2,2,16,128]{4,3,2,1,0:T(8,128)(2,1)S(1)}, bf16[8,2,2,16,128]{4,3,2,1,0:T(8,128)(2,1)S(1)}, u32[]{:S(2)}, u32[]{:S(2)}) %collective-permute-start.1) | collective-permute-done | bytes 131104 | tf_op jit(solution)/shard_map/ppermute | solution.py:275
  11.0 4.0 %collective-permute-done.2.refs_2_ = bf16[8,2,2,16,128]{4,3,2,1,0:T(8,128)(2,1)S(1)} collective-permute-done((bf16[8,2,2,16,128]{4,3,2,1,0:T(8,128)(2,1)S(1)}, bf16[8,2,2,16,128]{4,3,2,1,0:T(8,128)(2,1)S(1)}, u32[]{:S(2)}, u32[]{:S(2)}) %collective-permute-start.2) | collective-permute-done | bytes 131104 | tf_op jit(solution)/shard_map/ppermute | solution.py:275
  15.0 0.8 %project.1 = (f32[4,2,32,512]{3,2,1,0:T(8,128)S(1)}, f32[4,2,32,512]{3,2,1,0:T(8,128)S(1)}, bf16[4,2,32,512]{3,2,1,0:T(8,128)(2,1)S(1)}, bf16[4,2,32,512]{3,2,1,...) custom-call(bf16[8,2,2,16,128]{4,3,2,1,0:T(8,128)(2,1)S(1)} %get-tup, ...), custom_call_target="tpu_custom_call" | custom-call | tf_op jit(solution)/shard_map/project/pallas_call | solution.py:185
  15.8 1.6 %collective-permute-start.5 = (bf16[4,2,32,512]{3,2,1,0:T(8,128)(2,1)S(1)}, bf16[4,2,32,512]{3,2,1,0:T(8,128)(2,1)S(1)}, u32[]{:S(2)}, u32[]{:S(2)}) collective-permute-start(bf16[4,2,32,512]{3,2,1,0:T(8,128)(2,1)S(1)} %get-tuple-element.31), channel_id=1, source_target_pairs={{0,4},{1,5},{2,6},{3,7},{4,0},{5,1},{6,2},{7,3},{8,12},{9,13},{10,... | collective-permute-start | bytes 786440 | tf_op jit(solution)/shard_map/ppermute | solution.py:291
  17.4 2.1 %collective-permute-start.8 = (bf16[4,2,32,512]{3,2,1,0:T(8,128)(2,1)S(1)}, bf16[4,2,32,512]{3,2,1,0:T(8,128)(2,1)S(1)}, u32[]{:S(2)}, u32[]{:S(2)}) collective-permute-start(bf16[4,2,32,512]{3,2,1,0:T(8,128)(2,1)S(1)} %get-tuple-element.35), channel_id=1, source_target_pairs={{0,12},{1,13},{2,14},{3,15},{4,8},{5,9},{6,10},{7,11},{8,4},{9,5},... | collective-permute-start | bytes 786440 | tf_op jit(solution)/shard_map/ppermute | solution.py:291
  19.5 0.6 %collective-permute-start.4 = (bf16[4,2,32,512]{3,2,1,0:T(8,128)(2,1)S(1)}, bf16[4,2,32,512]{3,2,1,0:T(8,128)(2,1)S(1)}, u32[]{:S(2)}, u32[]{:S(2)}) collective-permute-start(bf16[4,2,32,512]{3,2,1,0:T(8,128)(2,1)S(1)} %get-tuple-element.29), channel_id=1, source_target_pairs={{0,4},{1,5},{2,6},{3,7},{4,0},{5,1},{6,2},{7,3},{8,12},{9,13},{10,... | collective-permute-start | bytes 786440 | tf_op jit(solution)/shard_map/ppermute | solution.py:291
  20.1 0.6 %collective-permute-start.7 = (bf16[4,2,32,512]{3,2,1,0:T(8,128)(2,1)S(1)}, bf16[4,2,32,512]{3,2,1,0:T(8,128)(2,1)S(1)}, u32[]{:S(2)}, u32[]{:S(2)}) collective-permute-start(bf16[4,2,32,512]{3,2,1,0:T(8,128)(2,1)S(1)} %get-tuple-element.33), channel_id=1, source_target_pairs={{0,12},{1,13},{2,14},{3,15},{4,8},{5,9},{6,10},{7,11},{8,4},{9,5},... | collective-permute-start | bytes 786440 | tf_op jit(solution)/shard_map/ppermute | solution.py:291
  20.7 1.6 %collective-permute-done.5.came = bf16[4,2,32,512]{3,2,1,0:T(8,128)(2,1)S(1)} collective-permute-done((bf16[4,2,32,512]{3,2,1,0:T(8,128)(2,1)S(1)}, bf16[4,2,32,512]{3,2,1,0:T(8,128)(2,1)S(1)}, u32[]{:S(2)}, u32[]{:S(2)}) %collective-permute-start.5) | collective-permute-done | bytes 262176 | tf_op jit(solution)/shard_map/ppermute | solution.py:291
  22.3 2.8 %collective-permute-start.6 = (bf16[4,2,32,512]{3,2,1,0:T(8,128)(2,1)S(1)}, bf16[4,2,32,512]{3,2,1,0:T(8,128)(2,1)S(1)}, u32[]{:S(2)}, u32[]{:S(2)}) collective-permute-start(bf16[4,2,32,512]{3,2,1,0:T(8,128)(2,1)S(1)} %relay.2), channel_id=1, source_target_pairs={{0,12},{1,13},{2,14},{3,15},{4,8},{5,9},{6,10},{7,11},{8,4},{9,5},... | collective-permute-start | bytes 786440 | tf_op jit(solution)/shard_map/ppermute | solution.py:291
  25.2 0.3 collective-permute-start.9
  25.5 0.3 collective-permute-done.4.refs_1_
  25.8 1.9 %collective-permute-done.7.refs_4_ = bf16[4,2,32,512]{3,2,1,0:T(8,128)(2,1)S(1)} collective-permute-done((bf16[4,2,32,512]{3,2,1,0:T(8,128)(2,1)S(1)}, bf16[4,2,32,512]{3,2,1,0:T(8,128)(2,1)S(1)}, u32[]{:S(2)}, u32[]{:S(2)}) %collective-permute-start.7) | collective-permute-done | bytes 262176 | tf_op jit(solution)/shard_map/ppermute | solution.py:291
  27.8 2.8 %collective-permute-done.6.refs_2_ = bf16[4,2,32,512]{3,2,1,0:T(8,128)(2,1)S(1)} collective-permute-done((bf16[4,2,32,512]{3,2,1,0:T(8,128)(2,1)S(1)}, bf16[4,2,32,512]{3,2,1,0:T(8,128)(2,1)S(1)}, u32[]{:S(2)}, u32[]{:S(2)}) %collective-permute-start.6) | collective-permute-done | bytes 262176 | tf_op jit(solution)/shard_map/ppermute | solution.py:291
  30.6 1.1 %collective-permute-done.9.refs_5_ = bf16[4,2,32,512]{3,2,1,0:T(8,128)(2,1)S(1)} collective-permute-done((bf16[4,2,32,512]{3,2,1,0:T(8,128)(2,1)S(1)}, bf16[4,2,32,512]{3,2,1,0:T(8,128)(2,1)S(1)}, u32[]{:S(2)}, u32[]{:S(2)}) %collective-permute-start.9) | collective-permute-done | bytes 262176 | tf_op jit(solution)/shard_map/ppermute | solution.py:291
  31.7 0.2 fold.1
  31.9 2.0 %collective-permute-start.10 = (bf16[8,16,512]{2,1,0:T(8,128)(2,1)S(1)}, bf16[8,16,512]{2,1,0:T(8,128)(2,1)S(1)}, u32[]{:S(2)}, u32[]{:S(2)}) collective-permute-start(bf16[8,16,512]{2,1,0:T(8,128)(2,1)S(1)} %get-tuple-element.37), channel_id=1, source_target_pairs={{0,1},{1,2},{2,3},{3,0},{4,5},{5,6},{6,7},{7,4},{8,9},{9,10},{10,1... | collective-permute-start | bytes 393224 | tf_op jit(solution)/shard_map/ppermute | solution.py:291
  33.9 3.6 %collective-permute-start.11 = (bf16[8,16,512]{2,1,0:T(8,128)(2,1)S(1)}, bf16[8,16,512]{2,1,0:T(8,128)(2,1)S(1)}, u32[]{:S(2)}, u32[]{:S(2)}) collective-permute-start(bf16[8,16,512]{2,1,0:T(8,128)(2,1)S(1)} %get-tuple-element.38), channel_id=1, source_target_pairs={{0,2},{1,3},{2,0},{3,1},{4,6},{5,7},{6,4},{7,5},{8,10},{9,11},{10,... | collective-permute-start | bytes 393224 | tf_op jit(solution)/shard_map/ppermute | solution.py:291
  37.4 1.0 %collective-permute-start.12 = (bf16[8,16,512]{2,1,0:T(8,128)(2,1)S(1)}, bf16[8,16,512]{2,1,0:T(8,128)(2,1)S(1)}, u32[]{:S(2)}, u32[]{:S(2)}) collective-permute-start(bf16[8,16,512]{2,1,0:T(8,128)(2,1)S(1)} %get-tuple-element.39), channel_id=1, source_target_pairs={{0,3},{1,0},{2,1},{3,2},{4,7},{5,4},{6,5},{7,6},{8,11},{9,8},{10,9... | collective-permute-start | bytes 393224 | tf_op jit(solution)/shard_map/ppermute | solution.py:291
  38.5 0.5 collective-permute-done.10.first
  38.9 2.9 %collective-permute-done.11.second = bf16[8,16,512]{2,1,0:T(8,128)(2,1)S(1)} collective-permute-done((bf16[8,16,512]{2,1,0:T(8,128)(2,1)S(1)}, bf16[8,16,512]{2,1,0:T(8,128)(2,1)S(1)}, u32[]{:S(2)}, u32[]{:S(2)}) %collective-permute-start.11) | collective-permute-done | bytes 131104 | tf_op jit(solution)/shard_map/ppermute | solution.py:291
  41.8 0.6 %collective-permute-done.12.third = bf16[8,16,512]{2,1,0:T(8,128)(2,1)S(1)} collective-permute-done((bf16[8,16,512]{2,1,0:T(8,128)(2,1)S(1)}, bf16[8,16,512]{2,1,0:T(8,128)(2,1)S(1)}, u32[]{:S(2)}, u32[]{:S(2)}) %collective-permute-start.12) | collective-permute-done | bytes 131104 | tf_op jit(solution)/shard_map/ppermute | solution.py:291
  42.4 1.3 %energy.1 = bf16[16,8,512]{2,1,0:T(8,128)(2,1)} custom-call(s32[128]{0:T(128)S(1)} %copy-done.1, s32[1,128]{1,0:T(1,128)S(1)} %bitcast.4, f32[8,16,512]{2,1,0:T(8,128)S(1)} %get-tuple-element.36.own, bf16[8,16,512]{2,1,0:T(8,128)(2,1)S(1)} %collective-permute-done.10.first, bf16[8,16,512]{2,1,0:T(8,128)(2,1)S(1)} %collective-permute-done.11.second, ...), custom_call_target="tpu_custom_call" | custom-call | tf_op jit(solution)/shard_map/energy/pallas_call | solution.py:310
  43.7 5.1 %all-to-all-start = ((bf16[16,8,512]{2,1,0:T(8,128)(2,1)}), bf16[16,8,512]{2,1,0:T(8,128)(2,1)S(1)}, u32[]{:S(2)}, u32[]{:S(2)}) async-start(bf16[16,8,512]{2,1,0:T(8,128)(2,1)} %energy.1), calls=%async_computation | async-start | bytes 262144 | tf_op jit(solution)/shard_map/all_to_all | solution.py:319
  48.8 0.8 %coefficients.1 = f32[8,2,8,512]{3,2,1,0:T(8,128)} custom-call(f32[8,16,512]{2,1,0:T(8,128)S(1)} %get-tuple-element.36.own, bf16[8,16,512]{2,1,0:T(8,128)(2,1)S(1)} %collective-permute-done.10.first, bf16[8,16,512]{2,1,0:T(8,128)(2,1)S(1)} %collective-permute-done.11.second, bf16[8,16,512]{2,1,0:T(8,128)(2,1)S(1)} %collective-permute-done.12.third), custom_call_target="tpu_custom_call" | custom-call | tf_op jit(solution)/shard_map/coefficients/pallas_call | solution.py:320
  49.6 7.0 %all-to-all-done.parts = bf16[16,8,512]{2,1,0:T(8,128)(2,1)S(1)} async-done(((bf16[16,8,512]{2,1,0:T(8,128)(2,1)}), bf16[16,8,512]{2,1,0:T(8,128)(2,1)S(1)}, u32[]{:S(2)}, u32[]{:S(2)}) %all-to-all-start) | async-done | bytes 131104 | tf_op jit(solution)/shard_map/all_to_all | solution.py:319
  56.7 0.6 %total.1 = f32[8,512]{1,0:T(8,128)} custom-call(bf16[16,8,512]{2,1,0:T(8,128)(2,1)S(1)} %all-to-all-done.parts), custom_call_target="tpu_custom_call" | custom-call | tf_op jit(solution)/shard_map/total/pallas_call | solution.py:328
  (9 shorter events, 0.2 us)
Async XLA Ops:
  0.6 14.3 %copy-start = (bf16[8,2,128,512]{3,2,1,0:T(8,128)(2,1)S(1)}, bf16[8,2,128,512]{3,2,1,0:T(8,128)(2,1)}, u32[]{:S(2)}) copy-start(bf16[8,2,128,512]{3,2,1,0:T(8,128)(2,1)} %param.7) | copy-start | bytes 6291460
  0.6 3.0 %collective-permute-start = (bf16[4096,128]{1,0:T(8,128)(2,1)}, bf16[4096,128]{1,0:T(8,128)(2,1)S(1)}, u32[]{:S(2)}, u32[]{:S(2)}) collective-permute-start(bf16[4096,128]{1,0:T(8,128)(2,1)} %snapshots_hbm.1), channel_id=1, source_target_pairs={{0,16},{16,0},{32,48},{48,32},{64,80},{80,64},{96,112},{112,96},{1... | collective-permute-start | bytes 3145736 | tf_op jit(solution)/shard_map/ppermute | solution.py:106
  4.0 7.0 %collective-permute-start.1 = (bf16[8,2,2,16,128]{4,3,2,1,0:T(8,128)(2,1)S(1)}, bf16[8,2,2,16,128]{4,3,2,1,0:T(8,128)(2,1)S(1)}, u32[]{:S(2)}, u32[]{:S(2)}) collective-permute-start(bf16[8,2,2,16,128]{4,3,2,1,0:T(8,128)(2,1)S(1)} %get-tuple-element.25), channel_id=1, source_target_pairs={{0,32},{16,48},{32,64},{48,80},{64,96},{80,112},{96,0},{112,16},{1... | collective-permute-start | bytes 393224 | tf_op jit(solution)/shard_map/ppermute | solution.py:275
  5.7 9.2 %collective-permute-start.2 = (bf16[8,2,2,16,128]{4,3,2,1,0:T(8,128)(2,1)S(1)}, bf16[8,2,2,16,128]{4,3,2,1,0:T(8,128)(2,1)S(1)}, u32[]{:S(2)}, u32[]{:S(2)}) collective-permute-start(bf16[8,2,2,16,128]{4,3,2,1,0:T(8,128)(2,1)S(1)} %get-tuple-element.26), channel_id=1, source_target_pairs={{0,64},{16,80},{32,96},{48,112},{64,0},{80,16},{96,32},{112,48},{1... | collective-permute-start | bytes 393224 | tf_op jit(solution)/shard_map/ppermute | solution.py:275
  8.6 6.3 %collective-permute-start.3 = (bf16[8,2,2,16,128]{4,3,2,1,0:T(8,128)(2,1)S(1)}, bf16[8,2,2,16,128]{4,3,2,1,0:T(8,128)(2,1)S(1)}, u32[]{:S(2)}, u32[]{:S(2)}) collective-permute-start(bf16[8,2,2,16,128]{4,3,2,1,0:T(8,128)(2,1)S(1)} %get-tuple-element.27), channel_id=1, source_target_pairs={{0,96},{16,112},{32,0},{48,16},{64,32},{80,48},{96,64},{112,80},{1... | collective-permute-start | bytes 393224 | tf_op jit(solution)/shard_map/ppermute | solution.py:275
  15.8 6.5 %collective-permute-start.5 = (bf16[4,2,32,512]{3,2,1,0:T(8,128)(2,1)S(1)}, bf16[4,2,32,512]{3,2,1,0:T(8,128)(2,1)S(1)}, u32[]{:S(2)}, u32[]{:S(2)}) collective-permute-start(bf16[4,2,32,512]{3,2,1,0:T(8,128)(2,1)S(1)} %get-tuple-element.31), channel_id=1, source_target_pairs={{0,4},{1,5},{2,6},{3,7},{4,0},{5,1},{6,2},{7,3},{8,12},{9,13},{10,... | collective-permute-start | bytes 786440 | tf_op jit(solution)/shard_map/ppermute | solution.py:291
  17.4 7.8 %collective-permute-start.8 = (bf16[4,2,32,512]{3,2,1,0:T(8,128)(2,1)S(1)}, bf16[4,2,32,512]{3,2,1,0:T(8,128)(2,1)S(1)}, u32[]{:S(2)}, u32[]{:S(2)}) collective-permute-start(bf16[4,2,32,512]{3,2,1,0:T(8,128)(2,1)S(1)} %get-tuple-element.35), channel_id=1, source_target_pairs={{0,12},{1,13},{2,14},{3,15},{4,8},{5,9},{6,10},{7,11},{8,4},{9,5},... | collective-permute-start | bytes 786440 | tf_op jit(solution)/shard_map/ppermute | solution.py:291
  19.5 6.4 %collective-permute-start.4 = (bf16[4,2,32,512]{3,2,1,0:T(8,128)(2,1)S(1)}, bf16[4,2,32,512]{3,2,1,0:T(8,128)(2,1)S(1)}, u32[]{:S(2)}, u32[]{:S(2)}) collective-permute-start(bf16[4,2,32,512]{3,2,1,0:T(8,128)(2,1)S(1)} %get-tuple-element.29), channel_id=1, source_target_pairs={{0,4},{1,5},{2,6},{3,7},{4,0},{5,1},{6,2},{7,3},{8,12},{9,13},{10,... | collective-permute-start | bytes 786440 | tf_op jit(solution)/shard_map/ppermute | solution.py:291
  20.1 7.7 %collective-permute-start.7 = (bf16[4,2,32,512]{3,2,1,0:T(8,128)(2,1)S(1)}, bf16[4,2,32,512]{3,2,1,0:T(8,128)(2,1)S(1)}, u32[]{:S(2)}, u32[]{:S(2)}) collective-permute-start(bf16[4,2,32,512]{3,2,1,0:T(8,128)(2,1)S(1)} %get-tuple-element.33), channel_id=1, source_target_pairs={{0,12},{1,13},{2,14},{3,15},{4,8},{5,9},{6,10},{7,11},{8,4},{9,5},... | collective-permute-start | bytes 786440 | tf_op jit(solution)/shard_map/ppermute | solution.py:291
  22.3 20.2 %copy-start.1 = (s32[128]{0:T(128)S(1)}, s32[128]{0:T(128)}, u32[]{:S(2)}) copy-start(s32[128]{0:T(128)} %tallies.1) | copy-start | bytes 1540
  22.3 8.3 %collective-permute-start.6 = (bf16[4,2,32,512]{3,2,1,0:T(8,128)(2,1)S(1)}, bf16[4,2,32,512]{3,2,1,0:T(8,128)(2,1)S(1)}, u32[]{:S(2)}, u32[]{:S(2)}) collective-permute-start(bf16[4,2,32,512]{3,2,1,0:T(8,128)(2,1)S(1)} %relay.2), channel_id=1, source_target_pairs={{0,12},{1,13},{2,14},{3,15},{4,8},{5,9},{6,10},{7,11},{8,4},{9,5},... | collective-permute-start | bytes 786440 | tf_op jit(solution)/shard_map/ppermute | solution.py:291
  25.2 6.5 %collective-permute-start.9 = (bf16[4,2,32,512]{3,2,1,0:T(8,128)(2,1)S(1)}, bf16[4,2,32,512]{3,2,1,0:T(8,128)(2,1)S(1)}, u32[]{:S(2)}, u32[]{:S(2)}) collective-permute-start(bf16[4,2,32,512]{3,2,1,0:T(8,128)(2,1)S(1)} %relay.3), channel_id=1, source_target_pairs={{0,4},{1,5},{2,6},{3,7},{4,0},{5,1},{6,2},{7,3},{8,12},{9,13},{10,... | collective-permute-start | bytes 786440 | tf_op jit(solution)/shard_map/ppermute | solution.py:291
  31.9 7.1 %collective-permute-start.10 = (bf16[8,16,512]{2,1,0:T(8,128)(2,1)S(1)}, bf16[8,16,512]{2,1,0:T(8,128)(2,1)S(1)}, u32[]{:S(2)}, u32[]{:S(2)}) collective-permute-start(bf16[8,16,512]{2,1,0:T(8,128)(2,1)S(1)} %get-tuple-element.37), channel_id=1, source_target_pairs={{0,1},{1,2},{2,3},{3,0},{4,5},{5,6},{6,7},{7,4},{8,9},{9,10},{10,1... | collective-permute-start | bytes 393224 | tf_op jit(solution)/shard_map/ppermute | solution.py:291
  33.9 7.9 %collective-permute-start.11 = (bf16[8,16,512]{2,1,0:T(8,128)(2,1)S(1)}, bf16[8,16,512]{2,1,0:T(8,128)(2,1)S(1)}, u32[]{:S(2)}, u32[]{:S(2)}) collective-permute-start(bf16[8,16,512]{2,1,0:T(8,128)(2,1)S(1)} %get-tuple-element.38), channel_id=1, source_target_pairs={{0,2},{1,3},{2,0},{3,1},{4,6},{5,7},{6,4},{7,5},{8,10},{9,11},{10,... | collective-permute-start | bytes 393224 | tf_op jit(solution)/shard_map/ppermute | solution.py:291
  37.4 5.0 %collective-permute-start.12 = (bf16[8,16,512]{2,1,0:T(8,128)(2,1)S(1)}, bf16[8,16,512]{2,1,0:T(8,128)(2,1)S(1)}, u32[]{:S(2)}, u32[]{:S(2)}) collective-permute-start(bf16[8,16,512]{2,1,0:T(8,128)(2,1)S(1)} %get-tuple-element.39), channel_id=1, source_target_pairs={{0,3},{1,0},{2,1},{3,2},{4,7},{5,4},{6,5},{7,6},{8,11},{9,8},{10,9... | collective-permute-start | bytes 393224 | tf_op jit(solution)/shard_map/ppermute | solution.py:291
  43.7 12.9 %all-to-all-start = ((bf16[16,8,512]{2,1,0:T(8,128)(2,1)}), bf16[16,8,512]{2,1,0:T(8,128)(2,1)S(1)}, u32[]{:S(2)}, u32[]{:S(2)}) async-start(bf16[16,8,512]{2,1,0:T(8,128)(2,1)} %energy.1), calls=%async_computation | async-start | bytes 262144 | tf_op jit(solution)/shard_map/all_to_all | solution.py:319

commit v6 on v5

--- a/solution.py
+++ b/solution.py
@@ -142,7 +142,7 @@
 def places():
     row = lax.axis_index("row")
     x, z = row // SIDE, row % SIDE
-    x_first = lax.axis_index("block") % 2 == 0
+    x_first = lax.axis_index("block") % 2 == 1
     return x_first, jnp.where(x_first, x, z), jnp.where(x_first, z, x)
 
 
@@ -235,33 +235,30 @@
     )(*parts)
 
 
-def energy_kernel(tallies, all_tallies, own, first, second, third, energy, own_energy):
-    freqs, rows, width = own.shape
-    blocks = rows // 2
+def finish_kernel(tallies, all_tallies, own, first, second, third, coefficients, energy, mine):
+    blocks = coefficients.shape[0]
+    total = own[...] + sum(part[...].astype(f32) for part in (first, second, third))
+    for c in range(2):
+        part = total[:, c * blocks : (c + 1) * blocks]
+        coefficients[:, c] = jnp.swapaxes(part, 0, 1)
     start = lax.axis_index("row") * blocks
     total_weight = jnp.sum(all_tallies[...].astype(f32), axis=1, keepdims=True)
-    spots = lax.broadcasted_iota(jnp.int32, (rows, width), 0) % blocks
-    weights = jnp.zeros((rows, width), f32)
     for j in range(blocks):
-        weights = jnp.where(spots == j, tallies[start + j].astype(f32), weights)
-    weights = weights / total_weight
-    for k in range(freqs):
-        total = own[k] + first[k].astype(f32) + second[k].astype(f32) + third[k].astype(f32)
-        power = jnp.sum(weights * (total * total), axis=0, keepdims=True)
-        own_energy[k : k + 1, :] = power
-    energy[...] = jnp.broadcast_to(own_energy[...].astype(bf16)[None], energy.shape)
-
-
-def coefficients_kernel(own, first, second, third, coefficients):
-    blocks = coefficients.shape[0]
-    for k in range(own.shape[0]):
-        total = own[k] + first[k].astype(f32) + second[k].astype(f32) + third[k].astype(f32)
-        coefficients[:, 0, k, :] = total[:blocks]
-        coefficients[:, 1, k, :] = total[blocks:]
-
-
-def sum_kernel(parts, energy):
+        weight = tallies[start + j].astype(f32) / total_weight
+        real, imag = coefficients[j, 0], coefficients[j, 1]
+        power = weight * (real * real + imag * imag)
+        mine[...] = power if j == 0 else mine[...] + power
+    energy[...] = jnp.broadcast_to(mine[...].astype(bf16)[None], energy.shape)
+
+
+def output_kernel(parts, coefficients, coefficients_hbm, energy_hbm, energy, sems):
+    copy = pltpu.make_async_copy(coefficients, coefficients_hbm, sems.at[0])
+    copy.start()
     energy[...] = jnp.sum(parts[...].astype(f32), axis=0)
+    last = pltpu.make_async_copy(energy, energy_hbm, sems.at[1])
+    last.start()
+    copy.wait()
+    last.wait()
 
 
 def shards(snapshots, usable_frame_tallies, retained_frequency_slots, modes):
@@ -283,7 +280,7 @@
         for block in range(groups):
             for x in range(SIDE):
                 for z in range(SIDE):
-                    if (block % 2 == 0) == (stage == 0):
+                    if (block % 2 == 1) == (stage == 0):
                         target = move(x) * SIDE + z
                     else:
                         target = x * SIDE + move(z)
@@ -307,32 +304,32 @@
     came = {i: onward(pieces[i], i) for i in (1, 3, 2)}
     last = [pieces[0]] + [came[i] for i in range(1, SIDE)]
     freqs, double, width = last[0].shape
-    energy_parts = pl.pallas_call(
-        energy_kernel,
-        out_shape=jax.ShapeDtypeStruct((rows, freqs, width), bf16),
+    placed = (double // 2, 2, freqs, width)
+    coefficients, energy_parts = pl.pallas_call(
+        finish_kernel,
+        out_shape=[
+            jax.ShapeDtypeStruct(placed, f32),
+            jax.ShapeDtypeStruct((rows, freqs, width), bf16),
+        ],
         in_specs=[SMEM] + [VMEM] * (1 + SIDE),
-        out_specs=VMEM,
+        out_specs=[VMEM, VMEM],
         scratch_shapes=[pltpu.VMEM((freqs, width), f32)],
         compiler_params=pltpu.CompilerParams(vmem_limit_bytes=SMALL),
-        name="energy",
+        name="finish",
     )(usable_frame_tallies, usable_frame_tallies.reshape(1, -1), *last)
     swapped = lax.all_to_all(energy_parts, "row", 0, 0, tiled=True)
-    coefficients = pl.pallas_call(
-        coefficients_kernel,
-        out_shape=jax.ShapeDtypeStruct((double // 2, 2, freqs, width), f32),
-        in_specs=[VMEM] * SIDE,
-        out_specs=VMEM,
-        compiler_params=pltpu.CompilerParams(vmem_limit_bytes=SMALL),
-        name="coefficients",
-    )(*last)
-    energy = pl.pallas_call(
-        sum_kernel,
-        out_shape=jax.ShapeDtypeStruct((freqs, width), f32),
-        in_specs=[VMEM],
-        out_specs=VMEM,
-        compiler_params=pltpu.CompilerParams(vmem_limit_bytes=SMALL),
-        name="total",
-    )(swapped)
+    coefficients, energy = pl.pallas_call(
+        output_kernel,
+        out_shape=[
+            jax.ShapeDtypeStruct(placed, f32),
+            jax.ShapeDtypeStruct((freqs, width), f32),
+        ],
+        in_specs=[VMEM, VMEM],
+        out_specs=[pl.BlockSpec(memory_space=pltpu.HBM)] * 2,
+        scratch_shapes=[pltpu.VMEM((freqs, width), f32), pltpu.SemaphoreType.DMA((2,))],
+        compiler_params=pltpu.CompilerParams(vmem_limit_bytes=SMALL),
+        name="output",
+    )(swapped, coefficients)
     return (coefficients, energy)
 
 

time: 57.5 us -> 56.6 us (0.984)
  blocking collectives: 0 us -> 12.6 us
  waiting for transfers between devices: 24.6 us -> 16.1 us
  starting transfers between devices: 25.7 us -> 22.1 us
  Pallas kernels: 6.28 us -> 4.98 us
    all_to_all x0 -> x1, blocking collectives: none -> 12.6 us  [shards(): swapped = lax.all_to_all(energy_parts, 'row', 0, 0, tiled=True)]
    all_to_all x1 -> x0, waiting for transfers between devices: 7.03 us -> none  [shards(): swapped = lax.all_to_all(energy_parts, 'row', 0, 0, tiled=True)]
    all_to_all x1 -> x0, starting transfers between devices: 5.07 us -> none  [shards(): swapped = lax.all_to_all(energy_parts, 'row', 0, 0, tiled=True)]
    ppermute x9, starting transfers between devices: 14.6 us -> 16.1 us  [along(): return lax.ppermute(value, ('block', 'row'), pairs)]
    ppermute x9, waiting for transfers between devices: 11.7 us -> 10.2 us  [along(): return lax.ppermute(value, ('block', 'row'), pairs)]
    pallas_call x3 -> x2, Pallas kernels: 2.78 us -> 1.49 us  [the longest x1 0.77 us: shards(): pl.pallas_call(finish_kernel, out_shape=[jax.ShapeDtypeStruct(placed, f32...]
  transfers between devices with their start and end apart: 14 -> 13, of which waited for: 12 -> 11; matrix products, arithmetic and copies ran while one was open for 0% -> 0% of each run, Pallas kernels for 5% -> 4%
where the time goes in v6:
time: 56.6 us; the launch traced here: 56.5 us
  starting transfers between devices  22.1 us (39%)
  waiting for transfers between devices  16.1 us (28%)
  blocking collectives  12.6 us (22%)
  Pallas kernels  4.98 us (9%)
  between operations  0.71 us (1%)
    ppermute x9, starting transfers between devices, along(): return lax.ppermute(value, ('block', 'row'), pairs)  16.1 us
    all_to_all x1, blocking collectives, shards(): swapped = lax.all_to_all(energy_parts, 'row', 0, 0, tiled=True)  12.6 us
    ppermute x9, waiting for transfers between devices, along(): return lax.ppermute(value, ('block', 'row'), pairs)  10.2 us
    ppermute x3, starting transfers between devices, along_y(): return lax.ppermute(value, 'block', pairs)  5.98 us
    ppermute x3, waiting for transfers between devices, along_y(): return lax.ppermute(value, 'block', pairs)  4.98 us
    pallas_call x1, Pallas kernels, transform(): pl.pallas_call(own_kernel, out_shape=[jax.ShapeDtypeStruct((2, SIDE, freq...  1.96 us
  transfers between devices with their start and end apart: 13, of which 11 were waited for; matrix products, arithmetic and copies ran while one was open for 0% of the time, Pallas kernels for 4%

profile of v6, /device:TPU:0, one launch (start us, length us, event | category | flops | bytes accessed | tf_op | source)
XLA Modules:
  0.0 56.5 jit_solution(14360812078603027937)
XLA Ops:
  0.6 0.1 collective-permute-start
  0.7 2.0 %transform_own.1 = (bf16[2,4,8,16,128]{4,3,2,1,0:T(8,128)(2,1)S(1)}, f32[64,256]{1,0:T(8,128)S(1)}, f32[16,256]{1,0:T(8,128)S(1)}) custom-call(s32[128]{0:T(128)} %tallies.1, s32[1,64]{1,0:T(1,128)} %bitcast.5, bf16[4096,128]{1,0:T(8,128)(2,1)} %snapshots_hbm.1), custom_call_target="tpu_custom_call" | custom-call | tf_op jit(solution)/shard_map/transform_own/pallas_call | solution.py:107
  2.7 0.9 %collective-permute-done.snapshots = bf16[4096,128]{1,0:T(8,128)(2,1)S(1)} collective-permute-done((bf16[4096,128]{1,0:T(8,128)(2,1)}, bf16[4096,128]{1,0:T(8,128)(2,1)S(1)}, u32[]{:S(2)}, u32[]{:S(2)}) %collective-permute-start) | collective-permute-done | bytes 1048608 | tf_op jit(solution)/shard_map/ppermute | solution.py:106
  3.6 0.4 transform_other.1
  4.0 1.7 %collective-permute-start.1 = (bf16[8,2,2,16,128]{4,3,2,1,0:T(8,128)(2,1)S(1)}, bf16[8,2,2,16,128]{4,3,2,1,0:T(8,128)(2,1)S(1)}, u32[]{:S(2)}, u32[]{:S(2)}) collective-permute-start(bf16[8,2,2,16,128]{4,3,2,1,0:T(8,128)(2,1)S(1)} %get-tuple-element.27), channel_id=1, source_target_pairs={{0,32},{16,48},{32,64},{48,80},{64,96},{80,112},{96,0},{112,16},{1... | collective-permute-start | bytes 393224 | tf_op jit(solution)/shard_map/ppermute | solution.py:272
  5.7 2.9 %collective-permute-start.2 = (bf16[8,2,2,16,128]{4,3,2,1,0:T(8,128)(2,1)S(1)}, bf16[8,2,2,16,128]{4,3,2,1,0:T(8,128)(2,1)S(1)}, u32[]{:S(2)}, u32[]{:S(2)}) collective-permute-start(bf16[8,2,2,16,128]{4,3,2,1,0:T(8,128)(2,1)S(1)} %get-tuple-element.28), channel_id=1, source_target_pairs={{0,64},{16,80},{32,96},{48,112},{64,0},{80,16},{96,32},{112,48},{1... | collective-permute-start | bytes 393224 | tf_op jit(solution)/shard_map/ppermute | solution.py:272
  8.6 1.3 %collective-permute-start.3 = (bf16[8,2,2,16,128]{4,3,2,1,0:T(8,128)(2,1)S(1)}, bf16[8,2,2,16,128]{4,3,2,1,0:T(8,128)(2,1)S(1)}, u32[]{:S(2)}, u32[]{:S(2)}) collective-permute-start(bf16[8,2,2,16,128]{4,3,2,1,0:T(8,128)(2,1)S(1)} %get-tuple-element.29), channel_id=1, source_target_pairs={{0,96},{16,112},{32,0},{48,16},{64,32},{80,48},{96,64},{112,80},{1... | collective-permute-start | bytes 393224 | tf_op jit(solution)/shard_map/ppermute | solution.py:272
  10.0 1.0 %collective-permute-done.1.refs_1_ = bf16[8,2,2,16,128]{4,3,2,1,0:T(8,128)(2,1)S(1)} collective-permute-done((bf16[8,2,2,16,128]{4,3,2,1,0:T(8,128)(2,1)S(1)}, bf16[8,2,2,16,128]{4,3,2,1,0:T(8,128)(2,1)S(1)}, u32[]{:S(2)}, u32[]{:S(2)}) %collective-permute-start.1) | collective-permute-done | bytes 131104 | tf_op jit(solution)/shard_map/ppermute | solution.py:272
  11.0 4.0 %collective-permute-done.2.refs_2_ = bf16[8,2,2,16,128]{4,3,2,1,0:T(8,128)(2,1)S(1)} collective-permute-done((bf16[8,2,2,16,128]{4,3,2,1,0:T(8,128)(2,1)S(1)}, bf16[8,2,2,16,128]{4,3,2,1,0:T(8,128)(2,1)S(1)}, u32[]{:S(2)}, u32[]{:S(2)}) %collective-permute-start.2) | collective-permute-done | bytes 131104 | tf_op jit(solution)/shard_map/ppermute | solution.py:272
  15.0 0.0 collective-permute-done.3.refs_3_
  15.0 0.8 %project.1 = (f32[4,2,32,512]{3,2,1,0:T(8,128)S(1)}, f32[4,2,32,512]{3,2,1,0:T(8,128)S(1)}, bf16[4,2,32,512]{3,2,1,0:T(8,128)(2,1)S(1)}, bf16[4,2,32,512]{3,2,1,...) custom-call(bf16[8,2,2,16,128]{4,3,2,1,0:T(8,128)(2,1)S(1)} %get-tup, ...), custom_call_target="tpu_custom_call" | custom-call | tf_op jit(solution)/shard_map/project/pallas_call | solution.py:185
  15.8 2.0 %collective-permute-start.5 = (bf16[4,2,32,512]{3,2,1,0:T(8,128)(2,1)S(1)}, bf16[4,2,32,512]{3,2,1,0:T(8,128)(2,1)S(1)}, u32[]{:S(2)}, u32[]{:S(2)}) collective-permute-start(bf16[4,2,32,512]{3,2,1,0:T(8,128)(2,1)S(1)} %get-tuple-element.33), channel_id=1, source_target_pairs={{0,1},{1,0},{2,3},{3,2},{4,5},{5,4},{6,7},{7,6},{8,9},{9,8},{10,11... | collective-permute-start | bytes 786440 | tf_op jit(solution)/shard_map/ppermute | solution.py:288
  17.8 2.5 %collective-permute-start.8 = (bf16[4,2,32,512]{3,2,1,0:T(8,128)(2,1)S(1)}, bf16[4,2,32,512]{3,2,1,0:T(8,128)(2,1)S(1)}, u32[]{:S(2)}, u32[]{:S(2)}) collective-permute-start(bf16[4,2,32,512]{3,2,1,0:T(8,128)(2,1)S(1)} %get-tuple-element.37), channel_id=1, source_target_pairs={{0,3},{1,2},{2,1},{3,0},{4,7},{5,6},{6,5},{7,4},{8,11},{9,10},{10,... | collective-permute-start | bytes 786440 | tf_op jit(solution)/shard_map/ppermute | solution.py:288
  20.3 1.0 %collective-permute-start.4 = (bf16[4,2,32,512]{3,2,1,0:T(8,128)(2,1)S(1)}, bf16[4,2,32,512]{3,2,1,0:T(8,128)(2,1)S(1)}, u32[]{:S(2)}, u32[]{:S(2)}) collective-permute-start(bf16[4,2,32,512]{3,2,1,0:T(8,128)(2,1)S(1)} %get-tuple-element.31), channel_id=1, source_target_pairs={{0,1},{1,0},{2,3},{3,2},{4,5},{5,4},{6,7},{7,6},{8,9},{9,8},{10,11... | collective-permute-start | bytes 786440 | tf_op jit(solution)/shard_map/ppermute | solution.py:288
  21.3 0.6 %collective-permute-start.7 = (bf16[4,2,32,512]{3,2,1,0:T(8,128)(2,1)S(1)}, bf16[4,2,32,512]{3,2,1,0:T(8,128)(2,1)S(1)}, u32[]{:S(2)}, u32[]{:S(2)}) collective-permute-start(bf16[4,2,32,512]{3,2,1,0:T(8,128)(2,1)S(1)} %get-tuple-element.35), channel_id=1, source_target_pairs={{0,3},{1,2},{2,1},{3,0},{4,7},{5,6},{6,5},{7,4},{8,11},{9,10},{10,... | collective-permute-start | bytes 786440 | tf_op jit(solution)/shard_map/ppermute | solution.py:288
  21.9 0.3 collective-permute-done.5.came
  22.3 4.1 %collective-permute-start.6 = (bf16[4,2,32,512]{3,2,1,0:T(8,128)(2,1)S(1)}, bf16[4,2,32,512]{3,2,1,0:T(8,128)(2,1)S(1)}, u32[]{:S(2)}, u32[]{:S(2)}) collective-permute-start(bf16[4,2,32,512]{3,2,1,0:T(8,128)(2,1)S(1)} %relay.2), channel_id=1, source_target_pairs={{0,3},{1,2},{2,1},{3,0},{4,7},{5,6},{6,5},{7,4},{8,11},{9,10},{10,... | collective-permute-start | bytes 786440 | tf_op jit(solution)/shard_map/ppermute | solution.py:288
  26.5 0.1 collective-permute-start.9
  26.6 0.1 collective-permute-done.4.refs_1_
  26.7 2.2 %collective-permute-done.7.refs_4_ = bf16[4,2,32,512]{3,2,1,0:T(8,128)(2,1)S(1)} collective-permute-done((bf16[4,2,32,512]{3,2,1,0:T(8,128)(2,1)S(1)}, bf16[4,2,32,512]{3,2,1,0:T(8,128)(2,1)S(1)}, u32[]{:S(2)}, u32[]{:S(2)}) %collective-permute-start.7) | collective-permute-done | bytes 262176 | tf_op jit(solution)/shard_map/ppermute | solution.py:288
  28.9 2.8 %collective-permute-done.6.refs_2_ = bf16[4,2,32,512]{3,2,1,0:T(8,128)(2,1)S(1)} collective-permute-done((bf16[4,2,32,512]{3,2,1,0:T(8,128)(2,1)S(1)}, bf16[4,2,32,512]{3,2,1,0:T(8,128)(2,1)S(1)}, u32[]{:S(2)}, u32[]{:S(2)}) %collective-permute-start.6) | collective-permute-done | bytes 262176 | tf_op jit(solution)/shard_map/ppermute | solution.py:288
  31.7 1.2 %collective-permute-done.9.refs_5_ = bf16[4,2,32,512]{3,2,1,0:T(8,128)(2,1)S(1)} collective-permute-done((bf16[4,2,32,512]{3,2,1,0:T(8,128)(2,1)S(1)}, bf16[4,2,32,512]{3,2,1,0:T(8,128)(2,1)S(1)}, u32[]{:S(2)}, u32[]{:S(2)}) %collective-permute-start.9) | collective-permute-done | bytes 262176 | tf_op jit(solution)/shard_map/ppermute | solution.py:288
  32.9 0.2 fold.1
  33.1 1.6 %collective-permute-start.10 = (bf16[8,16,512]{2,1,0:T(8,128)(2,1)S(1)}, bf16[8,16,512]{2,1,0:T(8,128)(2,1)S(1)}, u32[]{:S(2)}, u32[]{:S(2)}) collective-permute-start(bf16[8,16,512]{2,1,0:T(8,128)(2,1)S(1)} %get-tuple-element.39), channel_id=1, source_target_pairs={{0,4},{1,5},{2,6},{3,7},{4,8},{5,9},{6,10},{7,11},{8,12},{9,13},{1... | collective-permute-start | bytes 393224 | tf_op jit(solution)/shard_map/ppermute | solution.py:288
  34.7 2.7 %collective-permute-start.11 = (bf16[8,16,512]{2,1,0:T(8,128)(2,1)S(1)}, bf16[8,16,512]{2,1,0:T(8,128)(2,1)S(1)}, u32[]{:S(2)}, u32[]{:S(2)}) collective-permute-start(bf16[8,16,512]{2,1,0:T(8,128)(2,1)S(1)} %get-tuple-element.40), channel_id=1, source_target_pairs={{0,8},{1,9},{2,10},{3,11},{4,12},{5,13},{6,14},{7,15},{8,0},{9,1},... | collective-permute-start | bytes 393224 | tf_op jit(solution)/shard_map/ppermute | solution.py:288
  37.4 1.4 %collective-permute-start.12 = (bf16[8,16,512]{2,1,0:T(8,128)(2,1)S(1)}, bf16[8,16,512]{2,1,0:T(8,128)(2,1)S(1)}, u32[]{:S(2)}, u32[]{:S(2)}) collective-permute-start(bf16[8,16,512]{2,1,0:T(8,128)(2,1)S(1)} %get-tuple-element.41), channel_id=1, source_target_pairs={{0,12},{1,13},{2,14},{3,15},{4,0},{5,1},{6,2},{7,3},{8,4},{9,5},{1... | collective-permute-start | bytes 393224 | tf_op jit(solution)/shard_map/ppermute | solution.py:288
  38.9 0.5 collective-permute-done.10.first
  39.4 2.4 %collective-permute-done.11.second = bf16[8,16,512]{2,1,0:T(8,128)(2,1)S(1)} collective-permute-done((bf16[8,16,512]{2,1,0:T(8,128)(2,1)S(1)}, bf16[8,16,512]{2,1,0:T(8,128)(2,1)S(1)}, u32[]{:S(2)}, u32[]{:S(2)}) %collective-permute-start.11) | collective-permute-done | bytes 131104 | tf_op jit(solution)/shard_map/ppermute | solution.py:288
  41.8 0.6 %collective-permute-done.12.third = bf16[8,16,512]{2,1,0:T(8,128)(2,1)S(1)} collective-permute-done((bf16[8,16,512]{2,1,0:T(8,128)(2,1)S(1)}, bf16[8,16,512]{2,1,0:T(8,128)(2,1)S(1)}, u32[]{:S(2)}, u32[]{:S(2)}) %collective-permute-start.12) | collective-permute-done | bytes 131104 | tf_op jit(solution)/shard_map/ppermute | solution.py:288
  42.4 0.8 %finish.1 = (f32[8,2,8,512]{3,2,1,0:T(8,128)S(1)}, bf16[16,8,512]{2,1,0:T(8,128)(2,1)S(1)}) custom-call(s32[128]{0:T(128)S(1)} %copy-done.1, s32[1,128]{1,0:T(1,128)S(1)} %bitcast.4, f32[8,16,512]{2,1,0:T(8,128)S(1)} %get-tuple-element.38.own, bf16[8,16,512]{2,1,0:T(8,128)(2,1)S(1)} %collective-permute-done.10.first, ...), custom_call_target="tpu_custom_call" | custom-call | tf_op jit(solution)/shard_map/finish/pallas_call | solution.py:308
  43.2 12.6 %all_to_all.5.parts = bf16[16,8,512]{2,1,0:T(8,128)(2,1)S(1)} all-to-all(bf16[16,8,512]{2,1,0:T(8,128)(2,1)S(1)} %get-tuple-element.42), channel_id=1, replica_groups=mesh['block'=8,'row'=16] {'row'}, dimensions={0} | all-to-all | bytes 262144 | tf_op jit(solution)/shard_map/all_to_all | solution.py:320
  55.8 0.7 %output.1 = (f32[8,2,8,512]{3,2,1,0:T(8,128)}, f32[8,512]{1,0:T(8,128)}) custom-call(bf16[16,8,512]{2,1,0:T(8,128)(2,1)S(1)} %all_to_all.5.parts, f32[8,2,8,512]{3,2,1,0:T(8,128)S(1)} %get-tuple-element.43.coefficients), custom_call_target="tpu_custom_call" | custom-call | tf_op jit(solution)/shard_map/output/pallas_call | solution.py:321
  (7 shorter events, 0.1 us)
Async XLA Ops:
  0.6 14.3 %copy-start = (bf16[8,2,128,512]{3,2,1,0:T(8,128)(2,1)S(1)}, bf16[8,2,128,512]{3,2,1,0:T(8,128)(2,1)}, u32[]{:S(2)}) copy-start(bf16[8,2,128,512]{3,2,1,0:T(8,128)(2,1)} %param.7) | copy-start | bytes 6291460
  0.6 3.0 %collective-permute-start = (bf16[4096,128]{1,0:T(8,128)(2,1)}, bf16[4096,128]{1,0:T(8,128)(2,1)S(1)}, u32[]{:S(2)}, u32[]{:S(2)}) collective-permute-start(bf16[4096,128]{1,0:T(8,128)(2,1)} %snapshots_hbm.1), channel_id=1, source_target_pairs={{0,16},{16,0},{32,48},{48,32},{64,80},{80,64},{96,112},{112,96},{1... | collective-permute-start | bytes 3145736 | tf_op jit(solution)/shard_map/ppermute | solution.py:106
  4.0 7.0 %collective-permute-start.1 = (bf16[8,2,2,16,128]{4,3,2,1,0:T(8,128)(2,1)S(1)}, bf16[8,2,2,16,128]{4,3,2,1,0:T(8,128)(2,1)S(1)}, u32[]{:S(2)}, u32[]{:S(2)}) collective-permute-start(bf16[8,2,2,16,128]{4,3,2,1,0:T(8,128)(2,1)S(1)} %get-tuple-element.27), channel_id=1, source_target_pairs={{0,32},{16,48},{32,64},{48,80},{64,96},{80,112},{96,0},{112,16},{1... | collective-permute-start | bytes 393224 | tf_op jit(solution)/shard_map/ppermute | solution.py:272
  5.7 9.2 %collective-permute-start.2 = (bf16[8,2,2,16,128]{4,3,2,1,0:T(8,128)(2,1)S(1)}, bf16[8,2,2,16,128]{4,3,2,1,0:T(8,128)(2,1)S(1)}, u32[]{:S(2)}, u32[]{:S(2)}) collective-permute-start(bf16[8,2,2,16,128]{4,3,2,1,0:T(8,128)(2,1)S(1)} %get-tuple-element.28), channel_id=1, source_target_pairs={{0,64},{16,80},{32,96},{48,112},{64,0},{80,16},{96,32},{112,48},{1... | collective-permute-start | bytes 393224 | tf_op jit(solution)/shard_map/ppermute | solution.py:272
  8.6 6.3 %collective-permute-start.3 = (bf16[8,2,2,16,128]{4,3,2,1,0:T(8,128)(2,1)S(1)}, bf16[8,2,2,16,128]{4,3,2,1,0:T(8,128)(2,1)S(1)}, u32[]{:S(2)}, u32[]{:S(2)}) collective-permute-start(bf16[8,2,2,16,128]{4,3,2,1,0:T(8,128)(2,1)S(1)} %get-tuple-element.29), channel_id=1, source_target_pairs={{0,96},{16,112},{32,0},{48,16},{64,32},{80,48},{96,64},{112,80},{1... | collective-permute-start | bytes 393224 | tf_op jit(solution)/shard_map/ppermute | solution.py:272
  15.8 6.5 %collective-permute-start.5 = (bf16[4,2,32,512]{3,2,1,0:T(8,128)(2,1)S(1)}, bf16[4,2,32,512]{3,2,1,0:T(8,128)(2,1)S(1)}, u32[]{:S(2)}, u32[]{:S(2)}) collective-permute-start(bf16[4,2,32,512]{3,2,1,0:T(8,128)(2,1)S(1)} %get-tuple-element.33), channel_id=1, source_target_pairs={{0,1},{1,0},{2,3},{3,2},{4,5},{5,4},{6,7},{7,6},{8,9},{9,8},{10,11... | collective-permute-start | bytes 786440 | tf_op jit(solution)/shard_map/ppermute | solution.py:288
  17.8 8.6 %collective-permute-start.8 = (bf16[4,2,32,512]{3,2,1,0:T(8,128)(2,1)S(1)}, bf16[4,2,32,512]{3,2,1,0:T(8,128)(2,1)S(1)}, u32[]{:S(2)}, u32[]{:S(2)}) collective-permute-start(bf16[4,2,32,512]{3,2,1,0:T(8,128)(2,1)S(1)} %get-tuple-element.37), channel_id=1, source_target_pairs={{0,3},{1,2},{2,1},{3,0},{4,7},{5,6},{6,5},{7,4},{8,11},{9,10},{10,... | collective-permute-start | bytes 786440 | tf_op jit(solution)/shard_map/ppermute | solution.py:288
  20.3 6.4 %collective-permute-start.4 = (bf16[4,2,32,512]{3,2,1,0:T(8,128)(2,1)S(1)}, bf16[4,2,32,512]{3,2,1,0:T(8,128)(2,1)S(1)}, u32[]{:S(2)}, u32[]{:S(2)}) collective-permute-start(bf16[4,2,32,512]{3,2,1,0:T(8,128)(2,1)S(1)} %get-tuple-element.31), channel_id=1, source_target_pairs={{0,1},{1,0},{2,3},{3,2},{4,5},{5,4},{6,7},{7,6},{8,9},{9,8},{10,11... | collective-permute-start | bytes 786440 | tf_op jit(solution)/shard_map/ppermute | solution.py:288
  21.3 7.6 %collective-permute-start.7 = (bf16[4,2,32,512]{3,2,1,0:T(8,128)(2,1)S(1)}, bf16[4,2,32,512]{3,2,1,0:T(8,128)(2,1)S(1)}, u32[]{:S(2)}, u32[]{:S(2)}) collective-permute-start(bf16[4,2,32,512]{3,2,1,0:T(8,128)(2,1)S(1)} %get-tuple-element.35), channel_id=1, source_target_pairs={{0,3},{1,2},{2,1},{3,0},{4,7},{5,6},{6,5},{7,4},{8,11},{9,10},{10,... | collective-permute-start | bytes 786440 | tf_op jit(solution)/shard_map/ppermute | solution.py:288
  22.2 20.2 %copy-start.1 = (s32[128]{0:T(128)S(1)}, s32[128]{0:T(128)}, u32[]{:S(2)}) copy-start(s32[128]{0:T(128)} %tallies.1) | copy-start | bytes 1540
  22.3 9.4 %collective-permute-start.6 = (bf16[4,2,32,512]{3,2,1,0:T(8,128)(2,1)S(1)}, bf16[4,2,32,512]{3,2,1,0:T(8,128)(2,1)S(1)}, u32[]{:S(2)}, u32[]{:S(2)}) collective-permute-start(bf16[4,2,32,512]{3,2,1,0:T(8,128)(2,1)S(1)} %relay.2), channel_id=1, source_target_pairs={{0,3},{1,2},{2,1},{3,0},{4,7},{5,6},{6,5},{7,4},{8,11},{9,10},{10,... | collective-permute-start | bytes 786440 | tf_op jit(solution)/shard_map/ppermute | solution.py:288
  26.5 6.5 %collective-permute-start.9 = (bf16[4,2,32,512]{3,2,1,0:T(8,128)(2,1)S(1)}, bf16[4,2,32,512]{3,2,1,0:T(8,128)(2,1)S(1)}, u32[]{:S(2)}, u32[]{:S(2)}) collective-permute-start(bf16[4,2,32,512]{3,2,1,0:T(8,128)(2,1)S(1)} %relay.3), channel_id=1, source_target_pairs={{0,1},{1,0},{2,3},{3,2},{4,5},{5,4},{6,7},{7,6},{8,9},{9,8},{10,11... | collective-permute-start | bytes 786440 | tf_op jit(solution)/shard_map/ppermute | solution.py:288
  33.1 6.2 %collective-permute-start.10 = (bf16[8,16,512]{2,1,0:T(8,128)(2,1)S(1)}, bf16[8,16,512]{2,1,0:T(8,128)(2,1)S(1)}, u32[]{:S(2)}, u32[]{:S(2)}) collective-permute-start(bf16[8,16,512]{2,1,0:T(8,128)(2,1)S(1)} %get-tuple-element.39), channel_id=1, source_target_pairs={{0,4},{1,5},{2,6},{3,7},{4,8},{5,9},{6,10},{7,11},{8,12},{9,13},{1... | collective-permute-start | bytes 393224 | tf_op jit(solution)/shard_map/ppermute | solution.py:288
  34.7 7.1 %collective-permute-start.11 = (bf16[8,16,512]{2,1,0:T(8,128)(2,1)S(1)}, bf16[8,16,512]{2,1,0:T(8,128)(2,1)S(1)}, u32[]{:S(2)}, u32[]{:S(2)}) collective-permute-start(bf16[8,16,512]{2,1,0:T(8,128)(2,1)S(1)} %get-tuple-element.40), channel_id=1, source_target_pairs={{0,8},{1,9},{2,10},{3,11},{4,12},{5,13},{6,14},{7,15},{8,0},{9,1},... | collective-permute-start | bytes 393224 | tf_op jit(solution)/shard_map/ppermute | solution.py:288
  37.4 5.0 %collective-permute-start.12 = (bf16[8,16,512]{2,1,0:T(8,128)(2,1)S(1)}, bf16[8,16,512]{2,1,0:T(8,128)(2,1)S(1)}, u32[]{:S(2)}, u32[]{:S(2)}) collective-permute-start(bf16[8,16,512]{2,1,0:T(8,128)(2,1)S(1)} %get-tuple-element.41), channel_id=1, source_target_pairs={{0,12},{1,13},{2,14},{3,15},{4,0},{5,1},{6,2},{7,3},{8,4},{9,5},{1... | collective-permute-start | bytes 393224 | tf_op jit(solution)/shard_map/ppermute | solution.py:288

commit v7 on v6

--- a/solution.py
+++ b/solution.py
@@ -7,7 +7,7 @@
 
 FRAMES_PER_SEG = 256
 FARTHEST_FIRST = (2, 1, 3)
-PARTS = 4
+PARTS = 1
 SIDE = 4
 VMEM = pl.BlockSpec(memory_space=pltpu.VMEM)
 SMEM = pl.BlockSpec(memory_space=pltpu.SMEM)
@@ -26,19 +26,16 @@
     return window * (1.0 / jnp.sqrt(jnp.sum(window * window, axis=1, keepdims=True)))
 
 
-def transform_blocks(window, waves, snapshots, acc, arrived):
-    blocks, rows = window.shape[0], waves.shape[0]
+def transform_blocks(blocks, rows, table, snapshots, acc):
     for j in range(blocks):
-        arrived(j)
-        table = (window[j : j + 1] * waves).astype(bf16)
         frames = snapshots[j * FRAMES_PER_SEG : (j + 1) * FRAMES_PER_SEG, :]
         acc[pl.ds(j, rows, stride=blocks), :] = jnp.dot(
-            table, frames, preferred_element_type=f32
+            table(j), frames, preferred_element_type=f32
         )
 
 
 def own_kernel(
-    tallies_hbm, slots_hbm, snapshots_hbm, spectra, waves, other_window,
+    tallies_hbm, slots_hbm, snapshots_hbm, spectra, other_tables,
     acc, tallies, slots, snapshots, sems,
 ):
     copies = [
@@ -59,9 +56,9 @@
     copies[1].wait()
     block = lax.axis_index("block")
     core = block % 2
-    blocks = other_window.shape[0]
+    blocks = other_tables.shape[0]
     window = windows(tallies, block * blocks, blocks)
-    other_window[...] = windows(tallies, (block + 1 - 2 * core) * blocks, blocks)
+    other_window = windows(tallies, (block + 1 - 2 * core) * blocks, blocks)
     times = lax.broadcasted_iota(jnp.int32, (1, FRAMES_PER_SEG), 1)
     turns = lax.dot_general(
         slots[...].astype(f32).astype(bf16),
@@ -73,21 +70,24 @@
     turns = jnp.where(core == 0, turns[:, 0], turns[:, 1]).reshape(-1, FRAMES_PER_SEG)
     turns = (turns.astype(jnp.int32) % FRAMES_PER_SEG).astype(f32)
     phase = turns * (2.0 * jnp.pi / FRAMES_PER_SEG)
-    waves[...] = jnp.concatenate([jnp.cos(phase), -jnp.sin(phase)], axis=0)
-
-    def arrived(j):
-        if j % (blocks // PARTS) == 0:
-            copies[2 + j // (blocks // PARTS)].wait()
-
-    transform_blocks(window, waves[...], snapshots, acc, arrived)
+    waves = jnp.concatenate([jnp.cos(phase), -jnp.sin(phase)], axis=0)
+
+    def table(j):
+        return (window[j : j + 1] * waves).astype(bf16)
+
+    for copy in copies[2:]:
+        copy.wait()
+    transform_blocks(blocks, waves.shape[0], table, snapshots, acc)
     spectra[...] = acc[...].astype(bf16).reshape(spectra.shape)
-
-
-def other_kernel(own, waves, window, snapshots, *refs):
+    for j in range(blocks):
+        other_tables[j] = (other_window[j : j + 1] * waves).astype(bf16)
+
+
+def other_kernel(own, tables, snapshots, *refs):
     outs, acc = refs[:-1], refs[-1]
     block = lax.axis_index("block")
     y, core = block // 2, block % 2
-    transform_blocks(window[...], waves[...], snapshots, acc, lambda j: None)
+    transform_blocks(*tables.shape[:2], lambda j: tables[j], snapshots, acc)
     _, _, freqs, blocks, points = own.shape
     size = freqs * blocks
     for i in range(SIDE):
@@ -104,15 +104,14 @@
     rows = 2 * SIDE * freqs
     swap = [(b, b ^ 1) for b in range(lax.axis_size("block"))]
     others = lax.ppermute(snapshots, "block", swap)
-    own, waves, window = pl.pallas_call(
+    own, tables = pl.pallas_call(
         own_kernel,
         out_shape=[
             jax.ShapeDtypeStruct((2, SIDE, freqs, blocks, points), bf16),
-            jax.ShapeDtypeStruct((rows, FRAMES_PER_SEG), f32),
-            jax.ShapeDtypeStruct((blocks, FRAMES_PER_SEG), f32),
+            jax.ShapeDtypeStruct((blocks, rows, FRAMES_PER_SEG), bf16),
         ],
         in_specs=[pl.BlockSpec(memory_space=pltpu.HBM)] * 3,
-        out_specs=[VMEM] * 3,
+        out_specs=[VMEM] * 2,
         scratch_shapes=[
             pltpu.VMEM((rows * blocks, points), f32),
             pltpu.SMEM(tallies.shape, jnp.int32),
@@ -131,12 +130,12 @@
     return pl.pallas_call(
         other_kernel,
         out_shape=[jax.ShapeDtypeStruct((freqs, 2, 2, blocks, points), bf16)] * SIDE,
-        in_specs=[VMEM] * 4,
+        in_specs=[VMEM] * 3,
         out_specs=[VMEM] * SIDE,
         scratch_shapes=[pltpu.VMEM((rows * blocks, points), f32)],
         compiler_params=pltpu.CompilerParams(vmem_limit_bytes=SMALL),
         name="transform_other",
-    )(own, waves, window, others)
+    )(own, tables, others)
 
 
 def places():

time: 56.6 us -> 56.6 us (level)
  transfers between devices with their start and end apart: 13 -> 13, of which waited for: 11 -> 11; matrix products, arithmetic and copies ran while one was open for 0% -> 0% of each run, Pallas kernels for 4% -> 3%
where the time goes in v7:
time: 56.6 us; the launch traced here: 56.5 us
  starting transfers between devices  22.1 us (39%)
  waiting for transfers between devices  16.2 us (29%)
  blocking collectives  12.6 us (22%)
  Pallas kernels  4.85 us (9%)
  between operations  0.71 us (1%)
    ppermute x9, starting transfers between devices, along(): return lax.ppermute(value, ('block', 'row'), pairs)  16.1 us
    all_to_all x1, blocking collectives, shards(): swapped = lax.all_to_all(energy_parts, 'row', 0, 0, tiled=True)  12.6 us
    ppermute x9, waiting for transfers between devices, along(): return lax.ppermute(value, ('block', 'row'), pairs)  10.2 us
    ppermute x3, starting transfers between devices, along_y(): return lax.ppermute(value, 'block', pairs)  5.98 us
    ppermute x3, waiting for transfers between devices, along_y(): return lax.ppermute(value, 'block', pairs)  4.99 us
    pallas_call x1, Pallas kernels, transform(): pl.pallas_call(own_kernel, out_shape=[jax.ShapeDtypeStruct((2, SIDE, freq...  1.84 us
  transfers between devices with their start and end apart: 13, of which 11 were waited for; matrix products, arithmetic and copies ran while one was open for 0% of the time, Pallas kernels for 3%

profile of v7, /device:TPU:0, one launch (start us, length us, event | category | flops | bytes accessed | tf_op | source)
XLA Modules:
  0.0 56.5 jit_solution(8027828638720800613)
XLA Ops:
  0.6 0.1 collective-permute-start
  0.7 1.8 %transform_own.1 = (bf16[2,4,8,16,128]{4,3,2,1,0:T(8,128)(2,1)S(1)}, bf16[16,64,256]{2,1,0:T(8,128)(2,1)S(1)}) custom-call(s32[128]{0:T(128)} %tallies.1, s32[1,64]{1,0:T(1,128)} %bitcast.5, bf16[4096,128]{1,0:T(8,128)(2,1)} %snapshots_hbm.1), custom_call_target="tpu_custom_call" | custom-call | tf_op jit(solution)/shard_map/transform_own/pallas_call | solution.py:107
  2.6 1.0 %collective-permute-done.snapshots = bf16[4096,128]{1,0:T(8,128)(2,1)S(1)} collective-permute-done((bf16[4096,128]{1,0:T(8,128)(2,1)}, bf16[4096,128]{1,0:T(8,128)(2,1)S(1)}, u32[]{:S(2)}, u32[]{:S(2)}) %collective-permute-start) | collective-permute-done | bytes 1048608 | tf_op jit(solution)/shard_map/ppermute | solution.py:106
  3.6 0.4 transform_other.1
  4.0 1.7 %collective-permute-start.1 = (bf16[8,2,2,16,128]{4,3,2,1,0:T(8,128)(2,1)S(1)}, bf16[8,2,2,16,128]{4,3,2,1,0:T(8,128)(2,1)S(1)}, u32[]{:S(2)}, u32[]{:S(2)}) collective-permute-start(bf16[8,2,2,16,128]{4,3,2,1,0:T(8,128)(2,1)S(1)} %get-tuple-element.25), channel_id=1, source_target_pairs={{0,32},{16,48},{32,64},{48,80},{64,96},{80,112},{96,0},{112,16},{1... | collective-permute-start | bytes 393224 | tf_op jit(solution)/shard_map/ppermute | solution.py:271
  5.7 2.9 %collective-permute-start.2 = (bf16[8,2,2,16,128]{4,3,2,1,0:T(8,128)(2,1)S(1)}, bf16[8,2,2,16,128]{4,3,2,1,0:T(8,128)(2,1)S(1)}, u32[]{:S(2)}, u32[]{:S(2)}) collective-permute-start(bf16[8,2,2,16,128]{4,3,2,1,0:T(8,128)(2,1)S(1)} %get-tuple-element.26), channel_id=1, source_target_pairs={{0,64},{16,80},{32,96},{48,112},{64,0},{80,16},{96,32},{112,48},{1... | collective-permute-start | bytes 393224 | tf_op jit(solution)/shard_map/ppermute | solution.py:271
  8.6 1.3 %collective-permute-start.3 = (bf16[8,2,2,16,128]{4,3,2,1,0:T(8,128)(2,1)S(1)}, bf16[8,2,2,16,128]{4,3,2,1,0:T(8,128)(2,1)S(1)}, u32[]{:S(2)}, u32[]{:S(2)}) collective-permute-start(bf16[8,2,2,16,128]{4,3,2,1,0:T(8,128)(2,1)S(1)} %get-tuple-element.27), channel_id=1, source_target_pairs={{0,96},{16,112},{32,0},{48,16},{64,32},{80,48},{96,64},{112,80},{1... | collective-permute-start | bytes 393224 | tf_op jit(solution)/shard_map/ppermute | solution.py:271
  10.0 1.0 %collective-permute-done.1.refs_1_ = bf16[8,2,2,16,128]{4,3,2,1,0:T(8,128)(2,1)S(1)} collective-permute-done((bf16[8,2,2,16,128]{4,3,2,1,0:T(8,128)(2,1)S(1)}, bf16[8,2,2,16,128]{4,3,2,1,0:T(8,128)(2,1)S(1)}, u32[]{:S(2)}, u32[]{:S(2)}) %collective-permute-start.1) | collective-permute-done | bytes 131104 | tf_op jit(solution)/shard_map/ppermute | solution.py:271
  11.0 4.0 %collective-permute-done.2.refs_2_ = bf16[8,2,2,16,128]{4,3,2,1,0:T(8,128)(2,1)S(1)} collective-permute-done((bf16[8,2,2,16,128]{4,3,2,1,0:T(8,128)(2,1)S(1)}, bf16[8,2,2,16,128]{4,3,2,1,0:T(8,128)(2,1)S(1)}, u32[]{:S(2)}, u32[]{:S(2)}) %collective-permute-start.2) | collective-permute-done | bytes 131104 | tf_op jit(solution)/shard_map/ppermute | solution.py:271
  14.9 0.0 collective-permute-done.3.refs_3_
  15.0 0.8 %project.1 = (f32[4,2,32,512]{3,2,1,0:T(8,128)S(1)}, f32[4,2,32,512]{3,2,1,0:T(8,128)S(1)}, bf16[4,2,32,512]{3,2,1,0:T(8,128)(2,1)S(1)}, bf16[4,2,32,512]{3,2,1,...) custom-call(bf16[8,2,2,16,128]{4,3,2,1,0:T(8,128)(2,1)S(1)} %get-tup, ...), custom_call_target="tpu_custom_call" | custom-call | tf_op jit(solution)/shard_map/project/pallas_call | solution.py:184
  15.8 2.0 %collective-permute-start.5 = (bf16[4,2,32,512]{3,2,1,0:T(8,128)(2,1)S(1)}, bf16[4,2,32,512]{3,2,1,0:T(8,128)(2,1)S(1)}, u32[]{:S(2)}, u32[]{:S(2)}) collective-permute-start(bf16[4,2,32,512]{3,2,1,0:T(8,128)(2,1)S(1)} %get-tuple-element.31), channel_id=1, source_target_pairs={{0,1},{1,0},{2,3},{3,2},{4,5},{5,4},{6,7},{7,6},{8,9},{9,8},{10,11... | collective-permute-start | bytes 786440 | tf_op jit(solution)/shard_map/ppermute | solution.py:287
  17.8 2.5 %collective-permute-start.8 = (bf16[4,2,32,512]{3,2,1,0:T(8,128)(2,1)S(1)}, bf16[4,2,32,512]{3,2,1,0:T(8,128)(2,1)S(1)}, u32[]{:S(2)}, u32[]{:S(2)}) collective-permute-start(bf16[4,2,32,512]{3,2,1,0:T(8,128)(2,1)S(1)} %get-tuple-element.35), channel_id=1, source_target_pairs={{0,3},{1,2},{2,1},{3,0},{4,7},{5,6},{6,5},{7,4},{8,11},{9,10},{10,... | collective-permute-start | bytes 786440 | tf_op jit(solution)/shard_map/ppermute | solution.py:287
  20.3 1.0 %collective-permute-start.4 = (bf16[4,2,32,512]{3,2,1,0:T(8,128)(2,1)S(1)}, bf16[4,2,32,512]{3,2,1,0:T(8,128)(2,1)S(1)}, u32[]{:S(2)}, u32[]{:S(2)}) collective-permute-start(bf16[4,2,32,512]{3,2,1,0:T(8,128)(2,1)S(1)} %get-tuple-element.29), channel_id=1, source_target_pairs={{0,1},{1,0},{2,3},{3,2},{4,5},{5,4},{6,7},{7,6},{8,9},{9,8},{10,11... | collective-permute-start | bytes 786440 | tf_op jit(solution)/shard_map/ppermute | solution.py:287
  21.3 0.6 %collective-permute-start.7 = (bf16[4,2,32,512]{3,2,1,0:T(8,128)(2,1)S(1)}, bf16[4,2,32,512]{3,2,1,0:T(8,128)(2,1)S(1)}, u32[]{:S(2)}, u32[]{:S(2)}) collective-permute-start(bf16[4,2,32,512]{3,2,1,0:T(8,128)(2,1)S(1)} %get-tuple-element.33), channel_id=1, source_target_pairs={{0,3},{1,2},{2,1},{3,0},{4,7},{5,6},{6,5},{7,4},{8,11},{9,10},{10,... | collective-permute-start | bytes 786440 | tf_op jit(solution)/shard_map/ppermute | solution.py:287
  21.9 0.3 collective-permute-done.5.came
  22.3 4.1 %collective-permute-start.6 = (bf16[4,2,32,512]{3,2,1,0:T(8,128)(2,1)S(1)}, bf16[4,2,32,512]{3,2,1,0:T(8,128)(2,1)S(1)}, u32[]{:S(2)}, u32[]{:S(2)}) collective-permute-start(bf16[4,2,32,512]{3,2,1,0:T(8,128)(2,1)S(1)} %relay.2), channel_id=1, source_target_pairs={{0,3},{1,2},{2,1},{3,0},{4,7},{5,6},{6,5},{7,4},{8,11},{9,10},{10,... | collective-permute-start | bytes 786440 | tf_op jit(solution)/shard_map/ppermute | solution.py:287
  26.5 0.1 collective-permute-start.9
  26.6 0.1 collective-permute-done.4.refs_1_
  26.7 2.2 %collective-permute-done.7.refs_4_ = bf16[4,2,32,512]{3,2,1,0:T(8,128)(2,1)S(1)} collective-permute-done((bf16[4,2,32,512]{3,2,1,0:T(8,128)(2,1)S(1)}, bf16[4,2,32,512]{3,2,1,0:T(8,128)(2,1)S(1)}, u32[]{:S(2)}, u32[]{:S(2)}) %collective-permute-start.7) | collective-permute-done | bytes 262176 | tf_op jit(solution)/shard_map/ppermute | solution.py:287
  28.9 2.8 %collective-permute-done.6.refs_2_ = bf16[4,2,32,512]{3,2,1,0:T(8,128)(2,1)S(1)} collective-permute-done((bf16[4,2,32,512]{3,2,1,0:T(8,128)(2,1)S(1)}, bf16[4,2,32,512]{3,2,1,0:T(8,128)(2,1)S(1)}, u32[]{:S(2)}, u32[]{:S(2)}) %collective-permute-start.6) | collective-permute-done | bytes 262176 | tf_op jit(solution)/shard_map/ppermute | solution.py:287
  31.7 1.2 %collective-permute-done.9.refs_5_ = bf16[4,2,32,512]{3,2,1,0:T(8,128)(2,1)S(1)} collective-permute-done((bf16[4,2,32,512]{3,2,1,0:T(8,128)(2,1)S(1)}, bf16[4,2,32,512]{3,2,1,0:T(8,128)(2,1)S(1)}, u32[]{:S(2)}, u32[]{:S(2)}) %collective-permute-start.9) | collective-permute-done | bytes 262176 | tf_op jit(solution)/shard_map/ppermute | solution.py:287
  32.9 0.2 fold.1
  33.1 1.6 %collective-permute-start.10 = (bf16[8,16,512]{2,1,0:T(8,128)(2,1)S(1)}, bf16[8,16,512]{2,1,0:T(8,128)(2,1)S(1)}, u32[]{:S(2)}, u32[]{:S(2)}) collective-permute-start(bf16[8,16,512]{2,1,0:T(8,128)(2,1)S(1)} %get-tuple-element.37), channel_id=1, source_target_pairs={{0,4},{1,5},{2,6},{3,7},{4,8},{5,9},{6,10},{7,11},{8,12},{9,13},{1... | collective-permute-start | bytes 393224 | tf_op jit(solution)/shard_map/ppermute | solution.py:287
  34.7 2.7 %collective-permute-start.11 = (bf16[8,16,512]{2,1,0:T(8,128)(2,1)S(1)}, bf16[8,16,512]{2,1,0:T(8,128)(2,1)S(1)}, u32[]{:S(2)}, u32[]{:S(2)}) collective-permute-start(bf16[8,16,512]{2,1,0:T(8,128)(2,1)S(1)} %get-tuple-element.38), channel_id=1, source_target_pairs={{0,8},{1,9},{2,10},{3,11},{4,12},{5,13},{6,14},{7,15},{8,0},{9,1},... | collective-permute-start | bytes 393224 | tf_op jit(solution)/shard_map/ppermute | solution.py:287
  37.4 1.4 %collective-permute-start.12 = (bf16[8,16,512]{2,1,0:T(8,128)(2,1)S(1)}, bf16[8,16,512]{2,1,0:T(8,128)(2,1)S(1)}, u32[]{:S(2)}, u32[]{:S(2)}) collective-permute-start(bf16[8,16,512]{2,1,0:T(8,128)(2,1)S(1)} %get-tuple-element.39), channel_id=1, source_target_pairs={{0,12},{1,13},{2,14},{3,15},{4,0},{5,1},{6,2},{7,3},{8,4},{9,5},{1... | collective-permute-start | bytes 393224 | tf_op jit(solution)/shard_map/ppermute | solution.py:287
  38.9 0.5 collective-permute-done.10.first
  39.4 2.4 %collective-permute-done.11.second = bf16[8,16,512]{2,1,0:T(8,128)(2,1)S(1)} collective-permute-done((bf16[8,16,512]{2,1,0:T(8,128)(2,1)S(1)}, bf16[8,16,512]{2,1,0:T(8,128)(2,1)S(1)}, u32[]{:S(2)}, u32[]{:S(2)}) %collective-permute-start.11) | collective-permute-done | bytes 131104 | tf_op jit(solution)/shard_map/ppermute | solution.py:287
  41.8 0.6 %collective-permute-done.12.third = bf16[8,16,512]{2,1,0:T(8,128)(2,1)S(1)} collective-permute-done((bf16[8,16,512]{2,1,0:T(8,128)(2,1)S(1)}, bf16[8,16,512]{2,1,0:T(8,128)(2,1)S(1)}, u32[]{:S(2)}, u32[]{:S(2)}) %collective-permute-start.12) | collective-permute-done | bytes 131104 | tf_op jit(solution)/shard_map/ppermute | solution.py:287
  42.4 0.8 %finish.1 = (f32[8,2,8,512]{3,2,1,0:T(8,128)S(1)}, bf16[16,8,512]{2,1,0:T(8,128)(2,1)S(1)}) custom-call(s32[128]{0:T(128)S(1)} %copy-done.1, s32[1,128]{1,0:T(1,128)S(1)} %bitcast.4, f32[8,16,512]{2,1,0:T(8,128)S(1)} %get-tuple-element.36.own, bf16[8,16,512]{2,1,0:T(8,128)(2,1)S(1)} %collective-permute-done.10.first, ...), custom_call_target="tpu_custom_call" | custom-call | tf_op jit(solution)/shard_map/finish/pallas_call | solution.py:307
  43.2 12.6 %all_to_all.5.parts = bf16[16,8,512]{2,1,0:T(8,128)(2,1)S(1)} all-to-all(bf16[16,8,512]{2,1,0:T(8,128)(2,1)S(1)} %get-tuple-element.40), channel_id=1, replica_groups=mesh['block'=8,'row'=16] {'row'}, dimensions={0} | all-to-all | bytes 262144 | tf_op jit(solution)/shard_map/all_to_all | solution.py:319
  55.8 0.7 %output.1 = (f32[8,2,8,512]{3,2,1,0:T(8,128)}, f32[8,512]{1,0:T(8,128)}) custom-call(bf16[16,8,512]{2,1,0:T(8,128)(2,1)S(1)} %all_to_all.5.parts, f32[8,2,8,512]{3,2,1,0:T(8,128)S(1)} %get-tuple-element.41.coefficients), custom_call_target="tpu_custom_call" | custom-call | tf_op jit(solution)/shard_map/output/pallas_call | solution.py:320
  (7 shorter events, 0.1 us)
Async XLA Ops:
  0.6 14.3 %copy-start = (bf16[8,2,128,512]{3,2,1,0:T(8,128)(2,1)S(1)}, bf16[8,2,128,512]{3,2,1,0:T(8,128)(2,1)}, u32[]{:S(2)}) copy-start(bf16[8,2,128,512]{3,2,1,0:T(8,128)(2,1)} %param.7) | copy-start | bytes 6291460
  0.6 3.0 %collective-permute-start = (bf16[4096,128]{1,0:T(8,128)(2,1)}, bf16[4096,128]{1,0:T(8,128)(2,1)S(1)}, u32[]{:S(2)}, u32[]{:S(2)}) collective-permute-start(bf16[4096,128]{1,0:T(8,128)(2,1)} %snapshots_hbm.1), channel_id=1, source_target_pairs={{0,16},{16,0},{32,48},{48,32},{64,80},{80,64},{96,112},{112,96},{1... | collective-permute-start | bytes 3145736 | tf_op jit(solution)/shard_map/ppermute | solution.py:106
  4.0 7.0 %collective-permute-start.1 = (bf16[8,2,2,16,128]{4,3,2,1,0:T(8,128)(2,1)S(1)}, bf16[8,2,2,16,128]{4,3,2,1,0:T(8,128)(2,1)S(1)}, u32[]{:S(2)}, u32[]{:S(2)}) collective-permute-start(bf16[8,2,2,16,128]{4,3,2,1,0:T(8,128)(2,1)S(1)} %get-tuple-element.25), channel_id=1, source_target_pairs={{0,32},{16,48},{32,64},{48,80},{64,96},{80,112},{96,0},{112,16},{1... | collective-permute-start | bytes 393224 | tf_op jit(solution)/shard_map/ppermute | solution.py:271
  5.7 9.2 %collective-permute-start.2 = (bf16[8,2,2,16,128]{4,3,2,1,0:T(8,128)(2,1)S(1)}, bf16[8,2,2,16,128]{4,3,2,1,0:T(8,128)(2,1)S(1)}, u32[]{:S(2)}, u32[]{:S(2)}) collective-permute-start(bf16[8,2,2,16,128]{4,3,2,1,0:T(8,128)(2,1)S(1)} %get-tuple-element.26), channel_id=1, source_target_pairs={{0,64},{16,80},{32,96},{48,112},{64,0},{80,16},{96,32},{112,48},{1... | collective-permute-start | bytes 393224 | tf_op jit(solution)/shard_map/ppermute | solution.py:271
  8.6 6.3 %collective-permute-start.3 = (bf16[8,2,2,16,128]{4,3,2,1,0:T(8,128)(2,1)S(1)}, bf16[8,2,2,16,128]{4,3,2,1,0:T(8,128)(2,1)S(1)}, u32[]{:S(2)}, u32[]{:S(2)}) collective-permute-start(bf16[8,2,2,16,128]{4,3,2,1,0:T(8,128)(2,1)S(1)} %get-tuple-element.27), channel_id=1, source_target_pairs={{0,96},{16,112},{32,0},{48,16},{64,32},{80,48},{96,64},{112,80},{1... | collective-permute-start | bytes 393224 | tf_op jit(solution)/shard_map/ppermute | solution.py:271
  15.8 6.5 %collective-permute-start.5 = (bf16[4,2,32,512]{3,2,1,0:T(8,128)(2,1)S(1)}, bf16[4,2,32,512]{3,2,1,0:T(8,128)(2,1)S(1)}, u32[]{:S(2)}, u32[]{:S(2)}) collective-permute-start(bf16[4,2,32,512]{3,2,1,0:T(8,128)(2,1)S(1)} %get-tuple-element.31), channel_id=1, source_target_pairs={{0,1},{1,0},{2,3},{3,2},{4,5},{5,4},{6,7},{7,6},{8,9},{9,8},{10,11... | collective-permute-start | bytes 786440 | tf_op jit(solution)/shard_map/ppermute | solution.py:287
  17.8 8.6 %collective-permute-start.8 = (bf16[4,2,32,512]{3,2,1,0:T(8,128)(2,1)S(1)}, bf16[4,2,32,512]{3,2,1,0:T(8,128)(2,1)S(1)}, u32[]{:S(2)}, u32[]{:S(2)}) collective-permute-start(bf16[4,2,32,512]{3,2,1,0:T(8,128)(2,1)S(1)} %get-tuple-element.35), channel_id=1, source_target_pairs={{0,3},{1,2},{2,1},{3,0},{4,7},{5,6},{6,5},{7,4},{8,11},{9,10},{10,... | collective-permute-start | bytes 786440 | tf_op jit(solution)/shard_map/ppermute | solution.py:287
  20.3 6.4 %collective-permute-start.4 = (bf16[4,2,32,512]{3,2,1,0:T(8,128)(2,1)S(1)}, bf16[4,2,32,512]{3,2,1,0:T(8,128)(2,1)S(1)}, u32[]{:S(2)}, u32[]{:S(2)}) collective-permute-start(bf16[4,2,32,512]{3,2,1,0:T(8,128)(2,1)S(1)} %get-tuple-element.29), channel_id=1, source_target_pairs={{0,1},{1,0},{2,3},{3,2},{4,5},{5,4},{6,7},{7,6},{8,9},{9,8},{10,11... | collective-permute-start | bytes 786440 | tf_op jit(solution)/shard_map/ppermute | solution.py:287
  21.3 7.6 %collective-permute-start.7 = (bf16[4,2,32,512]{3,2,1,0:T(8,128)(2,1)S(1)}, bf16[4,2,32,512]{3,2,1,0:T(8,128)(2,1)S(1)}, u32[]{:S(2)}, u32[]{:S(2)}) collective-permute-start(bf16[4,2,32,512]{3,2,1,0:T(8,128)(2,1)S(1)} %get-tuple-element.33), channel_id=1, source_target_pairs={{0,3},{1,2},{2,1},{3,0},{4,7},{5,6},{6,5},{7,4},{8,11},{9,10},{10,... | collective-permute-start | bytes 786440 | tf_op jit(solution)/shard_map/ppermute | solution.py:287
  22.2 20.2 %copy-start.1 = (s32[128]{0:T(128)S(1)}, s32[128]{0:T(128)}, u32[]{:S(2)}) copy-start(s32[128]{0:T(128)} %tallies.1) | copy-start | bytes 1540
  22.3 9.4 %collective-permute-start.6 = (bf16[4,2,32,512]{3,2,1,0:T(8,128)(2,1)S(1)}, bf16[4,2,32,512]{3,2,1,0:T(8,128)(2,1)S(1)}, u32[]{:S(2)}, u32[]{:S(2)}) collective-permute-start(bf16[4,2,32,512]{3,2,1,0:T(8,128)(2,1)S(1)} %relay.2), channel_id=1, source_target_pairs={{0,3},{1,2},{2,1},{3,0},{4,7},{5,6},{6,5},{7,4},{8,11},{9,10},{10,... | collective-permute-start | bytes 786440 | tf_op jit(solution)/shard_map/ppermute | solution.py:287
  26.5 6.5 %collective-permute-start.9 = (bf16[4,2,32,512]{3,2,1,0:T(8,128)(2,1)S(1)}, bf16[4,2,32,512]{3,2,1,0:T(8,128)(2,1)S(1)}, u32[]{:S(2)}, u32[]{:S(2)}) collective-permute-start(bf16[4,2,32,512]{3,2,1,0:T(8,128)(2,1)S(1)} %relay.3), channel_id=1, source_target_pairs={{0,1},{1,0},{2,3},{3,2},{4,5},{5,4},{6,7},{7,6},{8,9},{9,8},{10,11... | collective-permute-start | bytes 786440 | tf_op jit(solution)/shard_map/ppermute | solution.py:287
  33.1 6.2 %collective-permute-start.10 = (bf16[8,16,512]{2,1,0:T(8,128)(2,1)S(1)}, bf16[8,16,512]{2,1,0:T(8,128)(2,1)S(1)}, u32[]{:S(2)}, u32[]{:S(2)}) collective-permute-start(bf16[8,16,512]{2,1,0:T(8,128)(2,1)S(1)} %get-tuple-element.37), channel_id=1, source_target_pairs={{0,4},{1,5},{2,6},{3,7},{4,8},{5,9},{6,10},{7,11},{8,12},{9,13},{1... | collective-permute-start | bytes 393224 | tf_op jit(solution)/shard_map/ppermute | solution.py:287
  34.7 7.1 %collective-permute-start.11 = (bf16[8,16,512]{2,1,0:T(8,128)(2,1)S(1)}, bf16[8,16,512]{2,1,0:T(8,128)(2,1)S(1)}, u32[]{:S(2)}, u32[]{:S(2)}) collective-permute-start(bf16[8,16,512]{2,1,0:T(8,128)(2,1)S(1)} %get-tuple-element.38), channel_id=1, source_target_pairs={{0,8},{1,9},{2,10},{3,11},{4,12},{5,13},{6,14},{7,15},{8,0},{9,1},... | collective-permute-start | bytes 393224 | tf_op jit(solution)/shard_map/ppermute | solution.py:287
  37.4 5.0 %collective-permute-start.12 = (bf16[8,16,512]{2,1,0:T(8,128)(2,1)S(1)}, bf16[8,16,512]{2,1,0:T(8,128)(2,1)S(1)}, u32[]{:S(2)}, u32[]{:S(2)}) collective-permute-start(bf16[8,16,512]{2,1,0:T(8,128)(2,1)S(1)} %get-tuple-element.39), channel_id=1, source_target_pairs={{0,12},{1,13},{2,14},{3,15},{4,0},{5,1},{6,2},{7,3},{8,4},{9,5},{1... | collective-permute-start | bytes 393224 | tf_op jit(solution)/shard_map/ppermute | solution.py:287
